TPU v7x, 256 devices: a whole 4x4x8 slice. The times are simulated.
256 devices in a mesh: dp: 8 (over x_hi, y), seq: 32 (over x_lo, z, core).
Axes of the slice: x: 4 (x_hi: 2, x_lo: 2; x = x_hi * 2 + x_lo), y: 4, z: 8, core: 2. Of those that a mesh axis runs over, the one named last changes fastest.
Arguments:
- query_seq: bfloat16 [8, 16384, 256], P('dp', 'seq'), may hold values from -6 to 6
- key_seq: bfloat16 [8, 16384, 256], P('dp', 'seq'), may hold values from -6 to 6
- value_seq: bfloat16 [8, 16384, 256], P('dp', 'seq'), may hold values from -6 to 6
- upstream: bfloat16 [8, 16384, 256], P('dp', 'seq'), may hold values from -6 to 6
- filter_param: float32 [16384, 256], P('seq'), may hold values from -6 to 6
Outputs:
- output: bfloat16 [8, 16384, 256], P('dp', 'seq')
- query_grad: bfloat16 [8, 16384, 256], P('dp', 'seq')
- key_grad: bfloat16 [8, 16384, 256], P('dp', 'seq')
- value_grad: bfloat16 [8, 16384, 256], P('dp', 'seq')
- filter_grad: float32 [16384, 256], P('seq')
All inputs are finite; a program needn't handle non-finite values.
Results may differ from a plain program's by a relative error of at most 0.0012.
Values sent between devices are 32-bit elements; how exact they have to be, the bound alone decides.
No kernel may reach another device: no remote copies, remote signals or barrier semaphores. Data moves between devices by JAX's collectives and lax.ppermute only.
A program may use at most 128 MiB of HBM per device.

v0:
```python
import math

import jax
import jax.numpy as jnp
from jax import lax
from jax.sharding import PartitionSpec as P

PRECISE = lax.Precision.HIGHEST


def cos_sin(row_len, col_len, period, offset):
    row_ids = lax.broadcasted_iota(jnp.int32, (row_len, col_len), 0)
    col_ids = lax.broadcasted_iota(jnp.int32, (row_len, col_len), 1) + offset
    angles = (row_ids * col_ids % period).astype(jnp.float32) * (2.0 * math.pi / period)
    return (jnp.cos(angles), jnp.sin(angles))


def forward(stacked, first_move, second_move):
    columns = first_move(stacked)
    shards = columns.shape[1]
    stride = columns.shape[2]
    period = 2 * shards * shards * stride
    cos_a, sin_a = cos_sin(2 * shards, shards, 2 * shards, 0)
    real_part = jnp.einsum("ka,nasc->nksc", cos_a, columns, precision=PRECISE)
    imag_part = -jnp.einsum("ka,nasc->nksc", sin_a, columns, precision=PRECISE)
    cos_t, sin_t = cos_sin(2 * shards, stride, period, lax.axis_index("seq") * stride)
    cos_t = cos_t[None, :, :, None]
    sin_t = sin_t[None, :, :, None]
    turned_real = real_part * cos_t + imag_part * sin_t
    turned_imag = imag_part * cos_t - real_part * sin_t
    rows_real, rows_imag = second_move(turned_real, turned_imag)
    row_count = rows_real.shape[2]
    cos_b, sin_b = cos_sin(row_count, row_count, row_count, 0)
    spec_real = jnp.einsum("nkbc,bm->nkmc", rows_real, cos_b, precision=PRECISE) + jnp.einsum(
        "nkbc,bm->nkmc", rows_imag, sin_b, precision=PRECISE
    )
    spec_imag = jnp.einsum("nkbc,bm->nkmc", rows_imag, cos_b, precision=PRECISE) - jnp.einsum(
        "nkbc,bm->nkmc", rows_real, sin_b, precision=PRECISE
    )
    return (spec_real, spec_imag)


def inverse(spec_real, spec_imag, first_move, second_move):
    row_count = spec_real.shape[2]
    cos_b, sin_b = cos_sin(row_count, row_count, row_count, 0)
    rows_real = jnp.einsum("nkmc,mb->nkbc", spec_real, cos_b, precision=PRECISE) - jnp.einsum(
        "nkmc,mb->nkbc", spec_imag, sin_b, precision=PRECISE
    )
    rows_imag = jnp.einsum("nkmc,mb->nkbc", spec_imag, cos_b, precision=PRECISE) + jnp.einsum(
        "nkmc,mb->nkbc", spec_real, sin_b, precision=PRECISE
    )
    moved_real, moved_imag = first_move(rows_real, rows_imag)
    doubled = moved_real.shape[1]
    stride = moved_real.shape[2]
    shards = doubled // 2
    period = doubled * shards * stride
    cos_t, sin_t = cos_sin(doubled, stride, period, lax.axis_index("seq") * stride)
    cos_t = cos_t[None, :, :, None]
    sin_t = sin_t[None, :, :, None]
    turned_real = moved_real * cos_t - moved_imag * sin_t
    turned_imag = moved_imag * cos_t + moved_real * sin_t
    cos_a, sin_a = cos_sin(shards, doubled, doubled, 0)
    blocks = jnp.einsum("ak,nksc->nasc", cos_a, turned_real, precision=PRECISE) - jnp.einsum(
        "ak,nksc->nasc", sin_a, turned_imag, precision=PRECISE
    )
    placed = second_move(blocks)
    return placed * (1.0 / period)


def local(query_seq, key_seq, value_seq, upstream, filter_param):
    query_rows = query_seq[0].astype(jnp.float32)
    key_rows = key_seq[0].astype(jnp.float32)
    value_rows = value_seq[0].astype(jnp.float32)
    grad_rows = upstream[0].astype(jnp.float32)
    length_total = lax.axis_size("seq") * filter_param.shape[0]
    norm_factor = 1.0 / math.sqrt(length_total)
    filt = filter_param * norm_factor
    mixed = key_rows * value_rows
    gated = grad_rows * query_rows
    stacked = jnp.stack([mixed, gated, filt])[:, None]
    spec_real, spec_imag = forward(
        stacked,
        lambda moved: lax.all_to_all(moved, "seq", split_axis=2, concat_axis=1, tiled=True),
        lambda first_arr, second_arr: (
            lax.all_to_all(first_arr, "seq", split_axis=1, concat_axis=2, tiled=True),
            lax.all_to_all(second_arr, "seq", split_axis=1, concat_axis=2, tiled=True),
        ),
    )
    filt_real = spec_real[2]
    filt_imag = spec_imag[2]
    mixed_real, mixed_imag = (spec_real[0], spec_imag[0])
    gated_real, gated_imag = (spec_real[1], spec_imag[1])
    conv_real = filt_real * mixed_real - filt_imag * mixed_imag
    conv_imag = filt_real * mixed_imag + filt_imag * mixed_real
    back_real = filt_real * gated_real + filt_imag * gated_imag
    back_imag = filt_real * gated_imag - filt_imag * gated_real
    lag_real = mixed_real * gated_real + mixed_imag * gated_imag
    lag_imag = mixed_real * gated_imag - mixed_imag * gated_real
    real_list = [conv_real, back_real]
    imag_list = [conv_imag, back_imag]
    real_list = real_list + [lag_real]
    imag_list = imag_list + [lag_imag]
    results = inverse(
        jnp.stack(real_list),
        jnp.stack(imag_list),
        lambda first_arr, second_arr: (
            lax.all_to_all(first_arr, "seq", split_axis=2, concat_axis=1, tiled=True),
            lax.all_to_all(second_arr, "seq", split_axis=2, concat_axis=1, tiled=True),
        ),
        lambda moved: lax.all_to_all(moved, "seq", split_axis=1, concat_axis=2, tiled=True),
    )
    conv = results[0, 0]
    back = results[1, 0]
    lag_index = 2
    filter_grad = lax.psum(results[lag_index, 0] * norm_factor, "dp")
    output = (query_rows * conv).astype(jnp.bfloat16)[None]
    query_grad = (grad_rows * conv).astype(jnp.bfloat16)[None]
    key_grad = (back * value_rows).astype(jnp.bfloat16)[None]
    value_grad = (back * key_rows).astype(jnp.bfloat16)[None]
    return (output, query_grad, key_grad, value_grad, filter_grad)


def solution(mesh):
    in_specs = (
        P("dp", "seq", None),
        P("dp", "seq", None),
        P("dp", "seq", None),
        P("dp", "seq", None),
        P("seq", None),
    )
    out_specs = (
        P("dp", "seq", None),
        P("dp", "seq", None),
        P("dp", "seq", None),
        P("dp", "seq", None),
        P("seq", None),
    )
    return jax.shard_map(local, mesh=mesh, in_specs=in_specs, out_specs=out_specs, check_vma=False)
```

profile of v0, /device:TPU:32, one launch (start us, length us, event | category | flops | bytes accessed | tf_op | source)
XLA Modules:
  0.0 607.1 jit_solution(10822744316326308723)
XLA Ops:
  7.2 1.1 multiply_bitcast_fusion
  8.2 1.3 convert_multiply_fusion.1
  9.6 0.1 maximum_bitcast_fusion
  9.7 2.8 copy.37
  12.5 9.9 %all-to-all-start = ((f32[3,1,512,256]{3,1,0,2:T(1,128)}), f32[3,1,512,256]{3,1,0,2:T(1,128)S(1)}, u32[]{:S(2)}, u32[]{:S(2)}) async-start(f32[3,1,512,256]{3,1,0,2:T(1,128)} %copy.37), calls=%async_computation | async-start | bytes 3145728 | tf_op jit(solution)/shard_map/all_to_all | solution.py:83
  22.4 0.1 fusion.85
  22.6 40.0 %all-to-all-done = f32[3,1,512,256]{3,1,0,2:T(1,128)S(1)} async-done(((f32[3,1,512,256]{3,1,0,2:T(1,128)}), f32[3,1,512,256]{3,1,0,2:T(1,128)S(1)}, u32[]{:S(2)}, u32[]{:S(2)}) %all-to-all-start) | async-done | bytes 1572896 | tf_op jit(solution)/shard_map/all_to_all | solution.py:83
  62.5 0.1 copy.38
  62.7 3.8 fusion.20
  66.4 6.3 %fusion = (f32[3,64,16,256]{3,1,2,0:T(8,128)S(1)}, f32[3,64,16,256]{3,1,2,0:T(8,128)}) fusion(f32[3,16,256,64]{2,3,1,0:T(8,128)S(1)} %fusion.20, f32[64,16]{0,1:T(8,128)S(1)} %get-tuple-element.21, f32[64,16]{0,1:T(8,128)S(1)} %get-tuple-element.20, f32[3,32,16,256]{3,2,1,0:T(8,128)S(1)} %bitcast.105), kind=kOutput, calls=%fused_computation.4 | convolution fusion | flops 307523584 | bytes 11018240 | tf_op jit(solution)/shard_map/ka,nasc->nksc/dot_general | solution.py:24
  72.7 3.6 copy.41
  76.3 4.3 all-to-all-start.1
  80.6 5.3 copy.43
  85.9 65.7 %all-to-all-done.1 = f32[3,64,16,256]{3,2,0,1:T(8,128)S(1)} async-done(((f32[3,64,16,256]{3,2,0,1:T(8,128)}), f32[3,64,16,256]{3,2,0,1:T(8,128)S(1)}, u32[]{:S(2)}, u32[]{:S(2)}) %all-to-all-start.1) | async-done | bytes 3145760 | tf_op jit(solution)/shard_map/all_to_all | solution.py:85
  151.6 7.6 %all-to-all-start.2 = ((f32[3,64,16,256]{3,2,0,1:T(8,128)}), f32[3,64,16,256]{3,2,0,1:T(8,128)}, u32[]{:S(2)}, u32[]{:S(2)}) async-start(f32[3,64,16,256]{3,2,0,1:T(8,128)} %copy.43), calls=%async_computation.2 | async-start | bytes 6291456 | tf_op jit(solution)/shard_map/all_to_all | solution.py:86
  159.2 0.3 copy.42
  159.5 0.0 copy-start.1
  159.6 1.7 copy-done.1
  161.3 9.0 %fusion.35 = f32[512,3,2,256]{3,0,2,1:T(8,128)S(1)} fusion(f32[3,2,512,256]{3,2,1,0:T(8,128)S(1)} %bitcast.110), kind=kOutput, calls=%fused_computation.51 | convolution fusion | flops 4835508224 | bytes 6291456 | tf_op jit(solution)/shard_map/nkbc,bm->nkmc/dot_general | solution.py:34
  170.3 60.5 %all-to-all-done.2 = f32[3,64,16,256]{3,2,0,1:T(8,128)} async-done(((f32[3,64,16,256]{3,2,0,1:T(8,128)}), f32[3,64,16,256]{3,2,0,1:T(8,128)}, u32[]{:S(2)}, u32[]{:S(2)}) %all-to-all-start.2) | async-done | bytes 3145760 | tf_op jit(solution)/shard_map/all_to_all | solution.py:86
  230.8 2.2 copy.44
  233.0 9.3 %fusion.33 = f32[512,3,2,256]{3,0,2,1:T(8,128)S(1)} fusion(f32[3,2,512,256]{3,2,1,0:T(8,128)S(1)} %bitcast.112), kind=kOutput, calls=%fused_computation.49 | convolution fusion | flops 4835508224 | bytes 6291456 | tf_op jit(solution)/shard_map/nkbc,bm->nkmc/dot_general | solution.py:37
  242.3 0.0 copy-start.2
  242.3 9.5 %add_bitcast_fusion.1 = f32[3,2,512,256]{3,2,1,0:T(8,128)S(1)} fusion(f32[512,3,2,256]{3,0,2,1:T(8,128)S(1)} %fusion.35, f32[3,2,512,256]{3,2,1,0:T(8,128)S(1)} %bitcast.113), kind=kOutput, calls=%fused_computation.21 | convolution fusion | flops 4836294656 | bytes 9437184 | tf_op jit(solution)/shard_map/nkbc,bm->nkmc/dot_general | solution.py:34
  251.9 0.0 copy-done.2
  251.9 9.3 %subtract_bitcast_fusion.1 = f32[3,2,512,256]{3,2,1,0:T(8,128)S(1)} fusion(f32[512,3,2,256]{3,0,2,1:T(8,128)S(1)} %fusion.33, f32[3,2,512,256]{3,2,1,0:T(8,128)S(1)} %bitcast.111), kind=kOutput, calls=%fused_computation.20 | convolution fusion | flops 4836294656 | bytes 9437184 | tf_op jit(solution)/shard_map/nkbc,bm->nkmc/dot_general | solution.py:37
  261.2 0.4 multiply_add_fusion.2
  261.6 0.0 copy-start.15
  261.6 0.0 copy-start.13
  261.6 0.9 multiply_subtract_fusion.2
  262.5 0.0 copy-start.7
  262.5 0.0 copy-start.8
  262.5 0.1 copy-done.15
  262.6 9.2 %fusion.11 = f32[512,3,2,256]{3,0,2,1:T(8,128)S(1)} fusion(f32[1,2,512,256]{3,2,1,0:T(8,128)S(1)} %get-tuple-element.10, f32[1,2,512,256]{3,2,1,0:T(8,128)S(1)} %get-tuple-element.9, f32[1,2,512,256]{3,2,1,0:T(8,128)S(1)} %get-tuple-element.12), kind=kOutput, calls=%fused_computation.23 | convolution fusion | flops 4837081088 | bytes 6291456 | tf_op jit(solution)/shard_map/nkmc,mb->nkbc/dot_general | solution.py:46
  271.8 9.5 %subtract_bitcast_fusion = f32[3,2,512,256]{3,2,1,0:T(8,128)S(1)} fusion(f32[512,3,2,256]{3,0,2,1:T(8,128)S(1)} %fusion.11, f32[1,2,512,256]{3,2,1,0:T(8,128)S(1)} %get-tuple-element.8, f32[1,2,512,256]{3,2,1,0:T(8,128)S(1)} %get-tuple-element.11, f32[1,2,512,256]{3,2,1,0:T(8,128)S(1)} %get-tuple-element.7), kind=kOutput, calls=%fused_computation.19 | convolution fusion | flops 4837867520 | bytes 9437184 | tf_op jit(solution)/shard_map/nkmc,mb->nkbc/dot_general | solution.py:46
  281.3 4.1 copy.45
  285.4 7.7 %all-to-all-start.3 = ((f32[3,2,512,256]{3,1,0,2:T(2,128)}), f32[3,2,512,256]{3,1,0,2:T(2,128)S(1)}, u32[]{:S(2)}, u32[]{:S(2)}) async-start(f32[3,2,512,256]{3,1,0,2:T(2,128)} %copy.45), calls=%async_computation.3 | async-start | bytes 6291456 | tf_op jit(solution)/shard_map/all_to_all | solution.py:107
  293.1 11.1 %fusion.10 = f32[512,3,2,256]{3,0,2,1:T(8,128)S(1)} fusion(f32[1,2,512,256]{3,2,1,0:T(8,128)} %copy-done.8, f32[1,2,512,256]{3,2,1,0:T(8,128)} %copy-done.7, f32[1,2,512,256]{3,2,1,0:T(8,128)} %copy-done.15), kind=kOutput, calls=%fused_computation.22 | convolution fusion | flops 4837081088 | bytes 6291456 | tf_op jit(solution)/shard_map/nkmc,mb->nkbc/dot_general | solution.py:49
  304.3 9.7 %add_bitcast_fusion = f32[3,2,512,256]{3,2,1,0:T(8,128)S(1)} fusion(f32[512,3,2,256]{3,0,2,1:T(8,128)S(1)} %fusion.10, f32[1,2,512,256]{3,2,1,0:T(8,128)S(1)} %copy-done.6, f32[1,2,512,256]{3,2,1,0:T(8,128)S(1)} %copy-done.14, f32[1,2,512,256]{3,2,1,0:T(8,128)S(1)} %copy-done.4), kind=kOutput, calls=%fused_computation.17 | convolution fusion | flops 4837867520 | bytes 9437184 | tf_op jit(solution)/shard_map/nkmc,mb->nkbc/dot_general | solution.py:49
  314.0 4.1 copy.47
  318.1 46.2 %all-to-all-done.3 = f32[3,2,512,256]{3,1,0,2:T(2,128)S(1)} async-done(((f32[3,2,512,256]{3,1,0,2:T(2,128)}), f32[3,2,512,256]{3,1,0,2:T(2,128)S(1)}, u32[]{:S(2)}, u32[]{:S(2)}) %all-to-all-start.3) | async-done | bytes 3145760 | tf_op jit(solution)/shard_map/all_to_all | solution.py:107
  364.4 7.6 %all-to-all-start.4 = ((f32[3,2,512,256]{3,1,0,2:T(2,128)}), f32[3,2,512,256]{3,1,0,2:T(2,128)}, u32[]{:S(2)}, u32[]{:S(2)}) async-start(f32[3,2,512,256]{3,1,0,2:T(2,128)} %copy.47), calls=%async_computation.4 | async-start | bytes 6291456 | tf_op jit(solution)/shard_map/all_to_all | solution.py:108
  371.9 0.0 all-reduce.2.cloned.1.call-start
  372.0 3.5 copy.67
  375.5 4.1 all_to_all.81
  379.5 64.0 %all-to-all-done.4 = f32[3,2,512,256]{3,1,0,2:T(2,128)} async-done(((f32[3,2,512,256]{3,1,0,2:T(2,128)}), f32[3,2,512,256]{3,1,0,2:T(2,128)}, u32[]{:S(2)}, u32[]{:S(2)}) %all-to-all-start.4) | async-done | bytes 3145760 | tf_op jit(solution)/shard_map/all_to_all | solution.py:108
  443.5 5.4 copy.66
  448.9 5.3 all_to_all.85
  454.1 4.3 fusion.2
  458.5 2.3 subtract_bitcast_fusion.2
  460.8 0.9 copy.49
  461.7 47.5 %all_to_all.93 = f32[3,32,16,256]{3,2,0,1:T(8,128)S(1)} all-to-all(f32[3,32,16,256]{3,2,0,1:T(8,128)S(1)} %copy.49), channel_id=1, replica_groups=mesh['dp'=8,'seq'=32] {'seq'}, dimensions={1} | all-to-all | bytes 3145728 | tf_op jit(solution)/shard_map/all_to_all | solution.py:110
  509.3 0.2 copy_multiply_fusion
  509.5 0.0 copy-start.11
  509.5 0.0 copy-start.12
  509.5 1.0 slice_multiply_fusion
  510.5 0.0 all-reduce.2.cloned.1.call-update
  510.5 0.0 copy-done.9
  510.5 0.0 copy-done.10
  510.5 0.9 fusion.41
  511.4 0.0 copy-done.12
  511.4 0.9 fusion.43
  512.3 85.9 %all-reduce.2.cloned.1.call-done = f32[512,256]{1,0:T(8,128)} async-done(((f32[512,256]{1,0:T(8,128)}), f32[512,256]{1,0:T(8,128)}) %all-reduce.2.cloned.1.call-update) | async-done | bytes 524304 | tf_op jit(solution)/shard_map/psum | solution.py:115
  598.2 1.9 copy.69
  (19 shorter events, 0.0 us)
Async XLA Ops:
  12.5 50.0 %all-to-all-start = ((f32[3,1,512,256]{3,1,0,2:T(1,128)}), f32[3,1,512,256]{3,1,0,2:T(1,128)S(1)}, u32[]{:S(2)}, u32[]{:S(2)}) async-start(f32[3,1,512,256]{3,1,0,2:T(1,128)} %copy.37), calls=%async_computation | async-start | bytes 3145728 | tf_op jit(solution)/shard_map/all_to_all | solution.py:83
  76.3 75.3 %all-to-all-start.1 = ((f32[3,64,16,256]{3,2,0,1:T(8,128)}), f32[3,64,16,256]{3,2,0,1:T(8,128)S(1)}, u32[]{:S(2)}, u32[]{:S(2)}) async-start(f32[3,64,16,256]{3,2,0,1:T(8,128)} %copy.41), calls=%async_computation.1 | async-start | bytes 6291456 | tf_op jit(solution)/shard_map/all_to_all | solution.py:85
  151.6 79.1 %all-to-all-start.2 = ((f32[3,64,16,256]{3,2,0,1:T(8,128)}), f32[3,64,16,256]{3,2,0,1:T(8,128)}, u32[]{:S(2)}, u32[]{:S(2)}) async-start(f32[3,64,16,256]{3,2,0,1:T(8,128)} %copy.43), calls=%async_computation.2 | async-start | bytes 6291456 | tf_op jit(solution)/shard_map/all_to_all | solution.py:86
  159.5 1.7 copy-start.1
  242.3 9.5 %copy-start.2 = (f32[3,32,2,16,256]{4,3,1,2,0:T(8,128)S(1)}, f32[3,32,2,16,256]{4,3,1,2,0:T(8,128)}, u32[]{:S(2)}) copy-start(f32[3,32,2,16,256]{4,3,1,2,0:T(8,128)} %copy-done.1) | copy-start | bytes 9437188
  261.6 1.0 copy-start.15
  261.6 10.2 %copy-start.13 = (f32[1,2,512,256]{3,2,1,0:T(8,128)}, f32[1,2,512,256]{3,2,1,0:T(8,128)S(1)}, u32[]{:S(2)}) copy-start(f32[1,2,512,256]{3,2,1,0:T(8,128)S(1)} %get-tuple-element.11) | copy-start | bytes 3145732
  262.5 9.3 %copy-start.7 = (f32[1,2,512,256]{3,2,1,0:T(8,128)}, f32[1,2,512,256]{3,2,1,0:T(8,128)S(1)}, u32[]{:S(2)}) copy-start(f32[1,2,512,256]{3,2,1,0:T(8,128)S(1)} %get-tuple-element.9) | copy-start | bytes 3145732
  262.5 9.3 %copy-start.8 = (f32[1,2,512,256]{3,2,1,0:T(8,128)}, f32[1,2,512,256]{3,2,1,0:T(8,128)S(1)}, u32[]{:S(2)}) copy-start(f32[1,2,512,256]{3,2,1,0:T(8,128)S(1)} %get-tuple-element.10) | copy-start | bytes 3145732
  262.5 9.4 %copy-start.3 = (f32[1,2,512,256]{3,2,1,0:T(8,128)}, f32[1,2,512,256]{3,2,1,0:T(8,128)S(1)}, u32[]{:S(2)}) copy-start(f32[1,2,512,256]{3,2,1,0:T(8,128)S(1)} %get-tuple-element.7) | copy-start | bytes 3145732
  262.5 9.4 %copy-start.5 = (f32[1,2,512,256]{3,2,1,0:T(8,128)}, f32[1,2,512,256]{3,2,1,0:T(8,128)S(1)}, u32[]{:S(2)}) copy-start(f32[1,2,512,256]{3,2,1,0:T(8,128)S(1)} %get-tuple-element.8) | copy-start | bytes 3145732
  285.4 79.0 %all-to-all-start.3 = ((f32[3,2,512,256]{3,1,0,2:T(2,128)}), f32[3,2,512,256]{3,1,0,2:T(2,128)S(1)}, u32[]{:S(2)}, u32[]{:S(2)}) async-start(f32[3,2,512,256]{3,1,0,2:T(2,128)} %copy.45), calls=%async_computation.3 | async-start | bytes 6291456 | tf_op jit(solution)/shard_map/all_to_all | solution.py:107
  293.1 11.2 %copy-start.4 = (f32[1,2,512,256]{3,2,1,0:T(8,128)S(1)}, f32[1,2,512,256]{3,2,1,0:T(8,128)}, u32[]{:S(2)}) copy-start(f32[1,2,512,256]{3,2,1,0:T(8,128)} %copy-done.3) | copy-start | bytes 3145732
  293.1 11.2 %copy-start.6 = (f32[1,2,512,256]{3,2,1,0:T(8,128)S(1)}, f32[1,2,512,256]{3,2,1,0:T(8,128)}, u32[]{:S(2)}) copy-start(f32[1,2,512,256]{3,2,1,0:T(8,128)} %copy-done.5) | copy-start | bytes 3145732
  293.1 11.2 %copy-start.14 = (f32[1,2,512,256]{3,2,1,0:T(8,128)S(1)}, f32[1,2,512,256]{3,2,1,0:T(8,128)}, u32[]{:S(2)}) copy-start(f32[1,2,512,256]{3,2,1,0:T(8,128)} %copy-done.13) | copy-start | bytes 3145732
  364.4 79.1 %all-to-all-start.4 = ((f32[3,2,512,256]{3,1,0,2:T(2,128)}), f32[3,2,512,256]{3,1,0,2:T(2,128)}, u32[]{:S(2)}, u32[]{:S(2)}) async-start(f32[3,2,512,256]{3,1,0,2:T(2,128)} %copy.47), calls=%async_computation.4 | async-start | bytes 6291456 | tf_op jit(solution)/shard_map/all_to_all | solution.py:108
  371.9 226.3 %all-reduce.2.cloned.1.call-start = ((), (), s32[]{:S(2)}) async-start(), calls=%async_computation.6 | async-start | bytes 1048576 | tf_op jit(solution)/shard_map/psum | solution.py:115
  454.1 4.3 copy-start
  509.2 1.2 copy-start.9
  509.2 1.3 copy-start.10
  509.5 1.9 copy-start.11
  509.5 1.9 copy-start.12
Sparse Core Ops, SparseCore 0:
  510.6 87.5 all-reduce.1
where the time goes:
time: 616 us; the launch traced here: 607 us
  waiting for transfers between devices  362 us (59%)
  matrix products  93.3 us (15%)
  blocking collectives  47.5 us (8%)
  local copies, waits for them, and re-layouts  45.4 us (7%)
  starting transfers between devices  37.1 us (6%)
  between operations  14.6 us (2%)
  other arithmetic  6.83 us (1%)
    psum x1, waiting for transfers between devices, local(): filter_grad = lax.psum(results[lag_index, 0] * norm_factor, 'dp')  85.9 us
    all_to_all x1, waiting for transfers between devices, local(): lax.all_to_all(first_arr, 'seq', split_axis=1, concat_axis=2, tiled=True)  65.7 us
    all_to_all x1, waiting for transfers between devices, local(): lax.all_to_all(second_arr, 'seq', split_axis=2, concat_axis=1, tiled=True)  64 us
    all_to_all x1, waiting for transfers between devices, local(): lax.all_to_all(second_arr, 'seq', split_axis=1, concat_axis=2, tiled=True)  60.5 us
    all_to_all x1, blocking collectives, local(): lax.all_to_all(moved, 'seq', split_axis=1, concat_axis=2, tiled=True)  47.5 us
    all_to_all x1, waiting for transfers between devices, local(): lax.all_to_all(first_arr, 'seq', split_axis=2, concat_axis=1, tiled=True)  46.2 us
    all_to_all x1, waiting for transfers between devices, local(): lax.all_to_all(moved, 'seq', split_axis=2, concat_axis=1, tiled=True)  40 us
  transfers between devices with their start and end apart: 6, of which 6 were waited for; matrix products, arithmetic and copies ran while one was open for 7% of the time, Pallas kernels for 0%

commit v1 on v0

v1 whole, which is shorter than its diff:
```python
import math

import jax
import jax.numpy as jnp
import ml_dtypes
import numpy as np
from jax import lax
from jax.experimental import pallas as pl
from jax.experimental.pallas import tpu as pltpu
from jax.sharding import PartitionSpec as P

LANES = 128
BLOCK = 512
CHANNELS = 256
SEQS = 8
OWNERS = 32
PIECES = BLOCK // LANES
ROWS_IN = 2 * PIECES + 1
ROWS_OUT = 3 * PIECES
HALF = 128
LENGTH = 2 * BLOCK * OWNERS
VMEM_LIMIT = 56 << 20


def split_parts(values):
    high = values.astype(np.float32).astype(ml_dtypes.bfloat16)
    low = (values - high.astype(np.float64)).astype(np.float32).astype(ml_dtypes.bfloat16)
    return high, low


def constants():
    freq = np.arange(HALF, dtype=np.int64)
    rows = np.arange(HALF, dtype=np.int64)
    coarse = (rows % OWNERS) * PIECES + rows // OWNERS
    turn = 2.0 * np.pi * (np.outer(2 * freq + 1, coarse) % (4 * HALF)) / (4 * HALF)
    outer = np.concatenate([np.cos(turn), -np.sin(turn)], axis=0)
    outer_high, outer_low = split_parts(outer)
    outer_cat = np.concatenate([outer_high, outer_high, outer_low], axis=1)
    scale = 2.0 / LENGTH / math.sqrt(LENGTH // 2)
    back_outer = outer.T * scale
    back_high, back_low = split_parts(back_outer)
    back_cat = np.concatenate([back_high, back_high, back_low], axis=1)
    lanes = np.arange(LANES, dtype=np.int64)
    inner_turn = 2.0 * np.pi * (np.outer(lanes, lanes) % LANES) / LANES
    cos_in, sin_in = np.cos(inner_turn), np.sin(inner_turn)
    inner = np.block([[cos_in, -sin_in], [sin_in, cos_in]])
    inner_high, inner_low = split_parts(inner)
    inner_cat = np.concatenate([inner_high, inner_high, inner_low], axis=0)
    inner_back = np.concatenate([inner_high.T, inner_high.T, inner_low.T], axis=0)
    twist = 2.0 * np.pi * np.outer(2 * freq + 1, lanes) / (2 * LENGTH)
    twiddle = np.stack([np.cos(twist), np.sin(twist)]).astype(np.float32)
    return (outer_cat, inner_cat, inner_back, back_cat, twiddle)


def pre_kernel(part_ref, q_ref, k_ref, v_ref, u_ref, f_ref, out_ref):
    del part_ref
    for piece in range(PIECES):
        at = pl.ds(piece * LANES, LANES)
        mixed = k_ref[0, at, :].astype(jnp.float32) * v_ref[0, at, :].astype(jnp.float32)
        gated = u_ref[0, at, :].astype(jnp.float32) * q_ref[0, at, :].astype(jnp.float32)
        out_ref[pl.ds(piece, CHANNELS, stride=ROWS_IN), :] = mixed.T
        out_ref[pl.ds(PIECES + piece, CHANNELS, stride=ROWS_IN), :] = gated.T
    out_ref[pl.ds(2 * PIECES, CHANNELS, stride=ROWS_IN), :] = f_ref[...].T


def halves(value, axis):
    high = value.astype(jnp.bfloat16)
    low = (value - high.astype(jnp.float32)).astype(jnp.bfloat16)
    return jnp.concatenate([high, low, high], axis=axis)


def dot(left, right):
    return jnp.dot(left, right, preferred_element_type=jnp.float32)


def fft_kernel(in_ref, outer_ref, inner_ref, inner_back_ref, back_ref, twiddle_ref, out_ref):
    cos_t = twiddle_ref[0]
    sin_t = twiddle_ref[1]

    def spectra(signals):
        stacked = halves(jnp.concatenate(signals, axis=1), 0)
        first = dot(outer_ref[...], stacked)
        turned = []
        for index in range(len(signals)):
            at = slice(index * LANES, (index + 1) * LANES)
            real, imag = first[:HALF, at], first[HALF:, at]
            turned.append(
                jnp.concatenate([real * cos_t + imag * sin_t, imag * cos_t - real * sin_t], axis=1)
            )
        return dot(halves(jnp.concatenate(turned, axis=0), 1), inner_ref[...])

    def signals_of(spectrum_list):
        rows = dot(halves(jnp.concatenate(spectrum_list, axis=0), 1), inner_back_ref[...])
        turned = []
        for index in range(len(spectrum_list)):
            at = slice(index * HALF, (index + 1) * HALF)
            real, imag = rows[at, :LANES], rows[at, LANES:]
            turned.append(
                jnp.concatenate([real * cos_t - imag * sin_t, imag * cos_t + real * sin_t], axis=0)
            )
        return dot(back_ref[...], halves(jnp.concatenate(turned, axis=1), 0))

    taps = jnp.concatenate(
        [
            in_ref[pl.ds(2 * piece * OWNERS * ROWS_IN + 2 * PIECES, OWNERS, stride=ROWS_IN), :]
            for piece in range(PIECES)
        ],
        axis=0,
    )
    taps_spec = spectra([taps])
    taps_real, taps_imag = taps_spec[:, :LANES], taps_spec[:, LANES:]
    lag_real = jnp.zeros((HALF, LANES), jnp.float32)
    lag_imag = jnp.zeros((HALF, LANES), jnp.float32)
    for seq in range(SEQS):
        signals = [
            jnp.concatenate(
                [
                    in_ref[pl.ds(seq * OWNERS * ROWS_IN + which * PIECES + piece, OWNERS, stride=ROWS_IN), :]
                    for piece in range(PIECES)
                ],
                axis=0,
            )
            for which in range(2)
        ]
        spec = spectra(signals)
        mixed_real, mixed_imag = spec[:HALF, :LANES], spec[:HALF, LANES:]
        gated_real, gated_imag = spec[HALF:, :LANES], spec[HALF:, LANES:]
        conv = jnp.concatenate(
            [
                taps_real * mixed_real - taps_imag * mixed_imag,
                taps_real * mixed_imag + taps_imag * mixed_real,
            ],
            axis=1,
        )
        back = jnp.concatenate(
            [
                taps_real * gated_real + taps_imag * gated_imag,
                taps_real * gated_imag - taps_imag * gated_real,
            ],
            axis=1,
        )
        lag_real = lag_real + (mixed_real * gated_real + mixed_imag * gated_imag)
        lag_imag = lag_imag + (mixed_real * gated_imag - mixed_imag * gated_real)
        result = signals_of([conv, back])
        for which in range(2):
            for piece in range(PIECES):
                out_ref[
                    pl.ds(seq * OWNERS * ROWS_OUT + which * PIECES + piece, OWNERS, stride=ROWS_OUT), :
                ] = result[piece * OWNERS : (piece + 1) * OWNERS, which * LANES : (which + 1) * LANES]
    lag = signals_of([jnp.concatenate([lag_real, lag_imag], axis=1)])
    for seq in range(SEQS):
        for piece in range(PIECES):
            out_ref[
                pl.ds(seq * OWNERS * ROWS_OUT + 2 * PIECES + piece, OWNERS, stride=ROWS_OUT), :
            ] = lag[piece * OWNERS : (piece + 1) * OWNERS, :]


def post_kernel(c_ref, q_ref, k_ref, v_ref, u_ref, o_ref, qg_ref, kg_ref, vg_ref, fg_ref):
    for piece in range(PIECES):
        at = pl.ds(piece * LANES, LANES)
        conv = c_ref[pl.ds(piece, CHANNELS, stride=ROWS_OUT), :].T
        back = c_ref[pl.ds(PIECES + piece, CHANNELS, stride=ROWS_OUT), :].T
        o_ref[0, at, :] = (q_ref[0, at, :].astype(jnp.float32) * conv).astype(jnp.bfloat16)
        qg_ref[0, at, :] = (u_ref[0, at, :].astype(jnp.float32) * conv).astype(jnp.bfloat16)
        kg_ref[0, at, :] = (back * v_ref[0, at, :].astype(jnp.float32)).astype(jnp.bfloat16)
        vg_ref[0, at, :] = (back * k_ref[0, at, :].astype(jnp.float32)).astype(jnp.bfloat16)
        fg_ref[at, :] = c_ref[pl.ds(2 * PIECES + piece, CHANNELS, stride=ROWS_OUT), :].T


def params():
    return pltpu.CompilerParams(vmem_limit_bytes=VMEM_LIMIT)


def pre(part, query_seq, key_seq, value_seq, upstream, filter_param):
    whole = pl.BlockSpec((1, BLOCK, CHANNELS), lambda i, part: (0, 0, 0))
    return pl.pallas_call(
        pre_kernel,
        out_shape=jax.ShapeDtypeStruct((CHANNELS * ROWS_IN, LANES), jnp.float32),
        grid_spec=pltpu.PrefetchScalarGridSpec(
            num_scalar_prefetch=1,
            grid=(1,),
            in_specs=[whole] * 4 + [pl.BlockSpec((LANES, CHANNELS), lambda i, part: (part[0], 0))],
            out_specs=pl.BlockSpec((CHANNELS * ROWS_IN, LANES), lambda i, part: (0, 0)),
        ),
        compiler_params=params(),
    )(part, query_seq, key_seq, value_seq, upstream, filter_param)


def transform(arrived, tables):
    return pl.pallas_call(
        fft_kernel,
        out_shape=jax.ShapeDtypeStruct((SEQS * OWNERS * ROWS_OUT, LANES), jnp.float32),
        compiler_params=params(),
    )(arrived, *tables)


def post(returned, query_seq, key_seq, value_seq, upstream):
    half = jax.ShapeDtypeStruct((1, BLOCK, CHANNELS), jnp.bfloat16)
    return pl.pallas_call(
        post_kernel,
        out_shape=(half, half, half, half, jax.ShapeDtypeStruct((BLOCK, CHANNELS), jnp.float32)),
        compiler_params=params(),
    )(returned, query_seq, key_seq, value_seq, upstream)


def exchange(rows, depth):
    shaped = rows.reshape(CHANNELS, depth, 1, LANES)
    moved = lax.all_to_all(shaped, ("dp", "seq"), split_axis=0, concat_axis=0, tiled=True)
    return moved.reshape(CHANNELS * depth, LANES)


def local(query_seq, key_seq, value_seq, upstream, filter_param):
    tables = [jnp.asarray(table) for table in constants()]
    part = (lax.axis_index("dp") // 2).astype(jnp.int32).reshape(1)
    sent = pre(part, query_seq, key_seq, value_seq, upstream, filter_param)
    arrived = exchange(sent, ROWS_IN)
    results = transform(arrived, tables)
    returned = exchange(results, ROWS_OUT)
    return post(returned, query_seq, key_seq, value_seq, upstream)


def solution(mesh):
    in_specs = (
        P("dp", "seq", None),
        P("dp", "seq", None),
        P("dp", "seq", None),
        P("dp", "seq", None),
        P("seq", None),
    )
    out_specs = (
        P("dp", "seq", None),
        P("dp", "seq", None),
        P("dp", "seq", None),
        P("dp", "seq", None),
        P("seq", None),
    )
    return jax.shard_map(local, mesh=mesh, in_specs=in_specs, out_specs=out_specs, check_vma=False)
```

time: 616 us -> 115 us (0.19)
  the two profiles are of different devices: /device:TPU:32 before, /device:TPU:1 now
where the time goes in v1:
time: 115 us
  blocking collectives  98.3 us (85%)
  Pallas kernels  16.2 us (14%)
    all_to_all x2, blocking collectives, exchange(): lax.all_to_all(shaped, ('dp', 'seq'), split_axis=0, concat_axis=0, tiled=...  98.3 us
    pallas_call x1, Pallas kernels, transform(): pl.pallas_call(fft_kernel, out_shape=jax.ShapeDtypeStruct((SEQS * OWNERS...  10.4 us
    pallas_call x1, Pallas kernels, post(): pl.pallas_call(post_kernel, out_shape=(half, half, half, half, jax.ShapeD...  3.2 us
    pallas_call x1, Pallas kernels, pre(): pl.pallas_call(pre_kernel, out_shape=jax.ShapeDtypeStruct((CHANNELS * ROW...  2.6 us

profile of v1, /device:TPU:1, one launch (start us, length us, event | category | flops | bytes accessed | tf_op | source)
XLA Modules:
  0.0 115.2 jit_solution(2629238511070347884)
XLA Ops:
  0.6 2.6 %shard_map.137 = f32[2304,128]{1,0:T(8,128)} custom-call(s32[1]{0:T(128)} %bitcast.part_ref, bf16[1,512,256]{2,1,0:T(8,128)(2,1)} %q_ref.3, bf16[1,512,256]{2,1,0:T(8,128)(2,1)} %k_ref.3, bf16[1,512,256]{2,1,0:T(8,128)(2,1)} %v_ref.3, bf16[1,512,256]{2,1,0:T(8,128)(2,1)} %u_ref.3, f32[512,256]{1,0:T(8,128)} %f_ref.1), custom_call_target="tpu_custom_call" | custom-call | tf_op jit(solution)/shard_map/pallas_call | solution.py:176
  3.2 49.5 %all_to_all.10 = f32[256,9,1,128]{3,2,1,0:T(1,128)} all-to-all(f32[256,9,1,128]{3,2,1,0:T(1,128)} %bitcast.7), channel_id=1, replica_groups=mesh['dp'=8,'seq'=32] {'dp','seq'}, dimensions={0} | all-to-all | bytes 2359296 | tf_op jit(solution)/shard_map/all_to_all | solution.py:208
  52.7 10.4 %shard_map.138 = f32[3072,128]{1,0:T(8,128)} custom-call(f32[2304,128]{1,0:T(8,128)} %bitcast.8, bf16[256,384]{1,0:T(8,128)(2,1)} %constant.30.clone.outer_ref, bf16[768,256]{1,0:T(8,128)(2,1)} %constant.31.clone.inner_ref, bf16[768,256]{1,0:T(8,128)(2,1)} %constant.32.clone.inner_back_ref, bf16[128,768]{1,0:T(8,128)(2,1)} %constant.33.clone.back_ref, ...), custom_call_target="tpu_custom_call" | custom-call | tf_op jit(solution)/shard_map/pallas_call | solution.py:190
  63.1 48.8 %all_to_all.11 = f32[256,12,1,128]{3,2,1,0:T(1,128)} all-to-all(f32[256,12,1,128]{3,2,1,0:T(1,128)} %bitcast.6), channel_id=1, replica_groups=mesh['dp'=8,'seq'=32] {'dp','seq'}, dimensions={0} | all-to-all | bytes 3145728 | tf_op jit(solution)/shard_map/all_to_all | solution.py:208
  112.0 3.2 %shard_map.139 = (bf16[1,512,256]{2,1,0:T(8,128)(2,1)}, bf16[1,512,256]{2,1,0:T(8,128)(2,1)}, bf16[1,512,256]{2,1,0:T(8,128)(2,1)}, bf16[1,512,256]{2,1,0:T(8,128)(2,1)}, f32[512,256]{1,0:T(8,128)}) custom-call(f32[3072,128]{1,0:T(8,128)} %bitcast.5, bf16[1,512,256]{2,1,0:T(8,128)(2,1)} %q_ref.3, bf16[1,512,256]{2,1,0:T(8,128)(2,1)} %k_ref.3, ...), custom_call_target="tpu_custom_call" | custom-call | tf_op jit(solution)/shard_map/pallas_call | solution.py:199

commit v2 on v1

--- a/solution.py
+++ b/solution.py
@@ -19,7 +19,8 @@
 ROWS_OUT = 3 * PIECES
 HALF = 128
 LENGTH = 2 * BLOCK * OWNERS
-VMEM_LIMIT = 56 << 20
+GROUP = 4
+VMEM_LIMIT = 32 << 20
 
 
 def split_parts(values):
@@ -77,9 +78,13 @@
     cos_t = twiddle_ref[0]
     sin_t = twiddle_ref[1]
 
-    def spectra(signals):
-        stacked = halves(jnp.concatenate(signals, axis=1), 0)
-        first = dot(outer_ref[...], stacked)
+    def load(base):
+        return jnp.concatenate(
+            [in_ref[pl.ds(base + piece, OWNERS, stride=ROWS_IN), :] for piece in range(PIECES)], axis=0
+        )
+
+    def outer(signals):
+        first = dot(outer_ref[...], halves(jnp.concatenate(signals, axis=1), 0))
         turned = []
         for index in range(len(signals)):
             at = slice(index * LANES, (index + 1) * LANES)
@@ -87,18 +92,26 @@
             turned.append(
                 jnp.concatenate([real * cos_t + imag * sin_t, imag * cos_t - real * sin_t], axis=1)
             )
-        return dot(halves(jnp.concatenate(turned, axis=0), 1), inner_ref[...])
-
-    def signals_of(spectrum_list):
-        rows = dot(halves(jnp.concatenate(spectrum_list, axis=0), 1), inner_back_ref[...])
+        return turned
+
+    def inner(blocks, table_ref):
+        return dot(halves(jnp.concatenate(blocks, axis=0), 1), table_ref[...])
+
+    def outer_back(rows):
         turned = []
-        for index in range(len(spectrum_list)):
+        for index in range(rows.shape[0] // HALF):
             at = slice(index * HALF, (index + 1) * HALF)
             real, imag = rows[at, :LANES], rows[at, LANES:]
             turned.append(
                 jnp.concatenate([real * cos_t - imag * sin_t, imag * cos_t + real * sin_t], axis=0)
             )
         return dot(back_ref[...], halves(jnp.concatenate(turned, axis=1), 0))
+
+    def store(result, base):
+        for piece in range(PIECES):
+            out_ref[pl.ds(base + piece, OWNERS, stride=ROWS_OUT), :] = result[
+                piece * OWNERS : (piece + 1) * OWNERS, :
+            ]
 
     taps = jnp.concatenate(
         [
@@ -107,52 +120,57 @@
         ],
         axis=0,
     )
-    taps_spec = spectra([taps])
-    taps_real, taps_imag = taps_spec[:, :LANES], taps_spec[:, LANES:]
     lag_real = jnp.zeros((HALF, LANES), jnp.float32)
     lag_imag = jnp.zeros((HALF, LANES), jnp.float32)
+    for start in range(0, SEQS, GROUP):
+        turned = []
+        for seq in range(start, start + GROUP):
+            base = seq * OWNERS * ROWS_IN
+            turned += outer([load(base), load(base + PIECES)])
+        if start == 0:
+            turned += outer([taps])
+        spec = inner(turned, inner_ref)
+        if start == 0:
+            taps_real, taps_imag = spec[2 * GROUP * HALF :, :LANES], spec[2 * GROUP * HALF :, LANES:]
+        products = []
+        for index in range(GROUP):
+            at = slice(2 * index * HALF, (2 * index + 1) * HALF)
+            mixed_real, mixed_imag = spec[at, :LANES], spec[at, LANES:]
+            at = slice((2 * index + 1) * HALF, (2 * index + 2) * HALF)
+            gated_real, gated_imag = spec[at, :LANES], spec[at, LANES:]
+            products.append(
+                jnp.concatenate(
+                    [
+                        taps_real * mixed_real - taps_imag * mixed_imag,
+                        taps_real * mixed_imag + taps_imag * mixed_real,
+                    ],
+                    axis=1,
+                )
+            )
+            products.append(
+                jnp.concatenate(
+                    [
+                        taps_real * gated_real + taps_imag * gated_imag,
+                        taps_real * gated_imag - taps_imag * gated_real,
+                    ],
+                    axis=1,
+                )
+            )
+            lag_real = lag_real + (mixed_real * gated_real + mixed_imag * gated_imag)
+            lag_imag = lag_imag + (mixed_real * gated_imag - mixed_imag * gated_real)
+        last = start + GROUP == SEQS
+        if last:
+            products.append(jnp.concatenate([lag_real, lag_imag], axis=1))
+        rows = inner(products, inner_back_ref)
+        for index in range(GROUP):
+            result = outer_back(rows[2 * index * HALF : 2 * (index + 1) * HALF])
+            base = (start + index) * OWNERS * ROWS_OUT
+            store(result[:, :LANES], base)
+            store(result[:, LANES:], base + PIECES)
+        if last:
+            lag = outer_back(rows[2 * GROUP * HALF :])
     for seq in range(SEQS):
-        signals = [
-            jnp.concatenate(
-                [
-                    in_ref[pl.ds(seq * OWNERS * ROWS_IN + which * PIECES + piece, OWNERS, stride=ROWS_IN), :]
-                    for piece in range(PIECES)
-                ],
-                axis=0,
-            )
-            for which in range(2)
-        ]
-        spec = spectra(signals)
-        mixed_real, mixed_imag = spec[:HALF, :LANES], spec[:HALF, LANES:]
-        gated_real, gated_imag = spec[HALF:, :LANES], spec[HALF:, LANES:]
-        conv = jnp.concatenate(
-            [
-                taps_real * mixed_real - taps_imag * mixed_imag,
-                taps_real * mixed_imag + taps_imag * mixed_real,
-            ],
-            axis=1,
-        )
-        back = jnp.concatenate(
-            [
-                taps_real * gated_real + taps_imag * gated_imag,
-                taps_real * gated_imag - taps_imag * gated_real,
-            ],
-            axis=1,
-        )
-        lag_real = lag_real + (mixed_real * gated_real + mixed_imag * gated_imag)
-        lag_imag = lag_imag + (mixed_real * gated_imag - mixed_imag * gated_real)
-        result = signals_of([conv, back])
-        for which in range(2):
-            for piece in range(PIECES):
-                out_ref[
-                    pl.ds(seq * OWNERS * ROWS_OUT + which * PIECES + piece, OWNERS, stride=ROWS_OUT), :
-                ] = result[piece * OWNERS : (piece + 1) * OWNERS, which * LANES : (which + 1) * LANES]
-    lag = signals_of([jnp.concatenate([lag_real, lag_imag], axis=1)])
-    for seq in range(SEQS):
-        for piece in range(PIECES):
-            out_ref[
-                pl.ds(seq * OWNERS * ROWS_OUT + 2 * PIECES + piece, OWNERS, stride=ROWS_OUT), :
-            ] = lag[piece * OWNERS : (piece + 1) * OWNERS, :]
+        store(lag, seq * OWNERS * ROWS_OUT + 2 * PIECES)
 
 
 def post_kernel(c_ref, q_ref, k_ref, v_ref, u_ref, o_ref, qg_ref, kg_ref, vg_ref, fg_ref):
@@ -211,7 +229,7 @@
 
 def local(query_seq, key_seq, value_seq, upstream, filter_param):
     tables = [jnp.asarray(table) for table in constants()]
-    part = (lax.axis_index("dp") // 2).astype(jnp.int32).reshape(1)
+    part = lax.div(lax.axis_index("dp"), 2).astype(jnp.int32).reshape(1)
     sent = pre(part, query_seq, key_seq, value_seq, upstream, filter_param)
     arrived = exchange(sent, ROWS_IN)
     results = transform(arrived, tables)

time: 115 us -> 110 us (0.957)
  Pallas kernels: 16.2 us -> 6.64 us
  local copies, waits for them, and re-layouts: 0 us -> 4.89 us
    pallas_call x1, Pallas kernels: 10.4 us -> 4.74 us  [transform(): pl.pallas_call(fft_kernel, out_shape=jax.ShapeDtypeStruct((SEQS * OWNERS...]
    unnamed x0 -> x28, local copies, waits for them, and re-layouts: none -> 4.89 us
    pallas_call x1, Pallas kernels: 2.6 us -> 0.36 us  [pre(): pl.pallas_call(pre_kernel, out_shape=jax.ShapeDtypeStruct((CHANNELS * ROW...]
    pallas_call x1, Pallas kernels: 3.2 us -> 1.55 us  [post(): pl.pallas_call(post_kernel, out_shape=(half, half, half, half, jax.ShapeD...]
where the time goes in v2:
time: 110 us
  blocking collectives  97.7 us (89%)
  Pallas kernels  6.64 us (6%)
  local copies, waits for them, and re-layouts  4.89 us (4%)
    all_to_all x2, blocking collectives, exchange(): lax.all_to_all(shaped, ('dp', 'seq'), split_axis=0, concat_axis=0, tiled=...  97.7 us
    unnamed x28, local copies, waits for them, and re-layouts  4.89 us
    pallas_call x1, Pallas kernels, transform(): pl.pallas_call(fft_kernel, out_shape=jax.ShapeDtypeStruct((SEQS * OWNERS...  4.74 us

profile of v2, /device:TPU:1, one launch (start us, length us, event | category | flops | bytes accessed | tf_op | source)
XLA Modules:
  0.0 110.0 jit_solution(5897357963292517142)
XLA Ops:
  0.6 0.0 copy-start
  0.6 0.9 copy-done
  1.6 0.0 copy-start.2
  1.6 0.9 copy-done.2
  2.5 0.0 copy-start.4
  2.5 0.9 copy-done.4
  3.5 0.0 copy-start.6
  3.5 0.9 copy-done.6
  4.4 0.0 copy-start.8
  4.4 1.0 copy-done.8
  5.5 0.4 shard_map.137
  5.8 0.0 copy-start.9
  5.9 0.0 copy-start.10
  5.9 0.0 copy-start.11
  5.9 0.0 copy-start.12
  5.9 0.0 copy-start.13
  5.9 49.2 %all_to_all.10 = f32[256,9,1,128]{3,2,1,0:T(1,128)S(1)} all-to-all(f32[256,9,1,128]{3,2,1,0:T(1,128)S(1)} %bitcast.7), channel_id=1, replica_groups=mesh['dp'=8,'seq'=32] {'dp','seq'}, dimensions={0} | all-to-all | bytes 2359296 | tf_op jit(solution)/shard_map/all_to_all | solution.py:226
  55.1 0.0 copy-done.9
  55.1 0.0 copy-done.10
  55.1 0.0 copy-done.11
  55.1 0.0 copy-done.12
  55.1 0.0 copy-done.13
  55.1 4.7 %shard_map.138 = f32[3072,128]{1,0:T(8,128)S(1)} custom-call(f32[2304,128]{1,0:T(8,128)S(1)} %bitcast.8, bf16[256,384]{1,0:T(8,128)(2,1)S(1)} %copy-done.12, bf16[768,256]{1,0:T(8,128)(2,1)S(1)} %copy-done.10, bf16[768,256]{1,0:T(8,128)(2,1)S(1)} %copy-done.9, bf16[128,768]{1,0:T(8,128)(2,1)S(1)} %copy-done.11, f32[2,128,128]{2,1,0:T(8,128)S(1)} %copy-done.13), custom_call_target="tpu_custom_call" | custom-call | tf_op jit(solution)/shard_map/pallas_call | solution.py:208
  59.9 0.0 copy-start.1
  59.9 0.0 copy-start.3
  59.9 0.0 copy-start.5
  59.9 0.0 copy-start.7
  59.9 48.5 %all_to_all.11 = f32[256,12,1,128]{3,2,1,0:T(1,128)S(1)} all-to-all(f32[256,12,1,128]{3,2,1,0:T(1,128)S(1)} %bitcast.6), channel_id=1, replica_groups=mesh['dp'=8,'seq'=32] {'dp','seq'}, dimensions={0} | all-to-all | bytes 3145728 | tf_op jit(solution)/shard_map/all_to_all | solution.py:226
  108.5 0.0 copy-done.1
  108.5 0.0 copy-done.3
  108.5 0.0 copy-done.5
  108.5 0.0 copy-done.7
  108.5 1.5 %shard_map.139 = (bf16[1,512,256]{2,1,0:T(8,128)(2,1)}, bf16[1,512,256]{2,1,0:T(8,128)(2,1)}, bf16[1,512,256]{2,1,0:T(8,128)(2,1)}, bf16[1,512,256]{2,1,0:T(8,128)(2,1)}, f32[512,256]{1,0:T(8,128)}) custom-call(f32[3072,128]{1,0:T(8,128)S(1)} %bitcast.5, bf16[1,512,256]{2,1,0:T(8,128)(2,1)S(1)} %copy-done.1, bf16[1,512,256]{2,1,0:T(8,128)(2,1)S(1)} %copy-done.3, ...), custom_call_target="tpu_custom_call" | custom-call | tf_op jit(solution)/shard_map/pallas_call | solution.py:217
Async XLA Ops:
  0.6 1.0 copy-start
  1.6 0.9 copy-start.2
  2.5 0.9 copy-start.4
  3.5 0.9 copy-start.6
  4.4 1.0 copy-start.8
  5.8 49.3 %copy-start.9 = (bf16[768,256]{1,0:T(8,128)(2,1)S(1)}, bf16[768,256]{1,0:T(8,128)(2,1)}, u32[]{:S(2)}) copy-start(bf16[768,256]{1,0:T(8,128)(2,1)} %constant.23.clone.inner_back_ref) | copy-start | bytes 1179652
  5.9 49.3 %copy-start.10 = (bf16[768,256]{1,0:T(8,128)(2,1)S(1)}, bf16[768,256]{1,0:T(8,128)(2,1)}, u32[]{:S(2)}) copy-start(bf16[768,256]{1,0:T(8,128)(2,1)} %constant.22.clone.inner_ref) | copy-start | bytes 1179652
  5.9 49.2 %copy-start.11 = (bf16[128,768]{1,0:T(8,128)(2,1)S(1)}, bf16[128,768]{1,0:T(8,128)(2,1)}, u32[]{:S(2)}) copy-start(bf16[128,768]{1,0:T(8,128)(2,1)} %constant.24.clone.back_ref) | copy-start | bytes 589828
  5.9 49.2 %copy-start.12 = (bf16[256,384]{1,0:T(8,128)(2,1)S(1)}, bf16[256,384]{1,0:T(8,128)(2,1)}, u32[]{:S(2)}) copy-start(bf16[256,384]{1,0:T(8,128)(2,1)} %constant.21.clone.outer_ref) | copy-start | bytes 589828
  5.9 49.2 %copy-start.13 = (f32[2,128,128]{2,1,0:T(8,128)S(1)}, f32[2,128,128]{2,1,0:T(8,128)}, u32[]{:S(2)}) copy-start(f32[2,128,128]{2,1,0:T(8,128)} %constant.25.clone.twiddle_ref) | copy-start | bytes 393220
  59.9 48.6 %copy-start.1 = (bf16[1,512,256]{2,1,0:T(8,128)(2,1)S(1)}, bf16[1,512,256]{2,1,0:T(8,128)(2,1)}, u32[]{:S(2)}) copy-start(bf16[1,512,256]{2,1,0:T(8,128)(2,1)} %q_ref.3) | copy-start | bytes 786436
  59.9 48.6 %copy-start.3 = (bf16[1,512,256]{2,1,0:T(8,128)(2,1)S(1)}, bf16[1,512,256]{2,1,0:T(8,128)(2,1)}, u32[]{:S(2)}) copy-start(bf16[1,512,256]{2,1,0:T(8,128)(2,1)} %k_ref.3) | copy-start | bytes 786436
  59.9 48.6 %copy-start.5 = (bf16[1,512,256]{2,1,0:T(8,128)(2,1)S(1)}, bf16[1,512,256]{2,1,0:T(8,128)(2,1)}, u32[]{:S(2)}) copy-start(bf16[1,512,256]{2,1,0:T(8,128)(2,1)} %v_ref.3) | copy-start | bytes 786436
  59.9 48.6 %copy-start.7 = (bf16[1,512,256]{2,1,0:T(8,128)(2,1)S(1)}, bf16[1,512,256]{2,1,0:T(8,128)(2,1)}, u32[]{:S(2)}) copy-start(bf16[1,512,256]{2,1,0:T(8,128)(2,1)} %u_ref.3) | copy-start | bytes 786436

commit v3 on v2

--- a/solution.py
+++ b/solution.py
@@ -21,6 +21,7 @@
 LENGTH = 2 * BLOCK * OWNERS
 GROUP = 4
 VMEM_LIMIT = 32 << 20
+PRE_VMEM_LIMIT = 56 << 20
 
 
 def split_parts(values):
@@ -53,15 +54,32 @@
     return (outer_cat, inner_cat, inner_back, back_cat, twiddle)
 
 
-def pre_kernel(part_ref, q_ref, k_ref, v_ref, u_ref, f_ref, out_ref):
-    del part_ref
+def pre_kernel(part_ref, q_hbm, k_hbm, v_hbm, u_hbm, f_hbm, out_ref, data, taps, sems, taps_sem):
+    sources = (k_hbm, v_hbm, u_hbm, q_hbm)
+    copies = []
     for piece in range(PIECES):
         at = pl.ds(piece * LANES, LANES)
-        mixed = k_ref[0, at, :].astype(jnp.float32) * v_ref[0, at, :].astype(jnp.float32)
-        gated = u_ref[0, at, :].astype(jnp.float32) * q_ref[0, at, :].astype(jnp.float32)
-        out_ref[pl.ds(piece, CHANNELS, stride=ROWS_IN), :] = mixed.T
-        out_ref[pl.ds(PIECES + piece, CHANNELS, stride=ROWS_IN), :] = gated.T
-    out_ref[pl.ds(2 * PIECES, CHANNELS, stride=ROWS_IN), :] = f_ref[...].T
+        copies.append(
+            [
+                pltpu.make_async_copy(source.at[0, at, :], data.at[index, at, :], sems.at[index, piece])
+                for index, source in enumerate(sources)
+            ]
+        )
+        for copy in copies[-1]:
+            copy.start()
+    first = pl.multiple_of(part_ref[0] * LANES, LANES)
+    taps_copy = pltpu.make_async_copy(f_hbm.at[pl.ds(first, LANES), :], taps, taps_sem)
+    taps_copy.start()
+    for piece in range(PIECES):
+        for copy in copies[piece]:
+            copy.wait()
+        key, value, grad, query = [
+            data[index, pl.ds(piece * LANES, LANES), :].astype(jnp.float32) for index in range(4)
+        ]
+        out_ref[pl.ds(piece, CHANNELS, stride=ROWS_IN), :] = (key * value).T
+        out_ref[pl.ds(PIECES + piece, CHANNELS, stride=ROWS_IN), :] = (grad * query).T
+    taps_copy.wait()
+    out_ref[pl.ds(2 * PIECES, CHANNELS, stride=ROWS_IN), :] = taps[...].T
 
 
 def halves(value, axis):
@@ -173,34 +191,50 @@
         store(lag, seq * OWNERS * ROWS_OUT + 2 * PIECES)
 
 
-def post_kernel(c_ref, q_ref, k_ref, v_ref, u_ref, o_ref, qg_ref, kg_ref, vg_ref, fg_ref):
+def post_kernel(
+    c_ref, q_ref, k_ref, v_ref, u_ref, o_hbm, qg_hbm, kg_hbm, vg_hbm, fg_hbm, small, large, sems, large_sems
+):
+    copies = []
     for piece in range(PIECES):
         at = pl.ds(piece * LANES, LANES)
         conv = c_ref[pl.ds(piece, CHANNELS, stride=ROWS_OUT), :].T
         back = c_ref[pl.ds(PIECES + piece, CHANNELS, stride=ROWS_OUT), :].T
-        o_ref[0, at, :] = (q_ref[0, at, :].astype(jnp.float32) * conv).astype(jnp.bfloat16)
-        qg_ref[0, at, :] = (u_ref[0, at, :].astype(jnp.float32) * conv).astype(jnp.bfloat16)
-        kg_ref[0, at, :] = (back * v_ref[0, at, :].astype(jnp.float32)).astype(jnp.bfloat16)
-        vg_ref[0, at, :] = (back * k_ref[0, at, :].astype(jnp.float32)).astype(jnp.bfloat16)
-        fg_ref[at, :] = c_ref[pl.ds(2 * PIECES + piece, CHANNELS, stride=ROWS_OUT), :].T
-
-
-def params():
-    return pltpu.CompilerParams(vmem_limit_bytes=VMEM_LIMIT)
+        large[at, :] = c_ref[pl.ds(2 * PIECES + piece, CHANNELS, stride=ROWS_OUT), :].T
+        pieces = (
+            (q_ref, conv, o_hbm),
+            (u_ref, conv, qg_hbm),
+            (v_ref, back, kg_hbm),
+            (k_ref, back, vg_hbm),
+        )
+        for index, (factor, result, target) in enumerate(pieces):
+            small[index, at, :] = (factor[0, at, :].astype(jnp.float32) * result).astype(jnp.bfloat16)
+            copies.append(
+                pltpu.make_async_copy(small.at[index, at, :], target.at[0, at, :], sems.at[index, piece])
+            )
+            copies[-1].start()
+        copies.append(pltpu.make_async_copy(large.at[at, :], fg_hbm.at[at, :], large_sems.at[piece]))
+        copies[-1].start()
+    for copy in copies:
+        copy.wait()
+
+
+def params(limit=VMEM_LIMIT):
+    return pltpu.CompilerParams(vmem_limit_bytes=limit)
 
 
 def pre(part, query_seq, key_seq, value_seq, upstream, filter_param):
-    whole = pl.BlockSpec((1, BLOCK, CHANNELS), lambda i, part: (0, 0, 0))
     return pl.pallas_call(
         pre_kernel,
         out_shape=jax.ShapeDtypeStruct((CHANNELS * ROWS_IN, LANES), jnp.float32),
-        grid_spec=pltpu.PrefetchScalarGridSpec(
-            num_scalar_prefetch=1,
-            grid=(1,),
-            in_specs=[whole] * 4 + [pl.BlockSpec((LANES, CHANNELS), lambda i, part: (part[0], 0))],
-            out_specs=pl.BlockSpec((CHANNELS * ROWS_IN, LANES), lambda i, part: (0, 0)),
-        ),
-        compiler_params=params(),
+        in_specs=[pl.BlockSpec(memory_space=pltpu.SMEM)] + [pl.BlockSpec(memory_space=pltpu.HBM)] * 5,
+        out_specs=pl.BlockSpec(memory_space=pltpu.VMEM),
+        scratch_shapes=[
+            pltpu.VMEM((4, BLOCK, CHANNELS), jnp.bfloat16),
+            pltpu.VMEM((LANES, CHANNELS), jnp.float32),
+            pltpu.SemaphoreType.DMA((4, PIECES)),
+            pltpu.SemaphoreType.DMA,
+        ],
+        compiler_params=params(PRE_VMEM_LIMIT),
     )(part, query_seq, key_seq, value_seq, upstream, filter_param)
 
 
@@ -217,6 +251,14 @@
     return pl.pallas_call(
         post_kernel,
         out_shape=(half, half, half, half, jax.ShapeDtypeStruct((BLOCK, CHANNELS), jnp.float32)),
+        in_specs=[pl.BlockSpec(memory_space=pltpu.VMEM)] * 5,
+        out_specs=[pl.BlockSpec(memory_space=pltpu.HBM)] * 5,
+        scratch_shapes=[
+            pltpu.VMEM((4, BLOCK, CHANNELS), jnp.bfloat16),
+            pltpu.VMEM((BLOCK, CHANNELS), jnp.float32),
+            pltpu.SemaphoreType.DMA((4, PIECES)),
+            pltpu.SemaphoreType.DMA((PIECES,)),
+        ],
         compiler_params=params(),
     )(returned, query_seq, key_seq, value_seq, upstream)
 

time: 110 us -> 108 us (0.982)
  local copies, waits for them, and re-layouts: 4.89 us -> 0.06 us
  Pallas kernels: 6.64 us -> 8.92 us
    unnamed x28 -> x18, local copies, waits for them, and re-layouts: 4.89 us -> 0.06 us
    pallas_call x1, Pallas kernels: 0.36 us -> 2.78 us  [pre(): pl.pallas_call(pre_kernel, out_shape=jax.ShapeDtypeStruct((CHANNELS * ROW...]
where the time goes in v3:
time: 108 us
  blocking collectives  97.9 us (91%)
  Pallas kernels  8.92 us (8%)
    all_to_all x2, blocking collectives, exchange(): lax.all_to_all(shaped, ('dp', 'seq'), split_axis=0, concat_axis=0, tiled=...  97.9 us
    pallas_call x1, Pallas kernels, transform(): pl.pallas_call(fft_kernel, out_shape=jax.ShapeDtypeStruct((SEQS * OWNERS...  4.74 us
    pallas_call x1, Pallas kernels, pre(): pl.pallas_call(pre_kernel, out_shape=jax.ShapeDtypeStruct((CHANNELS * ROW...  2.78 us

profile of v3, /device:TPU:1, one launch (start us, length us, event | category | flops | bytes accessed | tf_op | source)
XLA Modules:
  0.0 107.7 jit_solution(11229006174135736738)
XLA Ops:
  0.6 2.8 %shard_map.137 = f32[2304,128]{1,0:T(8,128)} custom-call(s32[1]{0:T(128)} %bitcast.part_ref, bf16[1,512,256]{2,1,0:T(8,128)(2,1)} %q_ref.1, bf16[1,512,256]{2,1,0:T(8,128)(2,1)} %k_ref.1, bf16[1,512,256]{2,1,0:T(8,128)(2,1)} %v_ref.1, bf16[1,512,256]{2,1,0:T(8,128)(2,1)} %u_ref.1, f32[512,256]{1,0:T(8,128)} %f_hbm.1), custom_call_target="tpu_custom_call" | custom-call | tf_op jit(solution)/shard_map/pallas_call | solution.py:226
  3.4 0.0 copy-start.4
  3.4 0.0 copy-start.5
  3.5 0.0 copy-start.6
  3.5 0.0 copy-start.7
  3.5 0.0 copy-start.8
  3.5 49.4 %all_to_all.10 = f32[256,9,1,128]{3,2,1,0:T(1,128)S(1)} all-to-all(f32[256,9,1,128]{3,2,1,0:T(1,128)} %bitcast.8), channel_id=1, replica_groups=mesh['dp'=8,'seq'=32] {'dp','seq'}, dimensions={0} | all-to-all | bytes 2359296 | tf_op jit(solution)/shard_map/all_to_all | solution.py:268
  52.9 0.0 copy-done.4
  52.9 0.0 copy-done.5
  52.9 0.0 copy-done.6
  52.9 0.0 copy-done.7
  52.9 0.0 copy-done.8
  52.9 4.7 %shard_map.138 = f32[3072,128]{1,0:T(8,128)S(1)} custom-call(f32[2304,128]{1,0:T(8,128)S(1)} %bitcast.7, bf16[256,384]{1,0:T(8,128)(2,1)S(1)} %copy-done.7, bf16[768,256]{1,0:T(8,128)(2,1)S(1)} %copy-done.5, bf16[768,256]{1,0:T(8,128)(2,1)S(1)} %copy-done.4, bf16[128,768]{1,0:T(8,128)(2,1)S(1)} %copy-done.6, f32[2,128,128]{2,1,0:T(8,128)S(1)} %copy-done.8), custom_call_target="tpu_custom_call" | custom-call | tf_op jit(solution)/shard_map/pallas_call | solution.py:242
  57.7 0.0 copy-start
  57.7 0.0 copy-start.1
  57.7 0.0 copy-start.2
  57.7 0.0 copy-start.3
  57.7 48.5 %all_to_all.11 = f32[256,12,1,128]{3,2,1,0:T(1,128)S(1)} all-to-all(f32[256,12,1,128]{3,2,1,0:T(1,128)S(1)} %bitcast.6), channel_id=1, replica_groups=mesh['dp'=8,'seq'=32] {'dp','seq'}, dimensions={0} | all-to-all | bytes 3145728 | tf_op jit(solution)/shard_map/all_to_all | solution.py:268
  106.3 0.0 copy-done
  106.3 0.0 copy-done.1
  106.3 0.0 copy-done.2
  106.3 0.0 copy-done.3
  106.3 1.4 %shard_map.139 = (bf16[1,512,256]{2,1,0:T(8,128)(2,1)}, bf16[1,512,256]{2,1,0:T(8,128)(2,1)}, bf16[1,512,256]{2,1,0:T(8,128)(2,1)}, bf16[1,512,256]{2,1,0:T(8,128)(2,1)}, f32[512,256]{1,0:T(8,128)}) custom-call(f32[3072,128]{1,0:T(8,128)S(1)} %bitcast.5, bf16[1,512,256]{2,1,0:T(8,128)(2,1)S(1)} %copy-done, bf16[1,512,256]{2,1,0:T(8,128)(2,1)S(1)} %copy-done.1, ...), custom_call_target="tpu_custom_call" | custom-call | tf_op jit(solution)/shard_map/pallas_call | solution.py:251
Async XLA Ops:
  3.4 49.5 %copy-start.4 = (bf16[768,256]{1,0:T(8,128)(2,1)S(1)}, bf16[768,256]{1,0:T(8,128)(2,1)}, u32[]{:S(2)}) copy-start(bf16[768,256]{1,0:T(8,128)(2,1)} %constant.23.clone.inner_back_ref) | copy-start | bytes 1179652
  3.4 49.5 %copy-start.5 = (bf16[768,256]{1,0:T(8,128)(2,1)S(1)}, bf16[768,256]{1,0:T(8,128)(2,1)}, u32[]{:S(2)}) copy-start(bf16[768,256]{1,0:T(8,128)(2,1)} %constant.22.clone.inner_ref) | copy-start | bytes 1179652
  3.5 49.5 %copy-start.6 = (bf16[128,768]{1,0:T(8,128)(2,1)S(1)}, bf16[128,768]{1,0:T(8,128)(2,1)}, u32[]{:S(2)}) copy-start(bf16[128,768]{1,0:T(8,128)(2,1)} %constant.24.clone.back_ref) | copy-start | bytes 589828
  3.5 49.4 %copy-start.7 = (bf16[256,384]{1,0:T(8,128)(2,1)S(1)}, bf16[256,384]{1,0:T(8,128)(2,1)}, u32[]{:S(2)}) copy-start(bf16[256,384]{1,0:T(8,128)(2,1)} %constant.21.clone.outer_ref) | copy-start | bytes 589828
  3.5 49.4 %copy-start.8 = (f32[2,128,128]{2,1,0:T(8,128)S(1)}, f32[2,128,128]{2,1,0:T(8,128)}, u32[]{:S(2)}) copy-start(f32[2,128,128]{2,1,0:T(8,128)} %constant.25.clone.twiddle_ref) | copy-start | bytes 393220
  57.7 48.6 %copy-start = (bf16[1,512,256]{2,1,0:T(8,128)(2,1)S(1)}, bf16[1,512,256]{2,1,0:T(8,128)(2,1)}, u32[]{:S(2)}) copy-start(bf16[1,512,256]{2,1,0:T(8,128)(2,1)} %q_ref.1) | copy-start | bytes 786436
  57.7 48.6 %copy-start.1 = (bf16[1,512,256]{2,1,0:T(8,128)(2,1)S(1)}, bf16[1,512,256]{2,1,0:T(8,128)(2,1)}, u32[]{:S(2)}) copy-start(bf16[1,512,256]{2,1,0:T(8,128)(2,1)} %k_ref.1) | copy-start | bytes 786436
  57.7 48.6 %copy-start.2 = (bf16[1,512,256]{2,1,0:T(8,128)(2,1)S(1)}, bf16[1,512,256]{2,1,0:T(8,128)(2,1)}, u32[]{:S(2)}) copy-start(bf16[1,512,256]{2,1,0:T(8,128)(2,1)} %v_ref.1) | copy-start | bytes 786436
  57.7 48.6 %copy-start.3 = (bf16[1,512,256]{2,1,0:T(8,128)(2,1)S(1)}, bf16[1,512,256]{2,1,0:T(8,128)(2,1)}, u32[]{:S(2)}) copy-start(bf16[1,512,256]{2,1,0:T(8,128)(2,1)} %u_ref.1) | copy-start | bytes 786436

commit v4 on v3

--- a/solution.py
+++ b/solution.py
@@ -21,7 +21,6 @@
 LENGTH = 2 * BLOCK * OWNERS
 GROUP = 4
 VMEM_LIMIT = 32 << 20
-PRE_VMEM_LIMIT = 56 << 20
 
 
 def split_parts(values):
@@ -218,11 +217,12 @@
         copy.wait()
 
 
-def params(limit=VMEM_LIMIT):
-    return pltpu.CompilerParams(vmem_limit_bytes=limit)
-
-
-def pre(part, query_seq, key_seq, value_seq, upstream, filter_param):
+def params():
+    return pltpu.CompilerParams(vmem_limit_bytes=VMEM_LIMIT)
+
+
+def pre(part, *arrays):
+    arrays = [pltpu.with_memory_space_constraint(array, pltpu.HBM) for array in arrays]
     return pl.pallas_call(
         pre_kernel,
         out_shape=jax.ShapeDtypeStruct((CHANNELS * ROWS_IN, LANES), jnp.float32),
@@ -234,8 +234,8 @@
             pltpu.SemaphoreType.DMA((4, PIECES)),
             pltpu.SemaphoreType.DMA,
         ],
-        compiler_params=params(PRE_VMEM_LIMIT),
-    )(part, query_seq, key_seq, value_seq, upstream, filter_param)
+        compiler_params=params(),
+    )(part, *arrays)
 
 
 def transform(arrived, tables):

time: 108 us -> 107 us (level)
  no operation moved by 1% of the time
where the time goes in v4:
time: 107 us; the launch traced here: 106 us
  blocking collectives  97.7 us (91%)
  Pallas kernels  7.93 us (7%)
    all_to_all x2, blocking collectives, exchange(): lax.all_to_all(shaped, ('dp', 'seq'), split_axis=0, concat_axis=0, tiled=...  97.7 us
    pallas_call x1, Pallas kernels, transform(): pl.pallas_call(fft_kernel, out_shape=jax.ShapeDtypeStruct((SEQS * OWNERS...  4.77 us

profile of v4, /device:TPU:1, one launch (start us, length us, event | category | flops | bytes accessed | tf_op | source)
XLA Modules:
  0.0 106.5 jit_solution(9404209762430643509)
XLA Ops:
  0.6 1.8 %shard_map.137 = f32[2304,128]{1,0:T(8,128)S(1)} custom-call(s32[1]{0:T(128)} %bitcast.part_ref, bf16[1,512,256]{2,1,0:T(8,128)(2,1)} %q_ref.1, bf16[1,512,256]{2,1,0:T(8,128)(2,1)} %k_ref.1, bf16[1,512,256]{2,1,0:T(8,128)(2,1)} %v_ref.1, bf16[1,512,256]{2,1,0:T(8,128)(2,1)} %u_ref.1, f32[512,256]{1,0:T(8,128)} %f_hbm.1), custom_call_target="tpu_custom_call" | custom-call | tf_op jit(solution)/shard_map/pallas_call | solution.py:226
  2.4 0.0 copy-start.4
  2.4 0.0 copy-start.5
  2.4 0.0 copy-start.6
  2.4 0.0 copy-start.7
  2.4 0.0 copy-start.8
  2.5 49.2 %all_to_all.10 = f32[256,9,1,128]{3,2,1,0:T(1,128)S(1)} all-to-all(f32[256,9,1,128]{3,2,1,0:T(1,128)S(1)} %bitcast.7), channel_id=1, replica_groups=mesh['dp'=8,'seq'=32] {'dp','seq'}, dimensions={0} | all-to-all | bytes 2359296 | tf_op jit(solution)/shard_map/all_to_all | solution.py:268
  51.7 0.0 copy-done.4
  51.7 0.0 copy-done.5
  51.7 0.0 copy-done.6
  51.7 0.0 copy-done.7
  51.7 0.0 copy-done.8
  51.7 4.8 %shard_map.138 = f32[3072,128]{1,0:T(8,128)S(1)} custom-call(f32[2304,128]{1,0:T(8,128)S(1)} %bitcast.8, bf16[256,384]{1,0:T(8,128)(2,1)S(1)} %copy-done.7, bf16[768,256]{1,0:T(8,128)(2,1)S(1)} %copy-done.5, bf16[768,256]{1,0:T(8,128)(2,1)S(1)} %copy-done.4, bf16[128,768]{1,0:T(8,128)(2,1)S(1)} %copy-done.6, f32[2,128,128]{2,1,0:T(8,128)S(1)} %copy-done.8), custom_call_target="tpu_custom_call" | custom-call | tf_op jit(solution)/shard_map/pallas_call | solution.py:242
  56.5 0.0 copy-start
  56.5 0.0 copy-start.1
  56.5 0.0 copy-start.2
  56.5 0.0 copy-start.3
  56.5 48.5 %all_to_all.11 = f32[256,12,1,128]{3,2,1,0:T(1,128)S(1)} all-to-all(f32[256,12,1,128]{3,2,1,0:T(1,128)S(1)} %bitcast.6), channel_id=1, replica_groups=mesh['dp'=8,'seq'=32] {'dp','seq'}, dimensions={0} | all-to-all | bytes 3145728 | tf_op jit(solution)/shard_map/all_to_all | solution.py:268
  105.1 0.0 copy-done
  105.1 0.0 copy-done.1
  105.1 0.0 copy-done.2
  105.1 0.0 copy-done.3
  105.1 1.4 %shard_map.139 = (bf16[1,512,256]{2,1,0:T(8,128)(2,1)}, bf16[1,512,256]{2,1,0:T(8,128)(2,1)}, bf16[1,512,256]{2,1,0:T(8,128)(2,1)}, bf16[1,512,256]{2,1,0:T(8,128)(2,1)}, f32[512,256]{1,0:T(8,128)}) custom-call(f32[3072,128]{1,0:T(8,128)S(1)} %bitcast.5, bf16[1,512,256]{2,1,0:T(8,128)(2,1)S(1)} %copy-done, bf16[1,512,256]{2,1,0:T(8,128)(2,1)S(1)} %copy-done.1, ...), custom_call_target="tpu_custom_call" | custom-call | tf_op jit(solution)/shard_map/pallas_call | solution.py:251
Async XLA Ops:
  2.4 49.3 %copy-start.4 = (bf16[768,256]{1,0:T(8,128)(2,1)S(1)}, bf16[768,256]{1,0:T(8,128)(2,1)}, u32[]{:S(2)}) copy-start(bf16[768,256]{1,0:T(8,128)(2,1)} %constant.23.clone.inner_back_ref) | copy-start | bytes 1179652
  2.4 49.3 %copy-start.5 = (bf16[768,256]{1,0:T(8,128)(2,1)S(1)}, bf16[768,256]{1,0:T(8,128)(2,1)}, u32[]{:S(2)}) copy-start(bf16[768,256]{1,0:T(8,128)(2,1)} %constant.22.clone.inner_ref) | copy-start | bytes 1179652
  2.4 49.2 %copy-start.6 = (bf16[128,768]{1,0:T(8,128)(2,1)S(1)}, bf16[128,768]{1,0:T(8,128)(2,1)}, u32[]{:S(2)}) copy-start(bf16[128,768]{1,0:T(8,128)(2,1)} %constant.24.clone.back_ref) | copy-start | bytes 589828
  2.4 49.2 %copy-start.7 = (bf16[256,384]{1,0:T(8,128)(2,1)S(1)}, bf16[256,384]{1,0:T(8,128)(2,1)}, u32[]{:S(2)}) copy-start(bf16[256,384]{1,0:T(8,128)(2,1)} %constant.21.clone.outer_ref) | copy-start | bytes 589828
  2.4 49.2 %copy-start.8 = (f32[2,128,128]{2,1,0:T(8,128)S(1)}, f32[2,128,128]{2,1,0:T(8,128)}, u32[]{:S(2)}) copy-start(f32[2,128,128]{2,1,0:T(8,128)} %constant.25.clone.twiddle_ref) | copy-start | bytes 393220
  56.5 48.6 %copy-start = (bf16[1,512,256]{2,1,0:T(8,128)(2,1)S(1)}, bf16[1,512,256]{2,1,0:T(8,128)(2,1)}, u32[]{:S(2)}) copy-start(bf16[1,512,256]{2,1,0:T(8,128)(2,1)} %q_ref.1) | copy-start | bytes 786436
  56.5 48.6 %copy-start.1 = (bf16[1,512,256]{2,1,0:T(8,128)(2,1)S(1)}, bf16[1,512,256]{2,1,0:T(8,128)(2,1)}, u32[]{:S(2)}) copy-start(bf16[1,512,256]{2,1,0:T(8,128)(2,1)} %k_ref.1) | copy-start | bytes 786436
  56.5 48.6 %copy-start.2 = (bf16[1,512,256]{2,1,0:T(8,128)(2,1)S(1)}, bf16[1,512,256]{2,1,0:T(8,128)(2,1)}, u32[]{:S(2)}) copy-start(bf16[1,512,256]{2,1,0:T(8,128)(2,1)} %v_ref.1) | copy-start | bytes 786436
  56.5 48.6 %copy-start.3 = (bf16[1,512,256]{2,1,0:T(8,128)(2,1)S(1)}, bf16[1,512,256]{2,1,0:T(8,128)(2,1)}, u32[]{:S(2)}) copy-start(bf16[1,512,256]{2,1,0:T(8,128)(2,1)} %u_ref.1) | copy-start | bytes 786436

commit v5 on v4

--- a/solution.py
+++ b/solution.py
@@ -16,7 +16,8 @@
 OWNERS = 32
 PIECES = BLOCK // LANES
 ROWS_IN = 2 * PIECES + 1
-ROWS_OUT = 3 * PIECES
+ROWS_OUT = 2 * PIECES
+Z_CHIPS = 8
 HALF = 128
 LENGTH = 2 * BLOCK * OWNERS
 GROUP = 4
@@ -91,7 +92,9 @@
     return jnp.dot(left, right, preferred_element_type=jnp.float32)
 
 
-def fft_kernel(in_ref, outer_ref, inner_ref, inner_back_ref, back_ref, twiddle_ref, out_ref):
+def fft_kernel(
+    place_ref, in_ref, outer_ref, inner_ref, inner_back_ref, back_ref, twiddle_ref, out_ref, lag_ref, blocks
+):
     cos_t = twiddle_ref[0]
     sin_t = twiddle_ref[1]
 
@@ -186,19 +189,18 @@
             store(result[:, LANES:], base + PIECES)
         if last:
             lag = outer_back(rows[2 * GROUP * HALF :])
-    for seq in range(SEQS):
-        store(lag, seq * OWNERS * ROWS_OUT + 2 * PIECES)
-
-
-def post_kernel(
-    c_ref, q_ref, k_ref, v_ref, u_ref, o_hbm, qg_hbm, kg_hbm, vg_hbm, fg_hbm, small, large, sems, large_sems
-):
+    for piece in range(PIECES):
+        blocks[:, piece, :] = lag[piece * OWNERS : (piece + 1) * OWNERS, :]
+    for other in range(OWNERS):
+        lag_ref[other] = blocks[lax.bitwise_xor(place_ref[1], other)]
+
+
+def post_kernel(c_ref, q_ref, k_ref, v_ref, u_ref, o_hbm, qg_hbm, kg_hbm, vg_hbm, small, sems):
     copies = []
     for piece in range(PIECES):
         at = pl.ds(piece * LANES, LANES)
         conv = c_ref[pl.ds(piece, CHANNELS, stride=ROWS_OUT), :].T
         back = c_ref[pl.ds(PIECES + piece, CHANNELS, stride=ROWS_OUT), :].T
-        large[at, :] = c_ref[pl.ds(2 * PIECES + piece, CHANNELS, stride=ROWS_OUT), :].T
         pieces = (
             (q_ref, conv, o_hbm),
             (u_ref, conv, qg_hbm),
@@ -211,10 +213,18 @@
                 pltpu.make_async_copy(small.at[index, at, :], target.at[0, at, :], sems.at[index, piece])
             )
             copies[-1].start()
-        copies.append(pltpu.make_async_copy(large.at[at, :], fg_hbm.at[at, :], large_sems.at[piece]))
-        copies[-1].start()
     for copy in copies:
         copy.wait()
+
+
+def taps_kernel(place_ref, *refs):
+    sources, fg_ref, blocks = refs[:SEQS], refs[SEQS], refs[SEQS + 1]
+    for other, source in enumerate(sources):
+        row = lax.bitwise_xor(place_ref[0], other) * OWNERS
+        for index in range(OWNERS):
+            blocks[row + lax.bitwise_xor(place_ref[1], index)] = source[index]
+    for piece in range(PIECES):
+        fg_ref[pl.ds(piece * LANES, LANES), :] = blocks[:, piece, :].T
 
 
 def params():
@@ -238,29 +248,44 @@
     )(part, *arrays)
 
 
-def transform(arrived, tables):
+def transform(place, arrived, tables):
     return pl.pallas_call(
         fft_kernel,
-        out_shape=jax.ShapeDtypeStruct((SEQS * OWNERS * ROWS_OUT, LANES), jnp.float32),
+        out_shape=(
+            jax.ShapeDtypeStruct((SEQS * OWNERS * ROWS_OUT, LANES), jnp.float32),
+            jax.ShapeDtypeStruct((OWNERS, PIECES, LANES), jnp.float32),
+        ),
+        in_specs=[pl.BlockSpec(memory_space=pltpu.SMEM)] + [pl.BlockSpec(memory_space=pltpu.VMEM)] * 6,
+        out_specs=[pl.BlockSpec(memory_space=pltpu.VMEM)] * 2,
+        scratch_shapes=[pltpu.VMEM((OWNERS, PIECES, LANES), jnp.float32)],
         compiler_params=params(),
-    )(arrived, *tables)
+    )(place, arrived, *tables)
 
 
 def post(returned, query_seq, key_seq, value_seq, upstream):
     half = jax.ShapeDtypeStruct((1, BLOCK, CHANNELS), jnp.bfloat16)
     return pl.pallas_call(
         post_kernel,
-        out_shape=(half, half, half, half, jax.ShapeDtypeStruct((BLOCK, CHANNELS), jnp.float32)),
+        out_shape=(half, half, half, half),
         in_specs=[pl.BlockSpec(memory_space=pltpu.VMEM)] * 5,
-        out_specs=[pl.BlockSpec(memory_space=pltpu.HBM)] * 5,
+        out_specs=[pl.BlockSpec(memory_space=pltpu.HBM)] * 4,
         scratch_shapes=[
             pltpu.VMEM((4, BLOCK, CHANNELS), jnp.bfloat16),
-            pltpu.VMEM((BLOCK, CHANNELS), jnp.float32),
             pltpu.SemaphoreType.DMA((4, PIECES)),
-            pltpu.SemaphoreType.DMA((PIECES,)),
         ],
         compiler_params=params(),
     )(returned, query_seq, key_seq, value_seq, upstream)
+
+
+def taps_grad(place, sources):
+    return pl.pallas_call(
+        taps_kernel,
+        out_shape=jax.ShapeDtypeStruct((BLOCK, CHANNELS), jnp.float32),
+        in_specs=[pl.BlockSpec(memory_space=pltpu.SMEM)] + [pl.BlockSpec(memory_space=pltpu.VMEM)] * SEQS,
+        out_specs=pl.BlockSpec(memory_space=pltpu.VMEM),
+        scratch_shapes=[pltpu.VMEM((CHANNELS, PIECES, LANES), jnp.float32)],
+        compiler_params=params(),
+    )(place, *sources)
 
 
 def exchange(rows, depth):
@@ -269,14 +294,30 @@
     return moved.reshape(CHANNELS * depth, LANES)
 
 
+def swap(value, axis, bits):
+    return lax.ppermute(value, axis, [(place, place ^ bits) for place in range(lax.axis_size(axis))])
+
+
+def spread(lag):
+    halves_x = lag.reshape(2, Z_CHIPS, 2, PIECES, LANES)
+    columns = [halves_x[:, 0]] + [swap(halves_x[:, z], "seq", 2 * z) for z in range(1, Z_CHIPS)]
+    by_z = jnp.stack(columns, axis=1)
+    by_x = jnp.stack([by_z[0], swap(by_z[1], "seq", 2 * Z_CHIPS)])
+    mine = jnp.stack([by_x[:, :, 0], swap(by_x[:, :, 1], "seq", 1)], axis=2)
+    mine = mine.reshape(OWNERS, PIECES, LANES)
+    return [mine] + [swap(mine, "dp", other) for other in range(1, SEQS)]
+
+
 def local(query_seq, key_seq, value_seq, upstream, filter_param):
     tables = [jnp.asarray(table) for table in constants()]
+    place = jnp.stack([lax.axis_index("dp"), lax.axis_index("seq")]).astype(jnp.int32)
     part = lax.div(lax.axis_index("dp"), 2).astype(jnp.int32).reshape(1)
     sent = pre(part, query_seq, key_seq, value_seq, upstream, filter_param)
     arrived = exchange(sent, ROWS_IN)
-    results = transform(arrived, tables)
+    results, lag = transform(place, arrived, tables)
     returned = exchange(results, ROWS_OUT)
-    return post(returned, query_seq, key_seq, value_seq, upstream)
+    filter_grad = taps_grad(place, spread(lag))
+    return (*post(returned, query_seq, key_seq, value_seq, upstream), filter_grad)
 
 
 def solution(mesh):

time: 107 us -> 125 us (1.17); the launches traced: 106 us -> 123 us
  blocking collectives: 97.7 us -> 0 us
  starting transfers between devices: 0 us -> 56.4 us
  waiting for transfers between devices: 0 us -> 53.4 us
  Pallas kernels: 7.93 us -> 12.2 us
    all_to_all x2 -> x0, blocking collectives: 97.7 us -> none  [exchange(): lax.all_to_all(shaped, ('dp', 'seq'), split_axis=0, concat_axis=0, tiled=...]
    all_to_all x0 -> x2, waiting for transfers between devices: none -> 33.7 us  [exchange(): lax.all_to_all(shaped, ('dp', 'seq'), split_axis=0, concat_axis=0, tiled=...]
    ppermute x0 -> x16, starting transfers between devices: none -> 33.4 us  [swap(): lax.ppermute(value, axis, [(place, place ^ bits) for place in range(lax.a...]
    all_to_all x0 -> x2, starting transfers between devices: none -> 23 us  [exchange(): lax.all_to_all(shaped, ('dp', 'seq'), split_axis=0, concat_axis=0, tiled=...]
    ppermute x0 -> x16, waiting for transfers between devices: none -> 19.7 us  [swap(): lax.ppermute(value, axis, [(place, place ^ bits) for place in range(lax.a...]
    pallas_call x2 -> x3, Pallas kernels: 6.18 us -> 9.38 us  [the longest x1 6.23 us: transform(): pl.pallas_call(fft_kernel, out_shape=(jax.ShapeDtypeStruct((SEQS * OWNERS...]
  transfers between devices with their start and end apart: 0 -> 18, of which waited for: 0 -> 9; matrix products, arithmetic and copies ran while one was open for 0% -> 0% of each run, Pallas kernels for 0% -> 2%
where the time goes in v5:
time: 125 us; the launch traced here: 123 us
  starting transfers between devices  56.4 us (45%)
  waiting for transfers between devices  53.4 us (43%)
  Pallas kernels  12.2 us (10%)
    all_to_all x2, waiting for transfers between devices, exchange(): lax.all_to_all(shaped, ('dp', 'seq'), split_axis=0, concat_axis=0, tiled=...  33.7 us
    ppermute x16, starting transfers between devices, swap(): lax.ppermute(value, axis, [(place, place ^ bits) for place in range(lax.a...  33.4 us
    all_to_all x2, starting transfers between devices, exchange(): lax.all_to_all(shaped, ('dp', 'seq'), split_axis=0, concat_axis=0, tiled=...  23 us
    ppermute x16, waiting for transfers between devices, swap(): lax.ppermute(value, axis, [(place, place ^ bits) for place in range(lax.a...  19.7 us
    pallas_call x1, Pallas kernels, transform(): pl.pallas_call(fft_kernel, out_shape=(jax.ShapeDtypeStruct((SEQS * OWNERS...  6.23 us
    pallas_call x1, Pallas kernels, pre(): pl.pallas_call(pre_kernel, out_shape=jax.ShapeDtypeStruct((CHANNELS * ROW...  2.78 us
  transfers between devices with their start and end apart: 18, of which 9 were waited for; matrix products, arithmetic and copies ran while one was open for 0% of the time, Pallas kernels for 2%

profile of v5, /device:TPU:1, one launch (start us, length us, event | category | flops | bytes accessed | tf_op | source)
XLA Modules:
  0.0 123.2 jit_solution(17313439917760345141)
XLA Ops:
  0.6 2.8 %shard_map.137 = f32[2304,128]{1,0:T(8,128)} custom-call(s32[1]{0:T(128)} %bitcast.2.part_ref, bf16[1,512,256]{2,1,0:T(8,128)(2,1)} %q_ref.1, bf16[1,512,256]{2,1,0:T(8,128)(2,1)} %k_ref.1, bf16[1,512,256]{2,1,0:T(8,128)(2,1)} %v_ref.1, bf16[1,512,256]{2,1,0:T(8,128)(2,1)} %u_ref.1, f32[512,256]{1,0:T(8,128)} %f_hbm.1), custom_call_target="tpu_custom_call" | custom-call | tf_op jit(solution)/shard_map/pallas_call | solution.py:236
  3.4 0.0 copy-start.4
  3.4 0.0 copy-start.5
  3.4 0.0 copy-start.6
  3.5 0.0 copy-start.7
  3.5 0.0 copy-start.8
  3.5 15.7 %all-to-all-start = ((f32[256,9,1,128]{3,2,1,0:T(1,128)}), f32[256,9,1,128]{3,2,1,0:T(1,128)S(1)}, u32[]{:S(2)}, u32[]{:S(2)}) async-start(f32[256,9,1,128]{3,2,1,0:T(1,128)} %bitcast.3), calls=%async_computation | async-start | bytes 2359296 | tf_op jit(solution)/shard_map/all_to_all | solution.py:293
  19.2 0.1 pad_add_fusion.place_ref
  19.2 33.6 %all-to-all-done = f32[256,9,1,128]{3,2,1,0:T(1,128)S(1)} async-done(((f32[256,9,1,128]{3,2,1,0:T(1,128)}), f32[256,9,1,128]{3,2,1,0:T(1,128)S(1)}, u32[]{:S(2)}, u32[]{:S(2)}) %all-to-all-start) | async-done | bytes 1179680 | tf_op jit(solution)/shard_map/all_to_all | solution.py:293
  52.9 0.0 copy-done.4
  52.9 0.0 copy-done.5
  52.9 0.0 copy-done.6
  52.9 0.0 copy-done.7
  52.9 0.0 copy-done.8
  52.9 6.2 %shard_map.138 = (f32[2048,128]{1,0:T(8,128)}, f32[32,4,128]{2,1,0:T(4,128)S(1)}) custom-call(s32[2]{0:T(128)S(1)} %pad_add_fusion.place_ref, f32[2304,128]{1,0:T(8,128)S(1)} %bitcast.67, bf16[256,384]{1,0:T(8,128)(2,1)S(1)} %copy-done.7, bf16[768,256]{1,0:T(8,128)(2,1)S(1)} %copy-done.5, bf16[768,256]{1,0:T(8,128)(2,1)S(1)} %copy-done.4, ...), custom_call_target="tpu_custom_call" | custom-call | tf_op jit(solution)/shard_map/pallas_call | solution.py:252
  59.2 0.7 collective-permute-start
  59.8 7.4 %all-to-all-start.1 = ((f32[256,8,1,128]{3,1,2,0:T(8,128)}), f32[256,8,1,128]{3,1,2,0:T(8,128)S(1)}, u32[]{:S(2)}, u32[]{:S(2)}) async-start(f32[256,8,1,128]{3,1,2,0:T(8,128)} %bitcast.6), calls=%async_computation.1 | async-start | bytes 2097152 | tf_op jit(solution)/shard_map/all_to_all | solution.py:293
  67.2 0.0 copy-start
  67.2 0.0 copy-start.1
  67.2 0.0 copy-start.2
  67.2 0.0 copy-start.3
  67.2 4.4 %collective-permute-start.6 = (f32[2,2,4,128]{3,2,1,0:T(4,128)S(1)}, f32[2,2,4,128]{3,2,1,0:T(4,128)S(1)}, u32[]{:S(2)}, u32[]{:S(2)}) collective-permute-start(f32[2,2,4,128]{3,2,1,0:T(4,128)S(1)} %get-tuple-element.21), channel_id=1, source_target_pairs={{0,14},{1,15},{2,12},{3,13},{4,10},{5,11},{6,8},{7,9},{8,6},{9,7},... | collective-permute-start | bytes 24584 | tf_op jit(solution)/shard_map/ppermute | solution.py:298
  71.7 1.6 %collective-permute-start.4 = (f32[2,2,4,128]{3,2,1,0:T(4,128)S(1)}, f32[2,2,4,128]{3,2,1,0:T(4,128)S(1)}, u32[]{:S(2)}, u32[]{:S(2)}) collective-permute-start(f32[2,2,4,128]{3,2,1,0:T(4,128)S(1)} %get-tuple-element.22), channel_id=1, source_target_pairs={{0,10},{1,11},{2,8},{3,9},{4,14},{5,15},{6,12},{7,13},{8,2},{9,3},... | collective-permute-start | bytes 24584 | tf_op jit(solution)/shard_map/ppermute | solution.py:298
  73.3 4.4 %collective-permute-start.3 = (f32[2,2,4,128]{3,2,1,0:T(4,128)S(1)}, f32[2,2,4,128]{3,2,1,0:T(4,128)S(1)}, u32[]{:S(2)}, u32[]{:S(2)}) collective-permute-start(f32[2,2,4,128]{3,2,1,0:T(4,128)S(1)} %get-tuple-element.23), channel_id=1, source_target_pairs={{0,8},{1,9},{2,10},{3,11},{4,12},{5,13},{6,14},{7,15},{8,0},{9,1},... | collective-permute-start | bytes 24584 | tf_op jit(solution)/shard_map/ppermute | solution.py:298
  77.7 1.8 %collective-permute-start.2 = (f32[2,2,4,128]{3,2,1,0:T(4,128)S(1)}, f32[2,2,4,128]{3,2,1,0:T(4,128)S(1)}, u32[]{:S(2)}, u32[]{:S(2)}) collective-permute-start(f32[2,2,4,128]{3,2,1,0:T(4,128)S(1)} %get-tuple-element.24), channel_id=1, source_target_pairs={{0,6},{1,7},{2,4},{3,5},{4,2},{5,3},{6,0},{7,1},{8,14},{9,15},{10,... | collective-permute-start | bytes 24584 | tf_op jit(solution)/shard_map/ppermute | solution.py:298
  79.5 0.0 collective-permute-done
  79.5 0.0 collective-permute-start.1
  79.5 11.3 %collective-permute-done.1 = f32[2,2,4,128]{3,2,1,0:T(4,128)S(1)} collective-permute-done((f32[2,2,4,128]{3,2,1,0:T(4,128)S(1)}, f32[2,2,4,128]{3,2,1,0:T(4,128)S(1)}, u32[]{:S(2)}, u32[]{:S(2)}) %collective-permute-start.1) | collective-permute-done | bytes 8224 | tf_op jit(solution)/shard_map/ppermute | solution.py:298
  90.8 5.5 %collective-permute-start.5 = (f32[2,2,4,128]{3,2,1,0:T(4,128)S(1)}, f32[2,2,4,128]{3,2,1,0:T(4,128)S(1)}, u32[]{:S(2)}, u32[]{:S(2)}) collective-permute-start(f32[2,2,4,128]{3,2,1,0:T(4,128)S(1)} %get-tuple-element.27), channel_id=1, source_target_pairs={{0,12},{1,13},{2,14},{3,15},{4,8},{5,9},{6,10},{7,11},{8,4},{9,5},... | collective-permute-start | bytes 24584 | tf_op jit(solution)/shard_map/ppermute | solution.py:298
  96.3 0.0 collective-permute-done.2
  96.3 0.0 collective-permute-done.3
  96.3 0.0 collective-permute-done.4
  96.4 1.3 %collective-permute-done.5 = f32[2,2,4,128]{3,2,1,0:T(4,128)S(1)} collective-permute-done((f32[2,2,4,128]{3,2,1,0:T(4,128)S(1)}, f32[2,2,4,128]{3,2,1,0:T(4,128)S(1)}, u32[]{:S(2)}, u32[]{:S(2)}) %collective-permute-start.5) | collective-permute-done | bytes 8224 | tf_op jit(solution)/shard_map/ppermute | solution.py:298
  97.6 0.0 collective-permute-done.6
  97.7 0.8 collective-permute-start.7
  98.5 2.0 %collective-permute-done.7 = f32[8,2,4,128]{3,2,0,1:T(4,128)S(1)} collective-permute-done((f32[8,2,4,128]{3,2,0,1:T(4,128)S(1)}, f32[8,2,4,128]{3,2,0,1:T(4,128)S(1)}, u32[]{:S(2)}, u32[]{:S(2)}) %collective-permute-start.7) | collective-permute-done | bytes 32800 | tf_op jit(solution)/shard_map/ppermute | solution.py:298
  100.5 2.7 %collective-permute-start.8 = (f32[2,8,4,128]{3,2,1,0:T(4,128)S(1)}, f32[2,8,4,128]{3,2,1,0:T(4,128)S(1)}, u32[]{:S(2)}, u32[]{:S(2)}) collective-permute-start(f32[2,8,4,128]{3,2,1,0:T(4,128)S(1)} %get-tuple-element.18), channel_id=1, source_target_pairs={{0,1},{1,0},{2,3},{3,2},{4,5},{5,4},{6,7},{7,6},{8,9},{9,8},{10,11... | collective-permute-start | bytes 98312 | tf_op jit(solution)/shard_map/ppermute | solution.py:298
  103.2 0.9 collective-permute-done.8
  104.1 5.1 %collective-permute-start.15 = (f32[32,4,128]{2,1,0:T(4,128)S(1)}, f32[32,4,128]{2,1,0:T(4,128)S(1)}, u32[]{:S(2)}, u32[]{:S(2)}) collective-permute-start(f32[32,4,128]{2,1,0:T(4,128)S(1)} %bitcast.69), channel_id=1, source_target_pairs={{0,224},{32,192},{64,160},{96,128},{128,96},{160,64},{192,32},{224... | collective-permute-start | bytes 196616 | tf_op jit(solution)/shard_map/ppermute | solution.py:298
  109.3 0.4 collective-permute-start.14
  109.7 2.6 %collective-permute-start.13 = (f32[32,4,128]{2,1,0:T(4,128)S(1)}, f32[32,4,128]{2,1,0:T(4,128)S(1)}, u32[]{:S(2)}, u32[]{:S(2)}) collective-permute-start(f32[32,4,128]{2,1,0:T(4,128)S(1)} %bitcast.71), channel_id=1, source_target_pairs={{0,160},{32,128},{64,224},{96,192},{128,32},{160,0},{192,96},{224,... | collective-permute-start | bytes 196616 | tf_op jit(solution)/shard_map/ppermute | solution.py:298
  112.3 0.3 collective-permute-start.12
  112.6 2.5 %collective-permute-start.11 = (f32[32,4,128]{2,1,0:T(4,128)S(1)}, f32[32,4,128]{2,1,0:T(4,128)S(1)}, u32[]{:S(2)}, u32[]{:S(2)}) collective-permute-start(f32[32,4,128]{2,1,0:T(4,128)S(1)} %bitcast.73), channel_id=1, source_target_pairs={{0,96},{32,64},{64,32},{96,0},{128,224},{160,192},{192,160},{224,1... | collective-permute-start | bytes 196616 | tf_op jit(solution)/shard_map/ppermute | solution.py:298
  115.2 0.0 collective-permute-done.15.refs_7_
  115.2 0.4 collective-permute-start.10
  115.6 0.7 collective-permute-done.14.refs_6_
  116.3 0.0 collective-permute-start.9
  116.3 0.0 collective-permute-done.13.refs_5_
  116.3 0.9 collective-permute-done.12.refs_4_
  117.2 0.4 collective-permute-done.11.refs_3_
  117.6 2.2 %collective-permute-done.10.refs_2_ = f32[32,4,128]{2,1,0:T(4,128)S(1)} collective-permute-done((f32[32,4,128]{2,1,0:T(4,128)S(1)}, f32[32,4,128]{2,1,0:T(4,128)S(1)}, u32[]{:S(2)}, u32[]{:S(2)}) %collective-permute-start.10) | collective-permute-done | bytes 65568 | tf_op jit(solution)/shard_map/ppermute | solution.py:298
  119.8 0.0 collective-permute-done.9.refs_1_
  119.8 1.9 %shard_map.140 = f32[512,256]{1,0:T(8,128)} custom-call(s32[2]{0:T(128)S(1)} %pad_add_fusion.place_ref, f32[32,4,128]{2,1,0:T(4,128)S(1)} %bitcast.76, f32[32,4,128]{2,1,0:T(4,128)S(1)} %collective-permute-done.9.refs_1_, f32[32,4,128]{2,1,0:T(4,128)S(1)} %collective-permute-done.10.refs_2_, f32[32,4,128]{2,1,0:T(4,128)S(1)} %collective-permute-done.11.refs_3_, ...), custom_call_target="tpu_custom_call" | custom-call | tf_op jit(solution)/shard_map/pallas_call | solution.py:281
  121.8 0.0 all-to-all-done.1
  121.8 0.0 copy-done
  121.8 0.0 copy-done.1
  121.8 0.0 copy-done.2
  121.8 0.0 copy-done.3
  121.8 1.2 shard_map.139
  (12 shorter events, 0.1 us)
Async XLA Ops:
  3.4 49.5 %copy-start.4 = (bf16[768,256]{1,0:T(8,128)(2,1)S(1)}, bf16[768,256]{1,0:T(8,128)(2,1)}, u32[]{:S(2)}) copy-start(bf16[768,256]{1,0:T(8,128)(2,1)} %constant.26.clone.inner_back_ref) | copy-start | bytes 1179652
  3.4 49.5 %copy-start.5 = (bf16[768,256]{1,0:T(8,128)(2,1)S(1)}, bf16[768,256]{1,0:T(8,128)(2,1)}, u32[]{:S(2)}) copy-start(bf16[768,256]{1,0:T(8,128)(2,1)} %constant.25.clone.inner_ref) | copy-start | bytes 1179652
  3.4 49.4 %copy-start.6 = (bf16[128,768]{1,0:T(8,128)(2,1)S(1)}, bf16[128,768]{1,0:T(8,128)(2,1)}, u32[]{:S(2)}) copy-start(bf16[128,768]{1,0:T(8,128)(2,1)} %constant.27.clone.back_ref) | copy-start | bytes 589828
  3.5 49.4 %copy-start.7 = (bf16[256,384]{1,0:T(8,128)(2,1)S(1)}, bf16[256,384]{1,0:T(8,128)(2,1)}, u32[]{:S(2)}) copy-start(bf16[256,384]{1,0:T(8,128)(2,1)} %constant.24.clone.outer_ref) | copy-start | bytes 589828
  3.5 49.4 %copy-start.8 = (f32[2,128,128]{2,1,0:T(8,128)S(1)}, f32[2,128,128]{2,1,0:T(8,128)}, u32[]{:S(2)}) copy-start(f32[2,128,128]{2,1,0:T(8,128)} %constant.28.clone.twiddle_ref) | copy-start | bytes 393220
  3.5 49.4 %all-to-all-start = ((f32[256,9,1,128]{3,2,1,0:T(1,128)}), f32[256,9,1,128]{3,2,1,0:T(1,128)S(1)}, u32[]{:S(2)}, u32[]{:S(2)}) async-start(f32[256,9,1,128]{3,2,1,0:T(1,128)} %bitcast.3), calls=%async_computation | async-start | bytes 2359296 | tf_op jit(solution)/shard_map/all_to_all | solution.py:293
  59.2 20.3 %collective-permute-start = (f32[2,2,4,128]{3,2,1,0:T(4,128)S(1)}, f32[2,2,4,128]{3,2,1,0:T(4,128)S(1)}, u32[]{:S(2)}, u32[]{:S(2)}) collective-permute-start(f32[2,2,4,128]{3,2,1,0:T(4,128)S(1)} %get-tuple-element.26), channel_id=1, source_target_pairs={{0,2},{1,3},{2,0},{3,1},{4,6},{5,7},{6,4},{7,5},{8,10},{9,11},{10,... | collective-permute-start | bytes 24584 | tf_op jit(solution)/shard_map/ppermute | solution.py:298
  59.8 61.9 %all-to-all-start.1 = ((f32[256,8,1,128]{3,1,2,0:T(8,128)}), f32[256,8,1,128]{3,1,2,0:T(8,128)S(1)}, u32[]{:S(2)}, u32[]{:S(2)}) async-start(f32[256,8,1,128]{3,1,2,0:T(8,128)} %bitcast.6), calls=%async_computation.1 | async-start | bytes 2097152 | tf_op jit(solution)/shard_map/all_to_all | solution.py:293
  67.2 54.6 %copy-start = (bf16[1,512,256]{2,1,0:T(8,128)(2,1)S(1)}, bf16[1,512,256]{2,1,0:T(8,128)(2,1)}, u32[]{:S(2)}) copy-start(bf16[1,512,256]{2,1,0:T(8,128)(2,1)} %q_ref.1) | copy-start | bytes 786436
  67.2 54.6 %copy-start.1 = (bf16[1,512,256]{2,1,0:T(8,128)(2,1)S(1)}, bf16[1,512,256]{2,1,0:T(8,128)(2,1)}, u32[]{:S(2)}) copy-start(bf16[1,512,256]{2,1,0:T(8,128)(2,1)} %k_ref.1) | copy-start | bytes 786436
  67.2 54.6 %copy-start.2 = (bf16[1,512,256]{2,1,0:T(8,128)(2,1)S(1)}, bf16[1,512,256]{2,1,0:T(8,128)(2,1)}, u32[]{:S(2)}) copy-start(bf16[1,512,256]{2,1,0:T(8,128)(2,1)} %v_ref.1) | copy-start | bytes 786436
  67.2 54.5 %copy-start.3 = (bf16[1,512,256]{2,1,0:T(8,128)(2,1)S(1)}, bf16[1,512,256]{2,1,0:T(8,128)(2,1)}, u32[]{:S(2)}) copy-start(bf16[1,512,256]{2,1,0:T(8,128)(2,1)} %u_ref.1) | copy-start | bytes 786436
  67.2 30.4 %collective-permute-start.6 = (f32[2,2,4,128]{3,2,1,0:T(4,128)S(1)}, f32[2,2,4,128]{3,2,1,0:T(4,128)S(1)}, u32[]{:S(2)}, u32[]{:S(2)}) collective-permute-start(f32[2,2,4,128]{3,2,1,0:T(4,128)S(1)} %get-tuple-element.21), channel_id=1, source_target_pairs={{0,14},{1,15},{2,12},{3,13},{4,10},{5,11},{6,8},{7,9},{8,6},{9,7},... | collective-permute-start | bytes 24584 | tf_op jit(solution)/shard_map/ppermute | solution.py:298
  71.7 24.7 %collective-permute-start.4 = (f32[2,2,4,128]{3,2,1,0:T(4,128)S(1)}, f32[2,2,4,128]{3,2,1,0:T(4,128)S(1)}, u32[]{:S(2)}, u32[]{:S(2)}) collective-permute-start(f32[2,2,4,128]{3,2,1,0:T(4,128)S(1)} %get-tuple-element.22), channel_id=1, source_target_pairs={{0,10},{1,11},{2,8},{3,9},{4,14},{5,15},{6,12},{7,13},{8,2},{9,3},... | collective-permute-start | bytes 24584 | tf_op jit(solution)/shard_map/ppermute | solution.py:298
  73.3 23.0 %collective-permute-start.3 = (f32[2,2,4,128]{3,2,1,0:T(4,128)S(1)}, f32[2,2,4,128]{3,2,1,0:T(4,128)S(1)}, u32[]{:S(2)}, u32[]{:S(2)}) collective-permute-start(f32[2,2,4,128]{3,2,1,0:T(4,128)S(1)} %get-tuple-element.23), channel_id=1, source_target_pairs={{0,8},{1,9},{2,10},{3,11},{4,12},{5,13},{6,14},{7,15},{8,0},{9,1},... | collective-permute-start | bytes 24584 | tf_op jit(solution)/shard_map/ppermute | solution.py:298
  77.7 18.6 %collective-permute-start.2 = (f32[2,2,4,128]{3,2,1,0:T(4,128)S(1)}, f32[2,2,4,128]{3,2,1,0:T(4,128)S(1)}, u32[]{:S(2)}, u32[]{:S(2)}) collective-permute-start(f32[2,2,4,128]{3,2,1,0:T(4,128)S(1)} %get-tuple-element.24), channel_id=1, source_target_pairs={{0,6},{1,7},{2,4},{3,5},{4,2},{5,3},{6,0},{7,1},{8,14},{9,15},{10,... | collective-permute-start | bytes 24584 | tf_op jit(solution)/shard_map/ppermute | solution.py:298
  79.5 11.3 %collective-permute-start.1 = (f32[2,2,4,128]{3,2,1,0:T(4,128)S(1)}, f32[2,2,4,128]{3,2,1,0:T(4,128)S(1)}, u32[]{:S(2)}, u32[]{:S(2)}) collective-permute-start(f32[2,2,4,128]{3,2,1,0:T(4,128)S(1)} %get-tuple-element.25), channel_id=1, source_target_pairs={{0,4},{1,5},{2,6},{3,7},{4,0},{5,1},{6,2},{7,3},{8,12},{9,13},{10,... | collective-permute-start | bytes 24584 | tf_op jit(solution)/shard_map/ppermute | solution.py:298
  90.8 6.8 %collective-permute-start.5 = (f32[2,2,4,128]{3,2,1,0:T(4,128)S(1)}, f32[2,2,4,128]{3,2,1,0:T(4,128)S(1)}, u32[]{:S(2)}, u32[]{:S(2)}) collective-permute-start(f32[2,2,4,128]{3,2,1,0:T(4,128)S(1)} %get-tuple-element.27), channel_id=1, source_target_pairs={{0,12},{1,13},{2,14},{3,15},{4,8},{5,9},{6,10},{7,11},{8,4},{9,5},... | collective-permute-start | bytes 24584 | tf_op jit(solution)/shard_map/ppermute | solution.py:298
  97.7 2.9 %collective-permute-start.7 = (f32[8,2,4,128]{3,2,0,1:T(4,128)S(1)}, f32[8,2,4,128]{3,2,0,1:T(4,128)S(1)}, u32[]{:S(2)}, u32[]{:S(2)}) collective-permute-start(f32[8,2,4,128]{3,2,0,1:T(4,128)S(1)} %get-tuple-element.20), channel_id=1, source_target_pairs={{0,16},{1,17},{2,18},{3,19},{4,20},{5,21},{6,22},{7,23},{8,24},{9,... | collective-permute-start | bytes 98312 | tf_op jit(solution)/shard_map/ppermute | solution.py:298
  100.5 3.6 %collective-permute-start.8 = (f32[2,8,4,128]{3,2,1,0:T(4,128)S(1)}, f32[2,8,4,128]{3,2,1,0:T(4,128)S(1)}, u32[]{:S(2)}, u32[]{:S(2)}) collective-permute-start(f32[2,8,4,128]{3,2,1,0:T(4,128)S(1)} %get-tuple-element.18), channel_id=1, source_target_pairs={{0,1},{1,0},{2,3},{3,2},{4,5},{5,4},{6,7},{7,6},{8,9},{9,8},{10,11... | collective-permute-start | bytes 98312 | tf_op jit(solution)/shard_map/ppermute | solution.py:298
  104.1 11.0 %collective-permute-start.15 = (f32[32,4,128]{2,1,0:T(4,128)S(1)}, f32[32,4,128]{2,1,0:T(4,128)S(1)}, u32[]{:S(2)}, u32[]{:S(2)}) collective-permute-start(f32[32,4,128]{2,1,0:T(4,128)S(1)} %bitcast.69), channel_id=1, source_target_pairs={{0,224},{32,192},{64,160},{96,128},{128,96},{160,64},{192,32},{224... | collective-permute-start | bytes 196616 | tf_op jit(solution)/shard_map/ppermute | solution.py:298
  109.3 7.0 %collective-permute-start.14 = (f32[32,4,128]{2,1,0:T(4,128)S(1)}, f32[32,4,128]{2,1,0:T(4,128)S(1)}, u32[]{:S(2)}, u32[]{:S(2)}) collective-permute-start(f32[32,4,128]{2,1,0:T(4,128)S(1)} %bitcast.70), channel_id=1, source_target_pairs={{0,192},{32,224},{64,128},{96,160},{128,64},{160,96},{192,0},{224,... | collective-permute-start | bytes 196616 | tf_op jit(solution)/shard_map/ppermute | solution.py:298
  109.7 6.6 %collective-permute-start.13 = (f32[32,4,128]{2,1,0:T(4,128)S(1)}, f32[32,4,128]{2,1,0:T(4,128)S(1)}, u32[]{:S(2)}, u32[]{:S(2)}) collective-permute-start(f32[32,4,128]{2,1,0:T(4,128)S(1)} %bitcast.71), channel_id=1, source_target_pairs={{0,160},{32,128},{64,224},{96,192},{128,32},{160,0},{192,96},{224,... | collective-permute-start | bytes 196616 | tf_op jit(solution)/shard_map/ppermute | solution.py:298
  112.3 4.9 %collective-permute-start.12 = (f32[32,4,128]{2,1,0:T(4,128)S(1)}, f32[32,4,128]{2,1,0:T(4,128)S(1)}, u32[]{:S(2)}, u32[]{:S(2)}) collective-permute-start(f32[32,4,128]{2,1,0:T(4,128)S(1)} %bitcast.72), channel_id=1, source_target_pairs={{0,128},{32,160},{64,192},{96,224},{128,0},{160,32},{192,64},{224,... | collective-permute-start | bytes 196616 | tf_op jit(solution)/shard_map/ppermute | solution.py:298
  112.6 5.0 %collective-permute-start.11 = (f32[32,4,128]{2,1,0:T(4,128)S(1)}, f32[32,4,128]{2,1,0:T(4,128)S(1)}, u32[]{:S(2)}, u32[]{:S(2)}) collective-permute-start(f32[32,4,128]{2,1,0:T(4,128)S(1)} %bitcast.73), channel_id=1, source_target_pairs={{0,96},{32,64},{64,32},{96,0},{128,224},{160,192},{192,160},{224,1... | collective-permute-start | bytes 196616 | tf_op jit(solution)/shard_map/ppermute | solution.py:298
  115.2 4.6 %collective-permute-start.10 = (f32[32,4,128]{2,1,0:T(4,128)S(1)}, f32[32,4,128]{2,1,0:T(4,128)S(1)}, u32[]{:S(2)}, u32[]{:S(2)}) collective-permute-start(f32[32,4,128]{2,1,0:T(4,128)S(1)} %bitcast.74), channel_id=1, source_target_pairs={{0,64},{32,96},{64,0},{96,32},{128,192},{160,224},{192,128},{224,1... | collective-permute-start | bytes 196616 | tf_op jit(solution)/shard_map/ppermute | solution.py:298
  116.3 3.5 %collective-permute-start.9 = (f32[32,4,128]{2,1,0:T(4,128)S(1)}, f32[32,4,128]{2,1,0:T(4,128)S(1)}, u32[]{:S(2)}, u32[]{:S(2)}) collective-permute-start(f32[32,4,128]{2,1,0:T(4,128)S(1)} %bitcast.75), channel_id=1, source_target_pairs={{0,32},{32,0},{64,96},{96,64},{128,160},{160,128},{192,224},{224,1... | collective-permute-start | bytes 196616 | tf_op jit(solution)/shard_map/ppermute | solution.py:298

commit v6 on v4

--- a/solution.py
+++ b/solution.py
@@ -19,7 +19,7 @@
 ROWS_OUT = 3 * PIECES
 HALF = 128
 LENGTH = 2 * BLOCK * OWNERS
-GROUP = 4
+GROUP = 2
 VMEM_LIMIT = 32 << 20
 
 
@@ -139,16 +139,20 @@
     )
     lag_real = jnp.zeros((HALF, LANES), jnp.float32)
     lag_imag = jnp.zeros((HALF, LANES), jnp.float32)
-    for start in range(0, SEQS, GROUP):
+    starts = range(0, SEQS, GROUP)
+    groups = []
+    for start in starts:
         turned = []
         for seq in range(start, start + GROUP):
             base = seq * OWNERS * ROWS_IN
             turned += outer([load(base), load(base + PIECES)])
-        if start == 0:
-            turned += outer([taps])
-        spec = inner(turned, inner_ref)
-        if start == 0:
-            taps_real, taps_imag = spec[2 * GROUP * HALF :, :LANES], spec[2 * GROUP * HALF :, LANES:]
+        groups.append(turned)
+    groups[0] += outer([taps])
+    spectra = [inner(turned, inner_ref) for turned in groups]
+    taps_spec = spectra[0][2 * GROUP * HALF :]
+    taps_real, taps_imag = taps_spec[:, :LANES], taps_spec[:, LANES:]
+    groups = []
+    for spec in spectra:
         products = []
         for index in range(GROUP):
             at = slice(2 * index * HALF, (2 * index + 1) * HALF)
@@ -175,17 +179,16 @@
             )
             lag_real = lag_real + (mixed_real * gated_real + mixed_imag * gated_imag)
             lag_imag = lag_imag + (mixed_real * gated_imag - mixed_imag * gated_real)
-        last = start + GROUP == SEQS
-        if last:
-            products.append(jnp.concatenate([lag_real, lag_imag], axis=1))
-        rows = inner(products, inner_back_ref)
+        groups.append(products)
+    groups[-1].append(jnp.concatenate([lag_real, lag_imag], axis=1))
+    row_groups = [inner(products, inner_back_ref) for products in groups]
+    for start, rows in zip(starts, row_groups):
         for index in range(GROUP):
             result = outer_back(rows[2 * index * HALF : 2 * (index + 1) * HALF])
             base = (start + index) * OWNERS * ROWS_OUT
             store(result[:, :LANES], base)
             store(result[:, LANES:], base + PIECES)
-        if last:
-            lag = outer_back(rows[2 * GROUP * HALF :])
+    lag = outer_back(row_groups[-1][2 * GROUP * HALF :])
     for seq in range(SEQS):
         store(lag, seq * OWNERS * ROWS_OUT + 2 * PIECES)
 

time: 107 us -> 105 us (0.981)
  Pallas kernels: 7.93 us -> 6.54 us
    pallas_call x1, Pallas kernels: 4.77 us -> 3.39 us  [transform(): pl.pallas_call(fft_kernel, out_shape=jax.ShapeDtypeStruct((SEQS * OWNERS...]
where the time goes in v6:
time: 105 us
  blocking collectives  97.7 us (93%)
  Pallas kernels  6.54 us (6%)
    all_to_all x2, blocking collectives, exchange(): lax.all_to_all(shaped, ('dp', 'seq'), split_axis=0, concat_axis=0, tiled=...  97.7 us
    pallas_call x1, Pallas kernels, transform(): pl.pallas_call(fft_kernel, out_shape=jax.ShapeDtypeStruct((SEQS * OWNERS...  3.39 us

profile of v6, /device:TPU:1, one launch (start us, length us, event | category | flops | bytes accessed | tf_op | source)
XLA Modules:
  0.0 105.1 jit_solution(15882671168388734395)
XLA Ops:
  0.6 1.8 %shard_map.137 = f32[2304,128]{1,0:T(8,128)S(1)} custom-call(s32[1]{0:T(128)} %bitcast.part_ref, bf16[1,512,256]{2,1,0:T(8,128)(2,1)} %q_ref.1, bf16[1,512,256]{2,1,0:T(8,128)(2,1)} %k_ref.1, bf16[1,512,256]{2,1,0:T(8,128)(2,1)} %v_ref.1, bf16[1,512,256]{2,1,0:T(8,128)(2,1)} %u_ref.1, f32[512,256]{1,0:T(8,128)} %f_hbm.1), custom_call_target="tpu_custom_call" | custom-call | tf_op jit(solution)/shard_map/pallas_call | solution.py:229
  2.4 0.0 copy-start.4
  2.4 0.0 copy-start.5
  2.4 0.0 copy-start.6
  2.4 0.0 copy-start.7
  2.4 0.0 copy-start.8
  2.5 49.2 %all_to_all.10 = f32[256,9,1,128]{3,2,1,0:T(1,128)S(1)} all-to-all(f32[256,9,1,128]{3,2,1,0:T(1,128)S(1)} %bitcast.7), channel_id=1, replica_groups=mesh['dp'=8,'seq'=32] {'dp','seq'}, dimensions={0} | all-to-all | bytes 2359296 | tf_op jit(solution)/shard_map/all_to_all | solution.py:271
  51.7 0.0 copy-done.4
  51.7 0.0 copy-done.5
  51.7 0.0 copy-done.6
  51.7 0.0 copy-done.7
  51.7 0.0 copy-done.8
  51.7 3.4 %shard_map.138 = f32[3072,128]{1,0:T(8,128)S(1)} custom-call(f32[2304,128]{1,0:T(8,128)S(1)} %bitcast.8, bf16[256,384]{1,0:T(8,128)(2,1)S(1)} %copy-done.7, bf16[768,256]{1,0:T(8,128)(2,1)S(1)} %copy-done.5, bf16[768,256]{1,0:T(8,128)(2,1)S(1)} %copy-done.4, bf16[128,768]{1,0:T(8,128)(2,1)S(1)} %copy-done.6, f32[2,128,128]{2,1,0:T(8,128)S(1)} %copy-done.8), custom_call_target="tpu_custom_call" | custom-call | tf_op jit(solution)/shard_map/pallas_call | solution.py:245
  55.1 0.0 copy-start
  55.1 0.0 copy-start.1
  55.1 0.0 copy-start.2
  55.1 0.0 copy-start.3
  55.1 48.5 %all_to_all.11 = f32[256,12,1,128]{3,2,1,0:T(1,128)S(1)} all-to-all(f32[256,12,1,128]{3,2,1,0:T(1,128)S(1)} %bitcast.6), channel_id=1, replica_groups=mesh['dp'=8,'seq'=32] {'dp','seq'}, dimensions={0} | all-to-all | bytes 3145728 | tf_op jit(solution)/shard_map/all_to_all | solution.py:271
  103.7 0.0 copy-done
  103.7 0.0 copy-done.1
  103.7 0.0 copy-done.2
  103.7 0.0 copy-done.3
  103.7 1.4 %shard_map.139 = (bf16[1,512,256]{2,1,0:T(8,128)(2,1)}, bf16[1,512,256]{2,1,0:T(8,128)(2,1)}, bf16[1,512,256]{2,1,0:T(8,128)(2,1)}, bf16[1,512,256]{2,1,0:T(8,128)(2,1)}, f32[512,256]{1,0:T(8,128)}) custom-call(f32[3072,128]{1,0:T(8,128)S(1)} %bitcast.5, bf16[1,512,256]{2,1,0:T(8,128)(2,1)S(1)} %copy-done, bf16[1,512,256]{2,1,0:T(8,128)(2,1)S(1)} %copy-done.1, ...), custom_call_target="tpu_custom_call" | custom-call | tf_op jit(solution)/shard_map/pallas_call | solution.py:254
Async XLA Ops:
  2.4 49.3 %copy-start.4 = (bf16[768,256]{1,0:T(8,128)(2,1)S(1)}, bf16[768,256]{1,0:T(8,128)(2,1)}, u32[]{:S(2)}) copy-start(bf16[768,256]{1,0:T(8,128)(2,1)} %constant.23.clone.inner_back_ref) | copy-start | bytes 1179652
  2.4 49.3 %copy-start.5 = (bf16[768,256]{1,0:T(8,128)(2,1)S(1)}, bf16[768,256]{1,0:T(8,128)(2,1)}, u32[]{:S(2)}) copy-start(bf16[768,256]{1,0:T(8,128)(2,1)} %constant.22.clone.inner_ref) | copy-start | bytes 1179652
  2.4 49.2 %copy-start.6 = (bf16[128,768]{1,0:T(8,128)(2,1)S(1)}, bf16[128,768]{1,0:T(8,128)(2,1)}, u32[]{:S(2)}) copy-start(bf16[128,768]{1,0:T(8,128)(2,1)} %constant.24.clone.back_ref) | copy-start | bytes 589828
  2.4 49.2 %copy-start.7 = (bf16[256,384]{1,0:T(8,128)(2,1)S(1)}, bf16[256,384]{1,0:T(8,128)(2,1)}, u32[]{:S(2)}) copy-start(bf16[256,384]{1,0:T(8,128)(2,1)} %constant.21.clone.outer_ref) | copy-start | bytes 589828
  2.4 49.2 %copy-start.8 = (f32[2,128,128]{2,1,0:T(8,128)S(1)}, f32[2,128,128]{2,1,0:T(8,128)}, u32[]{:S(2)}) copy-start(f32[2,128,128]{2,1,0:T(8,128)} %constant.25.clone.twiddle_ref) | copy-start | bytes 393220
  55.1 48.6 %copy-start = (bf16[1,512,256]{2,1,0:T(8,128)(2,1)S(1)}, bf16[1,512,256]{2,1,0:T(8,128)(2,1)}, u32[]{:S(2)}) copy-start(bf16[1,512,256]{2,1,0:T(8,128)(2,1)} %q_ref.1) | copy-start | bytes 786436
  55.1 48.6 %copy-start.1 = (bf16[1,512,256]{2,1,0:T(8,128)(2,1)S(1)}, bf16[1,512,256]{2,1,0:T(8,128)(2,1)}, u32[]{:S(2)}) copy-start(bf16[1,512,256]{2,1,0:T(8,128)(2,1)} %k_ref.1) | copy-start | bytes 786436
  55.1 48.6 %copy-start.2 = (bf16[1,512,256]{2,1,0:T(8,128)(2,1)S(1)}, bf16[1,512,256]{2,1,0:T(8,128)(2,1)}, u32[]{:S(2)}) copy-start(bf16[1,512,256]{2,1,0:T(8,128)(2,1)} %v_ref.1) | copy-start | bytes 786436
  55.1 48.6 %copy-start.3 = (bf16[1,512,256]{2,1,0:T(8,128)(2,1)S(1)}, bf16[1,512,256]{2,1,0:T(8,128)(2,1)}, u32[]{:S(2)}) copy-start(bf16[1,512,256]{2,1,0:T(8,128)(2,1)} %u_ref.1) | copy-start | bytes 786436

commit v7 on v6

--- a/solution.py
+++ b/solution.py
@@ -16,7 +16,7 @@
 OWNERS = 32
 PIECES = BLOCK // LANES
 ROWS_IN = 2 * PIECES + 1
-ROWS_OUT = 3 * PIECES
+ROWS_OUT = 2 * PIECES + 1
 HALF = 128
 LENGTH = 2 * BLOCK * OWNERS
 GROUP = 2
@@ -190,18 +190,17 @@
             store(result[:, LANES:], base + PIECES)
     lag = outer_back(row_groups[-1][2 * GROUP * HALF :])
     for seq in range(SEQS):
-        store(lag, seq * OWNERS * ROWS_OUT + 2 * PIECES)
-
-
-def post_kernel(
-    c_ref, q_ref, k_ref, v_ref, u_ref, o_hbm, qg_hbm, kg_hbm, vg_hbm, fg_hbm, small, large, sems, large_sems
-):
+        piece = seq % PIECES
+        base = seq * OWNERS * ROWS_OUT + 2 * PIECES
+        out_ref[pl.ds(base, OWNERS, stride=ROWS_OUT), :] = lag[piece * OWNERS : (piece + 1) * OWNERS, :]
+
+
+def post_kernel(c_ref, q_ref, k_ref, v_ref, u_ref, o_hbm, qg_hbm, kg_hbm, vg_hbm, small, sems):
     copies = []
     for piece in range(PIECES):
         at = pl.ds(piece * LANES, LANES)
         conv = c_ref[pl.ds(piece, CHANNELS, stride=ROWS_OUT), :].T
         back = c_ref[pl.ds(PIECES + piece, CHANNELS, stride=ROWS_OUT), :].T
-        large[at, :] = c_ref[pl.ds(2 * PIECES + piece, CHANNELS, stride=ROWS_OUT), :].T
         pieces = (
             (q_ref, conv, o_hbm),
             (u_ref, conv, qg_hbm),
@@ -214,7 +213,20 @@
                 pltpu.make_async_copy(small.at[index, at, :], target.at[0, at, :], sems.at[index, piece])
             )
             copies[-1].start()
-        copies.append(pltpu.make_async_copy(large.at[at, :], fg_hbm.at[at, :], large_sems.at[piece]))
+    for copy in copies:
+        copy.wait()
+
+
+def quarter_kernel(c_ref, out_ref):
+    out_ref[...] = c_ref[pl.ds(2 * PIECES, CHANNELS, stride=ROWS_OUT), :].T
+
+
+def place_kernel(part_ref, *refs):
+    quarters, fg_hbm, sems = refs[:PIECES], refs[PIECES], refs[PIECES + 1]
+    copies = []
+    for other, quarter in enumerate(quarters):
+        first = pl.multiple_of(lax.bitwise_xor(part_ref[1], other) * LANES, LANES)
+        copies.append(pltpu.make_async_copy(quarter, fg_hbm.at[pl.ds(first, LANES), :], sems.at[other]))
         copies[-1].start()
     for copy in copies:
         copy.wait()
@@ -253,17 +265,37 @@
     half = jax.ShapeDtypeStruct((1, BLOCK, CHANNELS), jnp.bfloat16)
     return pl.pallas_call(
         post_kernel,
-        out_shape=(half, half, half, half, jax.ShapeDtypeStruct((BLOCK, CHANNELS), jnp.float32)),
+        out_shape=(half, half, half, half),
         in_specs=[pl.BlockSpec(memory_space=pltpu.VMEM)] * 5,
-        out_specs=[pl.BlockSpec(memory_space=pltpu.HBM)] * 5,
+        out_specs=[pl.BlockSpec(memory_space=pltpu.HBM)] * 4,
         scratch_shapes=[
             pltpu.VMEM((4, BLOCK, CHANNELS), jnp.bfloat16),
-            pltpu.VMEM((BLOCK, CHANNELS), jnp.float32),
             pltpu.SemaphoreType.DMA((4, PIECES)),
-            pltpu.SemaphoreType.DMA((PIECES,)),
         ],
+        cost_estimate=pl.CostEstimate(flops=2 << 20, bytes_accessed=4 << 20, transcendentals=0),
         compiler_params=params(),
     )(returned, query_seq, key_seq, value_seq, upstream)
+
+
+def quarter_of(returned):
+    return pl.pallas_call(
+        quarter_kernel,
+        out_shape=jax.ShapeDtypeStruct((LANES, CHANNELS), jnp.float32),
+        in_specs=[pl.BlockSpec(memory_space=pltpu.VMEM)],
+        out_specs=pl.BlockSpec(memory_space=pltpu.VMEM),
+        compiler_params=params(),
+    )(returned)
+
+
+def place(part, quarters):
+    return pl.pallas_call(
+        place_kernel,
+        out_shape=jax.ShapeDtypeStruct((BLOCK, CHANNELS), jnp.float32),
+        in_specs=[pl.BlockSpec(memory_space=pltpu.SMEM)] + [pl.BlockSpec(memory_space=pltpu.VMEM)] * PIECES,
+        out_specs=pl.BlockSpec(memory_space=pltpu.HBM),
+        scratch_shapes=[pltpu.SemaphoreType.DMA((PIECES,))],
+        compiler_params=params(),
+    )(part, *quarters)
 
 
 def exchange(rows, depth):
@@ -274,12 +306,18 @@
 
 def local(query_seq, key_seq, value_seq, upstream, filter_param):
     tables = [jnp.asarray(table) for table in constants()]
-    part = lax.div(lax.axis_index("dp"), 2).astype(jnp.int32).reshape(1)
+    row = lax.axis_index("dp")
+    part = jnp.stack([lax.div(row, 2), lax.rem(row, PIECES)]).astype(jnp.int32)
     sent = pre(part, query_seq, key_seq, value_seq, upstream, filter_param)
     arrived = exchange(sent, ROWS_IN)
     results = transform(arrived, tables)
     returned = exchange(results, ROWS_OUT)
-    return post(returned, query_seq, key_seq, value_seq, upstream)
+    mine = quarter_of(returned)
+    quarters = [mine]
+    for other in range(1, PIECES):
+        quarters.append(lax.ppermute(mine, "dp", [(device, device ^ other) for device in range(SEQS)]))
+    outputs = post(returned, query_seq, key_seq, value_seq, upstream)
+    return (*outputs, place(part, quarters))
 
 
 def solution(mesh):

time: 105 us -> 107 us (1.019)
  blocking collectives: 97.7 us -> 89.3 us
  waiting for transfers between devices: 0 us -> 4.8 us
  starting transfers between devices: 0 us -> 3.34 us
  Pallas kernels: 6.54 us -> 8.2 us
    all_to_all x2, blocking collectives: 97.7 us -> 89.3 us  [exchange(): lax.all_to_all(shaped, ('dp', 'seq'), split_axis=0, concat_axis=0, tiled=...]
    ppermute x0 -> x3, waiting for transfers between devices: none -> 4.8 us  [local(): lax.ppermute(mine, 'dp', [(device, device ^ other) for device in range(SE...]
    ppermute x0 -> x3, starting transfers between devices: none -> 3.34 us  [local(): lax.ppermute(mine, 'dp', [(device, device ^ other) for device in range(SE...]
    pallas_call x1 -> x3, Pallas kernels: 1.4 us -> 2.65 us  [the longest x1 1.36 us: place(): pl.pallas_call(place_kernel, out_shape=jax.ShapeDtypeStruct((BLOCK, CHANN...]
  transfers between devices with their start and end apart: 0 -> 3, of which waited for: 0 -> 2; matrix products, arithmetic and copies ran while one was open for 0% -> 0% of each run, Pallas kernels for 0% -> 1%
where the time goes in v7:
time: 107 us
  blocking collectives  89.3 us (83%)
  Pallas kernels  8.2 us (8%)
  waiting for transfers between devices  4.8 us (4%)
  starting transfers between devices  3.34 us (3%)
    all_to_all x2, blocking collectives, exchange(): lax.all_to_all(shaped, ('dp', 'seq'), split_axis=0, concat_axis=0, tiled=...  89.3 us
    ppermute x3, waiting for transfers between devices, local(): lax.ppermute(mine, 'dp', [(device, device ^ other) for device in range(SE...  4.8 us
    ppermute x3, starting transfers between devices, local(): lax.ppermute(mine, 'dp', [(device, device ^ other) for device in range(SE...  3.34 us
    pallas_call x1, Pallas kernels, transform(): pl.pallas_call(fft_kernel, out_shape=jax.ShapeDtypeStruct((SEQS * OWNERS...  3.26 us
    pallas_call x1, Pallas kernels, pre(): pl.pallas_call(pre_kernel, out_shape=jax.ShapeDtypeStruct((CHANNELS * ROW...  2.29 us
  transfers between devices with their start and end apart: 3, of which 2 were waited for; matrix products, arithmetic and copies ran while one was open for 0% of the time, Pallas kernels for 1%

profile of v7, /device:TPU:1, one launch (start us, length us, event | category | flops | bytes accessed | tf_op | source)
XLA Modules:
  0.0 106.5 jit_solution(10322546114341394573)
XLA Ops:
  0.6 0.1 pad_add_fusion.part_ref
  0.7 2.3 %shard_map.137 = f32[2304,128]{1,0:T(8,128)S(1)} custom-call(s32[2]{0:T(128)S(1)} %pad_add_fusion.part_ref, bf16[1,512,256]{2,1,0:T(8,128)(2,1)} %q_ref.1, bf16[1,512,256]{2,1,0:T(8,128)(2,1)} %k_ref.1, bf16[1,512,256]{2,1,0:T(8,128)(2,1)} %v_ref.1, bf16[1,512,256]{2,1,0:T(8,128)(2,1)} %u_ref.1, f32[512,256]{1,0:T(8,128)} %f_hbm.1), custom_call_target="tpu_custom_call" | custom-call | tf_op jit(solution)/shard_map/pallas_call | solution.py:241
  3.0 0.0 copy-start.4
  3.0 0.0 copy-start.5
  3.0 0.0 copy-start.6
  3.0 0.0 copy-start.7
  3.1 0.0 copy-start.8
  3.1 49.2 %all_to_all.10 = f32[256,9,1,128]{3,2,1,0:T(1,128)S(1)} all-to-all(f32[256,9,1,128]{3,2,1,0:T(1,128)S(1)} %bitcast.10), channel_id=1, replica_groups=mesh['dp'=8,'seq'=32] {'dp','seq'}, dimensions={0} | all-to-all | bytes 2359296 | tf_op jit(solution)/shard_map/all_to_all | solution.py:303
  52.3 0.0 copy-done.4
  52.3 0.0 copy-done.5
  52.3 0.0 copy-done.6
  52.3 0.0 copy-done.7
  52.3 0.0 copy-done.8
  52.3 3.3 %shard_map.138 = f32[2304,128]{1,0:T(8,128)S(1)} custom-call(f32[2304,128]{1,0:T(8,128)S(1)} %bitcast.8, bf16[256,384]{1,0:T(8,128)(2,1)S(1)} %copy-done.7, bf16[768,256]{1,0:T(8,128)(2,1)S(1)} %copy-done.5, bf16[768,256]{1,0:T(8,128)(2,1)S(1)} %copy-done.4, bf16[128,768]{1,0:T(8,128)(2,1)S(1)} %copy-done.6, f32[2,128,128]{2,1,0:T(8,128)S(1)} %copy-done.8), custom_call_target="tpu_custom_call" | custom-call | tf_op jit(solution)/shard_map/pallas_call | solution.py:257
  55.6 40.1 %all_to_all.11 = f32[256,9,1,128]{3,2,1,0:T(1,128)S(1)} all-to-all(f32[256,9,1,128]{3,2,1,0:T(1,128)S(1)} %bitcast.9), channel_id=1, replica_groups=mesh['dp'=8,'seq'=32] {'dp','seq'}, dimensions={0} | all-to-all | bytes 2359296 | tf_op jit(solution)/shard_map/all_to_all | solution.py:303
  95.7 0.0 copy-start
  95.7 0.0 copy-start.1
  95.7 0.0 copy-start.2
  95.7 0.0 copy-start.3
  95.7 0.1 shard_map.140.refs_0_
  95.8 0.8 collective-permute-start.2
  96.6 2.3 %collective-permute-start.1 = (f32[128,256]{1,0:T(8,128)S(1)}, f32[128,256]{1,0:T(8,128)S(1)}, u32[]{:S(2)}, u32[]{:S(2)}) collective-permute-start(f32[128,256]{1,0:T(8,128)S(1)} %shard_map.140.refs_0_), channel_id=1, source_target_pairs={{0,64},{32,96},{64,0},{96,32},{128,192},{160,224},{192,128},{224,1... | collective-permute-start | bytes 393224 | tf_op jit(solution)/shard_map/ppermute | solution.py:318
  98.8 0.3 collective-permute-start
  99.1 0.0 copy-done
  99.1 0.0 copy-done.1
  99.1 0.0 copy-done.2
  99.1 0.0 copy-done.3
  99.1 1.2 %shard_map.139 = (bf16[1,512,256]{2,1,0:T(8,128)(2,1)}, bf16[1,512,256]{2,1,0:T(8,128)(2,1)}, bf16[1,512,256]{2,1,0:T(8,128)(2,1)}, bf16[1,512,256]{2,1,0:T(8,128)(2,1)}) custom-call(f32[2304,128]{1,0:T(8,128)S(1)} %bitcast.7, bf16[1,512,256]{2,1,0:T(8,128)(2,1)S(1)} %copy-done, bf16[1,512,256]{2,1,0:T(8,128)(2,1)S(1)} %copy-done.1, ...), custom_call_target="tpu_custom_call" | custom-call | flops 2097152 | bytes 4194304 | tf_op jit(solution)/shard_map/pallas_call | solution.py:266
  100.3 4.3 %collective-permute-done.2.refs_3_ = f32[128,256]{1,0:T(8,128)S(1)} collective-permute-done((f32[128,256]{1,0:T(8,128)S(1)}, f32[128,256]{1,0:T(8,128)S(1)}, u32[]{:S(2)}, u32[]{:S(2)}) %collective-permute-start.2) | collective-permute-done | bytes 131104 | tf_op jit(solution)/shard_map/ppermute | solution.py:318
  104.6 0.0 collective-permute-done.1.refs_2_
  104.6 0.5 collective-permute-done.refs_1_
  105.1 1.4 %shard_map.141 = f32[512,256]{1,0:T(8,128)} custom-call(s32[2]{0:T(128)S(1)} %pad_add_fusion.part_ref, f32[128,256]{1,0:T(8,128)S(1)} %shard_map.140.refs_0_, f32[128,256]{1,0:T(8,128)S(1)} %collective-permute-done.refs_1_, f32[128,256]{1,0:T(8,128)S(1)} %collective-permute-done.1.refs_2_, f32[128,256]{1,0:T(8,128)S(1)} %collective-permute-done.2.refs_3_), custom_call_target="tpu_custom_call" | custom-call | tf_op jit(solution)/shard_map/pallas_call | solution.py:291
Async XLA Ops:
  3.0 49.3 %copy-start.4 = (bf16[768,256]{1,0:T(8,128)(2,1)S(1)}, bf16[768,256]{1,0:T(8,128)(2,1)}, u32[]{:S(2)}) copy-start(bf16[768,256]{1,0:T(8,128)(2,1)} %constant.27.clone.inner_back_ref) | copy-start | bytes 1179652
  3.0 49.3 %copy-start.5 = (bf16[768,256]{1,0:T(8,128)(2,1)S(1)}, bf16[768,256]{1,0:T(8,128)(2,1)}, u32[]{:S(2)}) copy-start(bf16[768,256]{1,0:T(8,128)(2,1)} %constant.26.clone.inner_ref) | copy-start | bytes 1179652
  3.0 49.2 %copy-start.6 = (bf16[128,768]{1,0:T(8,128)(2,1)S(1)}, bf16[128,768]{1,0:T(8,128)(2,1)}, u32[]{:S(2)}) copy-start(bf16[128,768]{1,0:T(8,128)(2,1)} %constant.28.clone.back_ref) | copy-start | bytes 589828
  3.0 49.2 %copy-start.7 = (bf16[256,384]{1,0:T(8,128)(2,1)S(1)}, bf16[256,384]{1,0:T(8,128)(2,1)}, u32[]{:S(2)}) copy-start(bf16[256,384]{1,0:T(8,128)(2,1)} %constant.25.clone.outer_ref) | copy-start | bytes 589828
  3.1 49.2 %copy-start.8 = (f32[2,128,128]{2,1,0:T(8,128)S(1)}, f32[2,128,128]{2,1,0:T(8,128)}, u32[]{:S(2)}) copy-start(f32[2,128,128]{2,1,0:T(8,128)} %constant.29.clone.twiddle_ref) | copy-start | bytes 393220
  95.7 3.5 %copy-start = (bf16[1,512,256]{2,1,0:T(8,128)(2,1)S(1)}, bf16[1,512,256]{2,1,0:T(8,128)(2,1)}, u32[]{:S(2)}) copy-start(bf16[1,512,256]{2,1,0:T(8,128)(2,1)} %q_ref.1) | copy-start | bytes 786436
  95.7 3.5 %copy-start.1 = (bf16[1,512,256]{2,1,0:T(8,128)(2,1)S(1)}, bf16[1,512,256]{2,1,0:T(8,128)(2,1)}, u32[]{:S(2)}) copy-start(bf16[1,512,256]{2,1,0:T(8,128)(2,1)} %k_ref.1) | copy-start | bytes 786436
  95.7 3.5 %copy-start.2 = (bf16[1,512,256]{2,1,0:T(8,128)(2,1)S(1)}, bf16[1,512,256]{2,1,0:T(8,128)(2,1)}, u32[]{:S(2)}) copy-start(bf16[1,512,256]{2,1,0:T(8,128)(2,1)} %v_ref.1) | copy-start | bytes 786436
  95.7 3.5 %copy-start.3 = (bf16[1,512,256]{2,1,0:T(8,128)(2,1)S(1)}, bf16[1,512,256]{2,1,0:T(8,128)(2,1)}, u32[]{:S(2)}) copy-start(bf16[1,512,256]{2,1,0:T(8,128)(2,1)} %u_ref.1) | copy-start | bytes 786436
  95.8 8.8 %collective-permute-start.2 = (f32[128,256]{1,0:T(8,128)S(1)}, f32[128,256]{1,0:T(8,128)S(1)}, u32[]{:S(2)}, u32[]{:S(2)}) collective-permute-start(f32[128,256]{1,0:T(8,128)S(1)} %shard_map.140.refs_0_), channel_id=1, source_target_pairs={{0,96},{32,64},{64,32},{96,0},{128,224},{160,192},{192,160},{224,1... | collective-permute-start | bytes 393224 | tf_op jit(solution)/shard_map/ppermute | solution.py:318
  96.6 8.0 %collective-permute-start.1 = (f32[128,256]{1,0:T(8,128)S(1)}, f32[128,256]{1,0:T(8,128)S(1)}, u32[]{:S(2)}, u32[]{:S(2)}) collective-permute-start(f32[128,256]{1,0:T(8,128)S(1)} %shard_map.140.refs_0_), channel_id=1, source_target_pairs={{0,64},{32,96},{64,0},{96,32},{128,192},{160,224},{192,128},{224,1... | collective-permute-start | bytes 393224 | tf_op jit(solution)/shard_map/ppermute | solution.py:318
  98.8 6.3 %collective-permute-start = (f32[128,256]{1,0:T(8,128)S(1)}, f32[128,256]{1,0:T(8,128)S(1)}, u32[]{:S(2)}, u32[]{:S(2)}) collective-permute-start(f32[128,256]{1,0:T(8,128)S(1)} %shard_map.140.refs_0_), channel_id=1, source_target_pairs={{0,32},{32,0},{64,96},{96,64},{128,160},{160,128},{192,224},{224,1... | collective-permute-start | bytes 393224 | tf_op jit(solution)/shard_map/ppermute | solution.py:318

commit v8 on v6

--- a/solution.py
+++ b/solution.py
@@ -53,7 +53,7 @@
     return (outer_cat, inner_cat, inner_back, back_cat, twiddle)
 
 
-def pre_kernel(part_ref, q_hbm, k_hbm, v_hbm, u_hbm, f_hbm, out_ref, data, taps, sems, taps_sem):
+def pre_kernel(q_hbm, k_hbm, v_hbm, u_hbm, f_hbm, out_ref, data, taps, sems, taps_sem):
     sources = (k_hbm, v_hbm, u_hbm, q_hbm)
     copies = []
     for piece in range(PIECES):
@@ -66,7 +66,7 @@
         )
         for copy in copies[-1]:
             copy.start()
-    first = pl.multiple_of(part_ref[0] * LANES, LANES)
+    first = pl.multiple_of(lax.div(lax.axis_index("dp"), 2) * LANES, LANES)
     taps_copy = pltpu.make_async_copy(f_hbm.at[pl.ds(first, LANES), :], taps, taps_sem)
     taps_copy.start()
     for piece in range(PIECES):
@@ -224,12 +224,12 @@
     return pltpu.CompilerParams(vmem_limit_bytes=VMEM_LIMIT)
 
 
-def pre(part, *arrays):
+def pre(*arrays):
     arrays = [pltpu.with_memory_space_constraint(array, pltpu.HBM) for array in arrays]
     return pl.pallas_call(
         pre_kernel,
         out_shape=jax.ShapeDtypeStruct((CHANNELS * ROWS_IN, LANES), jnp.float32),
-        in_specs=[pl.BlockSpec(memory_space=pltpu.SMEM)] + [pl.BlockSpec(memory_space=pltpu.HBM)] * 5,
+        in_specs=[pl.BlockSpec(memory_space=pltpu.HBM)] * 5,
         out_specs=pl.BlockSpec(memory_space=pltpu.VMEM),
         scratch_shapes=[
             pltpu.VMEM((4, BLOCK, CHANNELS), jnp.bfloat16),
@@ -238,7 +238,7 @@
             pltpu.SemaphoreType.DMA,
         ],
         compiler_params=params(),
-    )(part, *arrays)
+    )(*arrays)
 
 
 def transform(arrived, tables):
@@ -274,8 +274,7 @@
 
 def local(query_seq, key_seq, value_seq, upstream, filter_param):
     tables = [jnp.asarray(table) for table in constants()]
-    part = lax.div(lax.axis_index("dp"), 2).astype(jnp.int32).reshape(1)
-    sent = pre(part, query_seq, key_seq, value_seq, upstream, filter_param)
+    sent = pre(query_seq, key_seq, value_seq, upstream, filter_param)
     arrived = exchange(sent, ROWS_IN)
     results = transform(arrived, tables)
     returned = exchange(results, ROWS_OUT)

time: 105 us -> 105 us (level)
  no operation moved by 1% of the time
where the time goes in v8:
time: 105 us
  blocking collectives  97.7 us (93%)
  Pallas kernels  6.45 us (6%)
    all_to_all x2, blocking collectives, exchange(): lax.all_to_all(shaped, ('dp', 'seq'), split_axis=0, concat_axis=0, tiled=...  97.7 us
    pallas_call x1, Pallas kernels, transform(): pl.pallas_call(fft_kernel, out_shape=jax.ShapeDtypeStruct((SEQS * OWNERS...  3.29 us

profile of v8, /device:TPU:1, one launch (start us, length us, event | category | flops | bytes accessed | tf_op | source)
XLA Modules:
  0.0 105.0 jit_solution(2418333604337183870)
XLA Ops:
  0.6 1.8 %shard_map.137 = f32[2304,128]{1,0:T(8,128)S(1)} custom-call(bf16[1,512,256]{2,1,0:T(8,128)(2,1)} %q_ref.1, bf16[1,512,256]{2,1,0:T(8,128)(2,1)} %k_ref.1, bf16[1,512,256]{2,1,0:T(8,128)(2,1)} %v_ref.1, bf16[1,512,256]{2,1,0:T(8,128)(2,1)} %u_ref.1, f32[512,256]{1,0:T(8,128)} %f_hbm.1), custom_call_target="tpu_custom_call" | custom-call | tf_op jit(solution)/shard_map/pallas_call | solution.py:229
  2.4 0.0 copy-start.4
  2.4 0.0 copy-start.5
  2.4 0.0 copy-start.6
  2.4 0.0 copy-start.7
  2.4 0.0 copy-start.8
  2.5 49.2 %all_to_all.10 = f32[256,9,1,128]{3,2,1,0:T(1,128)S(1)} all-to-all(f32[256,9,1,128]{3,2,1,0:T(1,128)S(1)} %bitcast.7), channel_id=1, replica_groups=mesh['dp'=8,'seq'=32] {'dp','seq'}, dimensions={0} | all-to-all | bytes 2359296 | tf_op jit(solution)/shard_map/all_to_all | solution.py:271
  51.6 0.0 copy-done.4
  51.7 0.0 copy-done.5
  51.7 0.0 copy-done.6
  51.7 0.0 copy-done.7
  51.7 0.0 copy-done.8
  51.7 3.3 %shard_map.138 = f32[3072,128]{1,0:T(8,128)S(1)} custom-call(f32[2304,128]{1,0:T(8,128)S(1)} %bitcast.6, bf16[256,384]{1,0:T(8,128)(2,1)S(1)} %copy-done.7, bf16[768,256]{1,0:T(8,128)(2,1)S(1)} %copy-done.5, bf16[768,256]{1,0:T(8,128)(2,1)S(1)} %copy-done.4, bf16[128,768]{1,0:T(8,128)(2,1)S(1)} %copy-done.6, f32[2,128,128]{2,1,0:T(8,128)S(1)} %copy-done.8), custom_call_target="tpu_custom_call" | custom-call | tf_op jit(solution)/shard_map/pallas_call | solution.py:245
  55.0 0.0 copy-start
  55.0 0.0 copy-start.1
  55.0 0.0 copy-start.2
  55.0 0.0 copy-start.3
  55.0 48.5 %all_to_all.11 = f32[256,12,1,128]{3,2,1,0:T(1,128)S(1)} all-to-all(f32[256,12,1,128]{3,2,1,0:T(1,128)S(1)} %bitcast.5), channel_id=1, replica_groups=mesh['dp'=8,'seq'=32] {'dp','seq'}, dimensions={0} | all-to-all | bytes 3145728 | tf_op jit(solution)/shard_map/all_to_all | solution.py:271
  103.6 0.0 copy-done
  103.6 0.0 copy-done.1
  103.6 0.0 copy-done.2
  103.6 0.0 copy-done.3
  103.6 1.4 %shard_map.139 = (bf16[1,512,256]{2,1,0:T(8,128)(2,1)}, bf16[1,512,256]{2,1,0:T(8,128)(2,1)}, bf16[1,512,256]{2,1,0:T(8,128)(2,1)}, bf16[1,512,256]{2,1,0:T(8,128)(2,1)}, f32[512,256]{1,0:T(8,128)}) custom-call(f32[3072,128]{1,0:T(8,128)S(1)} %bitcast.4, bf16[1,512,256]{2,1,0:T(8,128)(2,1)S(1)} %copy-done, bf16[1,512,256]{2,1,0:T(8,128)(2,1)S(1)} %copy-done.1, ...), custom_call_target="tpu_custom_call" | custom-call | tf_op jit(solution)/shard_map/pallas_call | solution.py:254
Async XLA Ops:
  2.4 49.3 %copy-start.4 = (bf16[768,256]{1,0:T(8,128)(2,1)S(1)}, bf16[768,256]{1,0:T(8,128)(2,1)}, u32[]{:S(2)}) copy-start(bf16[768,256]{1,0:T(8,128)(2,1)} %constant.12.clone.inner_back_ref) | copy-start | bytes 1179652
  2.4 49.3 %copy-start.5 = (bf16[768,256]{1,0:T(8,128)(2,1)S(1)}, bf16[768,256]{1,0:T(8,128)(2,1)}, u32[]{:S(2)}) copy-start(bf16[768,256]{1,0:T(8,128)(2,1)} %constant.11.clone.inner_ref) | copy-start | bytes 1179652
  2.4 49.2 %copy-start.6 = (bf16[128,768]{1,0:T(8,128)(2,1)S(1)}, bf16[128,768]{1,0:T(8,128)(2,1)}, u32[]{:S(2)}) copy-start(bf16[128,768]{1,0:T(8,128)(2,1)} %constant.13.clone.back_ref) | copy-start | bytes 589828
  2.4 49.2 %copy-start.7 = (bf16[256,384]{1,0:T(8,128)(2,1)S(1)}, bf16[256,384]{1,0:T(8,128)(2,1)}, u32[]{:S(2)}) copy-start(bf16[256,384]{1,0:T(8,128)(2,1)} %constant.10.clone.outer_ref) | copy-start | bytes 589828
  2.4 49.2 %copy-start.8 = (f32[2,128,128]{2,1,0:T(8,128)S(1)}, f32[2,128,128]{2,1,0:T(8,128)}, u32[]{:S(2)}) copy-start(f32[2,128,128]{2,1,0:T(8,128)} %constant.14.clone.twiddle_ref) | copy-start | bytes 393220
  55.0 48.6 %copy-start = (bf16[1,512,256]{2,1,0:T(8,128)(2,1)S(1)}, bf16[1,512,256]{2,1,0:T(8,128)(2,1)}, u32[]{:S(2)}) copy-start(bf16[1,512,256]{2,1,0:T(8,128)(2,1)} %q_ref.1) | copy-start | bytes 786436
  55.0 48.6 %copy-start.1 = (bf16[1,512,256]{2,1,0:T(8,128)(2,1)S(1)}, bf16[1,512,256]{2,1,0:T(8,128)(2,1)}, u32[]{:S(2)}) copy-start(bf16[1,512,256]{2,1,0:T(8,128)(2,1)} %k_ref.1) | copy-start | bytes 786436
  55.0 48.6 %copy-start.2 = (bf16[1,512,256]{2,1,0:T(8,128)(2,1)S(1)}, bf16[1,512,256]{2,1,0:T(8,128)(2,1)}, u32[]{:S(2)}) copy-start(bf16[1,512,256]{2,1,0:T(8,128)(2,1)} %v_ref.1) | copy-start | bytes 786436
  55.0 48.6 %copy-start.3 = (bf16[1,512,256]{2,1,0:T(8,128)(2,1)S(1)}, bf16[1,512,256]{2,1,0:T(8,128)(2,1)}, u32[]{:S(2)}) copy-start(bf16[1,512,256]{2,1,0:T(8,128)(2,1)} %u_ref.1) | copy-start | bytes 786436

commit v9 on v8

--- a/solution.py
+++ b/solution.py
@@ -15,7 +15,12 @@
 SEQS = 8
 OWNERS = 32
 PIECES = BLOCK // LANES
-ROWS_IN = 2 * PIECES + 1
+CHIPS = OWNERS // 2
+PLACES = SEQS * CHIPS
+ROWS_ONE = 2 * PIECES
+ROWS_IN = 2 * ROWS_ONE + 1
+ROWS_SWAP = ROWS_ONE + 1
+TAPS = BLOCK // SEQS
 ROWS_OUT = 3 * PIECES
 HALF = 128
 LENGTH = 2 * BLOCK * OWNERS
@@ -34,12 +39,15 @@
     rows = np.arange(HALF, dtype=np.int64)
     coarse = (rows % OWNERS) * PIECES + rows // OWNERS
     turn = 2.0 * np.pi * (np.outer(2 * freq + 1, coarse) % (4 * HALF)) / (4 * HALF)
+    back_outer = np.concatenate([np.cos(turn), -np.sin(turn)], axis=0).T
+    owner = (rows % CHIPS) * 2 + rows % OWNERS // CHIPS
+    coarse = owner * PIECES + rows // OWNERS
+    turn = 2.0 * np.pi * (np.outer(2 * freq + 1, coarse) % (4 * HALF)) / (4 * HALF)
     outer = np.concatenate([np.cos(turn), -np.sin(turn)], axis=0)
     outer_high, outer_low = split_parts(outer)
     outer_cat = np.concatenate([outer_high, outer_high, outer_low], axis=1)
     scale = 2.0 / LENGTH / math.sqrt(LENGTH // 2)
-    back_outer = outer.T * scale
-    back_high, back_low = split_parts(back_outer)
+    back_high, back_low = split_parts(back_outer * scale)
     back_cat = np.concatenate([back_high, back_high, back_low], axis=1)
     lanes = np.arange(LANES, dtype=np.int64)
     inner_turn = 2.0 * np.pi * (np.outer(lanes, lanes) % LANES) / LANES
@@ -66,19 +74,35 @@
         )
         for copy in copies[-1]:
             copy.start()
-    first = pl.multiple_of(lax.div(lax.axis_index("dp"), 2) * LANES, LANES)
-    taps_copy = pltpu.make_async_copy(f_hbm.at[pl.ds(first, LANES), :], taps, taps_sem)
+    first = pl.multiple_of(lax.axis_index("dp") * TAPS, TAPS)
+    taps_copy = pltpu.make_async_copy(f_hbm.at[pl.ds(first, TAPS), :], taps, taps_sem)
     taps_copy.start()
+    even = lax.axis_index("core") == 0
+
+    def store(rows, row):
+        lower, upper = rows[:PLACES], rows[PLACES:]
+        out_ref[pl.ds(row, PLACES, stride=ROWS_IN), :] = jnp.where(even, lower, upper)
+        out_ref[pl.ds(ROWS_ONE + row, PLACES, stride=ROWS_IN), :] = jnp.where(even, upper, lower)
+
     for piece in range(PIECES):
         for copy in copies[piece]:
             copy.wait()
         key, value, grad, query = [
             data[index, pl.ds(piece * LANES, LANES), :].astype(jnp.float32) for index in range(4)
         ]
-        out_ref[pl.ds(piece, CHANNELS, stride=ROWS_IN), :] = (key * value).T
-        out_ref[pl.ds(PIECES + piece, CHANNELS, stride=ROWS_IN), :] = (grad * query).T
+        store((key * value).T, piece)
+        store((grad * query).T, PIECES + piece)
     taps_copy.wait()
-    out_ref[pl.ds(2 * PIECES, CHANNELS, stride=ROWS_IN), :] = taps[...].T
+    lower, upper = taps[:, :PLACES], taps[:, PLACES:]
+    both = jnp.concatenate([jnp.where(even, lower, upper), jnp.where(even, upper, lower)], axis=0)
+    out_ref[pl.ds(2 * ROWS_ONE, PLACES, stride=ROWS_IN), :] = both.T
+
+
+def other_kernel(in_ref, out_ref):
+    for row in range(ROWS_SWAP):
+        out_ref[pl.ds(row, PLACES, stride=ROWS_SWAP), :] = in_ref[
+            pl.ds(ROWS_ONE + row, PLACES, stride=ROWS_IN), :
+        ]
 
 
 def halves(value, axis):
@@ -91,14 +115,38 @@
     return jnp.dot(left, right, preferred_element_type=jnp.float32)
 
 
-def fft_kernel(in_ref, outer_ref, inner_ref, inner_back_ref, back_ref, twiddle_ref, out_ref):
+def fft_kernel(in_ref, swap_ref, outer_ref, inner_ref, inner_back_ref, back_ref, twiddle_ref, out_ref):
     cos_t = twiddle_ref[0]
     sin_t = twiddle_ref[1]
 
-    def load(base):
-        return jnp.concatenate(
-            [in_ref[pl.ds(base + piece, OWNERS, stride=ROWS_IN), :] for piece in range(PIECES)], axis=0
-        )
+    even = lax.axis_index("core") == 0
+
+    def by_core(mine, other):
+        return [jnp.where(even, mine, other), jnp.where(even, other, mine)]
+
+    def load(seq, first):
+        rows = []
+        for piece in range(first, first + PIECES):
+            mine = in_ref[pl.ds(seq * CHIPS * ROWS_IN + piece, CHIPS, stride=ROWS_IN), :]
+            other = swap_ref[pl.ds(seq * CHIPS * ROWS_SWAP + piece, CHIPS, stride=ROWS_SWAP), :]
+            rows += by_core(mine, other)
+        return jnp.concatenate(rows, axis=0)
+
+    def load_taps():
+        lower = lax.broadcasted_iota(jnp.int32, (CHIPS, LANES), 1) < TAPS
+        rows = []
+        for piece in range(PIECES):
+            mine, other = [], []
+            for seq in (2 * piece, 2 * piece + 1):
+                mine.append(in_ref[pl.ds(seq * CHIPS * ROWS_IN + 2 * ROWS_ONE, CHIPS, stride=ROWS_IN), :])
+                other.append(
+                    swap_ref[pl.ds(seq * CHIPS * ROWS_SWAP + ROWS_ONE, CHIPS, stride=ROWS_SWAP), :]
+                )
+            rows += by_core(
+                jnp.where(lower, mine[0], pltpu.roll(mine[1], TAPS, 1)),
+                jnp.where(lower, pltpu.roll(other[0], TAPS, 1), other[1]),
+            )
+        return jnp.concatenate(rows, axis=0)
 
     def outer(signals):
         first = dot(outer_ref[...], halves(jnp.concatenate(signals, axis=1), 0))
@@ -130,13 +178,6 @@
                 piece * OWNERS : (piece + 1) * OWNERS, :
             ]
 
-    taps = jnp.concatenate(
-        [
-            in_ref[pl.ds(2 * piece * OWNERS * ROWS_IN + 2 * PIECES, OWNERS, stride=ROWS_IN), :]
-            for piece in range(PIECES)
-        ],
-        axis=0,
-    )
     lag_real = jnp.zeros((HALF, LANES), jnp.float32)
     lag_imag = jnp.zeros((HALF, LANES), jnp.float32)
     starts = range(0, SEQS, GROUP)
@@ -144,10 +185,9 @@
     for start in starts:
         turned = []
         for seq in range(start, start + GROUP):
-            base = seq * OWNERS * ROWS_IN
-            turned += outer([load(base), load(base + PIECES)])
+            turned += outer([load(seq, 0), load(seq, PIECES)])
         groups.append(turned)
-    groups[0] += outer([taps])
+    groups[0] += outer([load_taps()])
     spectra = [inner(turned, inner_ref) for turned in groups]
     taps_spec = spectra[0][2 * GROUP * HALF :]
     taps_real, taps_imag = taps_spec[:, :LANES], taps_spec[:, LANES:]
@@ -196,12 +236,18 @@
 def post_kernel(
     c_ref, q_ref, k_ref, v_ref, u_ref, o_hbm, qg_hbm, kg_hbm, vg_hbm, fg_hbm, small, large, sems, large_sems
 ):
+    def arrived(row):
+        cores = [
+            c_ref[pl.ds(core * ROWS_OUT + row, PLACES, stride=2 * ROWS_OUT), :] for core in range(2)
+        ]
+        return jnp.concatenate(cores, axis=0).T
+
     copies = []
     for piece in range(PIECES):
         at = pl.ds(piece * LANES, LANES)
-        conv = c_ref[pl.ds(piece, CHANNELS, stride=ROWS_OUT), :].T
-        back = c_ref[pl.ds(PIECES + piece, CHANNELS, stride=ROWS_OUT), :].T
-        large[at, :] = c_ref[pl.ds(2 * PIECES + piece, CHANNELS, stride=ROWS_OUT), :].T
+        conv = arrived(piece)
+        back = arrived(PIECES + piece)
+        large[at, :] = arrived(2 * PIECES + piece)
         pieces = (
             (q_ref, conv, o_hbm),
             (u_ref, conv, qg_hbm),
@@ -228,12 +274,12 @@
     arrays = [pltpu.with_memory_space_constraint(array, pltpu.HBM) for array in arrays]
     return pl.pallas_call(
         pre_kernel,
-        out_shape=jax.ShapeDtypeStruct((CHANNELS * ROWS_IN, LANES), jnp.float32),
+        out_shape=jax.ShapeDtypeStruct((PLACES * ROWS_IN, LANES), jnp.float32),
         in_specs=[pl.BlockSpec(memory_space=pltpu.HBM)] * 5,
         out_specs=pl.BlockSpec(memory_space=pltpu.VMEM),
         scratch_shapes=[
             pltpu.VMEM((4, BLOCK, CHANNELS), jnp.bfloat16),
-            pltpu.VMEM((LANES, CHANNELS), jnp.float32),
+            pltpu.VMEM((TAPS, CHANNELS), jnp.float32),
             pltpu.SemaphoreType.DMA((4, PIECES)),
             pltpu.SemaphoreType.DMA,
         ],
@@ -241,12 +287,20 @@
     )(*arrays)
 
 
-def transform(arrived, tables):
+def other_half(arrived):
+    return pl.pallas_call(
+        other_kernel,
+        out_shape=jax.ShapeDtypeStruct((PLACES * ROWS_SWAP, LANES), jnp.float32),
+        compiler_params=params(),
+    )(arrived)
+
+
+def transform(arrived, swapped, tables):
     return pl.pallas_call(
         fft_kernel,
         out_shape=jax.ShapeDtypeStruct((SEQS * OWNERS * ROWS_OUT, LANES), jnp.float32),
         compiler_params=params(),
-    )(arrived, *tables)
+    )(arrived, swapped, *tables)
 
 
 def post(returned, query_seq, key_seq, value_seq, upstream):
@@ -266,34 +320,30 @@
     )(returned, query_seq, key_seq, value_seq, upstream)
 
 
-def exchange(rows, depth):
-    shaped = rows.reshape(CHANNELS, depth, 1, LANES)
-    moved = lax.all_to_all(shaped, ("dp", "seq"), split_axis=0, concat_axis=0, tiled=True)
-    return moved.reshape(CHANNELS * depth, LANES)
+def exchange(rows, axes, count):
+    shaped = rows.reshape(count, rows.shape[0] // count, 1, LANES)
+    moved = lax.all_to_all(shaped, axes, split_axis=0, concat_axis=0, tiled=True)
+    return moved.reshape(rows.shape)
 
 
 def local(query_seq, key_seq, value_seq, upstream, filter_param):
     tables = [jnp.asarray(table) for table in constants()]
     sent = pre(query_seq, key_seq, value_seq, upstream, filter_param)
-    arrived = exchange(sent, ROWS_IN)
-    results = transform(arrived, tables)
-    returned = exchange(results, ROWS_OUT)
+    arrived = exchange(sent, ("dp", "chip"), PLACES)
+    swapped = lax.ppermute(other_half(arrived), "core", [(0, 1), (1, 0)])
+    results = transform(arrived, swapped, tables)
+    returned = exchange(results, ("dp", "chip", "core"), CHANNELS)
     return post(returned, query_seq, key_seq, value_seq, upstream)
 
 
 def solution(mesh):
-    in_specs = (
-        P("dp", "seq", None),
-        P("dp", "seq", None),
-        P("dp", "seq", None),
-        P("dp", "seq", None),
-        P("seq", None),
+    by_chip = jax.sharding.Mesh(mesh.devices.reshape(SEQS, CHIPS, 2), ("dp", "chip", "core"))
+    whole = P("dp", ("chip", "core"), None)
+    taps = P(("chip", "core"), None)
+    return jax.shard_map(
+        local,
+        mesh=by_chip,
+        in_specs=(whole, whole, whole, whole, taps),
+        out_specs=(whole, whole, whole, whole, taps),
+        check_vma=False,
     )
-    out_specs = (
-        P("dp", "seq", None),
-        P("dp", "seq", None),
-        P("dp", "seq", None),
-        P("dp", "seq", None),
-        P("seq", None),
-    )
-    return jax.shard_map(local, mesh=mesh, in_specs=in_specs, out_specs=out_specs, check_vma=False)

time: 105 us -> 107 us (1.019)
  starting transfers between devices: 0 us -> 2.37 us
  blocking collectives: 97.7 us -> 95.8 us
  waiting for transfers between devices: 0 us -> 1.63 us
    ppermute x0 -> x1, starting transfers between devices: none -> 2.37 us  [local(): swapped = lax.ppermute(other_half(arrived), 'core', [(0, 1), (1, 0)])]
    all_to_all x2, blocking collectives: 97.7 us -> 95.8 us  [exchange(): lax.all_to_all(shaped, axes, split_axis=0, concat_axis=0, tiled=True)]
    ppermute x0 -> x1, waiting for transfers between devices: none -> 1.63 us  [local(): swapped = lax.ppermute(other_half(arrived), 'core', [(0, 1), (1, 0)])]
  transfers between devices with their start and end apart: 0 -> 1, of which waited for: 0 -> 1; matrix products, arithmetic and copies ran while one was open for 0% -> 0% of each run, Pallas kernels for 0% -> 0%
where the time goes in v9:
time: 107 us
  blocking collectives  95.8 us (90%)
  Pallas kernels  6.49 us (6%)
  starting transfers between devices  2.37 us (2%)
  waiting for transfers between devices  1.63 us (2%)
    all_to_all x2, blocking collectives, exchange(): lax.all_to_all(shaped, axes, split_axis=0, concat_axis=0, tiled=True)  95.8 us
    pallas_call x1, Pallas kernels, transform(): pl.pallas_call(fft_kernel, out_shape=jax.ShapeDtypeStruct((SEQS * OWNERS...  3.28 us
    ppermute x1, starting transfers between devices, local(): swapped = lax.ppermute(other_half(arrived), 'core', [(0, 1), (1, 0)])  2.37 us
  transfers between devices with their start and end apart: 1, of which 1 were waited for; matrix products, arithmetic and copies ran while one was open for 0% of the time, Pallas kernels for 0%

profile of v9, /device:TPU:1, one launch (start us, length us, event | category | flops | bytes accessed | tf_op | source)
XLA Modules:
  0.0 107.1 jit_solution(11887748430946238100)
XLA Ops:
  0.6 1.8 %shard_map.137 = f32[2176,128]{1,0:T(8,128)S(1)} custom-call(bf16[1,512,256]{2,1,0:T(8,128)(2,1)} %q_ref.1, bf16[1,512,256]{2,1,0:T(8,128)(2,1)} %k_ref.1, bf16[1,512,256]{2,1,0:T(8,128)(2,1)} %v_ref.1, bf16[1,512,256]{2,1,0:T(8,128)(2,1)} %u_ref.1, f32[512,256]{1,0:T(8,128)} %f_hbm.1), custom_call_target="tpu_custom_call" | custom-call | tf_op jit(solution)/shard_map/pallas_call | solution.py:275
  2.4 0.0 copy-start.4
  2.4 0.0 copy-start.5
  2.4 0.0 copy-start.6
  2.4 0.0 copy-start.7
  2.4 0.0 copy-start.8
  2.5 48.3 %all_to_all.10 = f32[128,17,1,128]{3,2,1,0:T(1,128)S(1)} all-to-all(f32[128,17,1,128]{3,2,1,0:T(1,128)S(1)} %bitcast.8), channel_id=1, replica_groups=mesh['dp'=8,'chip'=16,'core'=2] {'dp','chip'}, dimensions={0} | all-to-all | bytes 2228224 | tf_op jit(solution)/shard_map/all_to_all | solution.py:325
  50.7 0.1 shard_map.138
  50.8 2.4 %collective-permute-start = (f32[1152,128]{1,0:T(8,128)S(1)}, f32[1152,128]{1,0:T(8,128)S(1)}, u32[]{:S(2)}, u32[]{:S(2)}) collective-permute-start(f32[1152,128]{1,0:T(8,128)S(1)} %shard_map.138), channel_id=1, source_target_pairs={{0,1},{1,0},{2,3},{3,2},{4,5},{5,4},{6,7},{7,6},{8,9},{9,8},{10,11... | collective-permute-start | bytes 1769480 | tf_op jit(solution)/shard_map/ppermute | solution.py:333
  53.1 1.6 %collective-permute-done.swap_ref = f32[1152,128]{1,0:T(8,128)S(1)} collective-permute-done((f32[1152,128]{1,0:T(8,128)S(1)}, f32[1152,128]{1,0:T(8,128)S(1)}, u32[]{:S(2)}, u32[]{:S(2)}) %collective-permute-start) | collective-permute-done | bytes 589856 | tf_op jit(solution)/shard_map/ppermute | solution.py:333
  54.8 0.0 copy-done.4
  54.8 0.0 copy-done.5
  54.8 0.0 copy-done.6
  54.8 0.0 copy-done.7
  54.8 0.0 copy-done.8
  54.8 3.3 %shard_map.139 = f32[3072,128]{1,0:T(8,128)S(1)} custom-call(f32[2176,128]{1,0:T(8,128)S(1)} %bitcast.5, f32[1152,128]{1,0:T(8,128)S(1)} %collective-permute-done.swap_ref, bf16[256,384]{1,0:T(8,128)(2,1)S(1)} %copy-done.7, bf16[768,256]{1,0:T(8,128)(2,1)S(1)} %copy-done.5, bf16[768,256]{1,0:T(8,128)(2,1)S(1)} %copy-done.4, bf16[128,768]{1,0:T(8,128)(2,1)S(1)} %copy-done.6, ...), custom_call_target="tpu_custom_call" | custom-call | tf_op jit(solution)/shard_map/pallas_call | solution.py:299
  58.1 0.0 copy-start
  58.1 0.0 copy-start.1
  58.1 0.0 copy-start.2
  58.1 0.0 copy-start.3
  58.1 47.6 %all_to_all.11 = f32[256,12,1,128]{3,2,1,0:T(1,128)S(1)} all-to-all(f32[256,12,1,128]{3,2,1,0:T(1,128)S(1)} %bitcast.6), channel_id=1, replica_groups=mesh['dp'=8,'chip'=16,'core'=2] {'dp','chip','core'}, dimensions={0} | all-to-all | bytes 3145728 | tf_op jit(solution)/shard_map/all_to_all | solution.py:325
  105.7 0.0 copy-done
  105.7 0.0 copy-done.1
  105.7 0.0 copy-done.2
  105.7 0.0 copy-done.3
  105.7 1.4 %shard_map.140 = (bf16[1,512,256]{2,1,0:T(8,128)(2,1)}, bf16[1,512,256]{2,1,0:T(8,128)(2,1)}, bf16[1,512,256]{2,1,0:T(8,128)(2,1)}, bf16[1,512,256]{2,1,0:T(8,128)(2,1)}, f32[512,256]{1,0:T(8,128)}) custom-call(f32[3072,128]{1,0:T(8,128)S(1)} %bitcast.7, bf16[1,512,256]{2,1,0:T(8,128)(2,1)S(1)} %copy-done, bf16[1,512,256]{2,1,0:T(8,128)(2,1)S(1)} %copy-done.1, ...), custom_call_target="tpu_custom_call" | custom-call | tf_op jit(solution)/shard_map/pallas_call | solution.py:308
Async XLA Ops:
  2.4 52.4 %copy-start.4 = (bf16[768,256]{1,0:T(8,128)(2,1)S(1)}, bf16[768,256]{1,0:T(8,128)(2,1)}, u32[]{:S(2)}) copy-start(bf16[768,256]{1,0:T(8,128)(2,1)} %constant.12.clone.inner_back_ref) | copy-start | bytes 1179652
  2.4 52.4 %copy-start.5 = (bf16[768,256]{1,0:T(8,128)(2,1)S(1)}, bf16[768,256]{1,0:T(8,128)(2,1)}, u32[]{:S(2)}) copy-start(bf16[768,256]{1,0:T(8,128)(2,1)} %constant.11.clone.inner_ref) | copy-start | bytes 1179652
  2.4 52.4 %copy-start.6 = (bf16[128,768]{1,0:T(8,128)(2,1)S(1)}, bf16[128,768]{1,0:T(8,128)(2,1)}, u32[]{:S(2)}) copy-start(bf16[128,768]{1,0:T(8,128)(2,1)} %constant.13.clone.back_ref) | copy-start | bytes 589828
  2.4 52.4 %copy-start.7 = (bf16[256,384]{1,0:T(8,128)(2,1)S(1)}, bf16[256,384]{1,0:T(8,128)(2,1)}, u32[]{:S(2)}) copy-start(bf16[256,384]{1,0:T(8,128)(2,1)} %constant.10.clone.outer_ref) | copy-start | bytes 589828
  2.4 52.4 %copy-start.8 = (f32[2,128,128]{2,1,0:T(8,128)S(1)}, f32[2,128,128]{2,1,0:T(8,128)}, u32[]{:S(2)}) copy-start(f32[2,128,128]{2,1,0:T(8,128)} %constant.14.clone.twiddle_ref) | copy-start | bytes 393220
  50.8 4.0 %collective-permute-start = (f32[1152,128]{1,0:T(8,128)S(1)}, f32[1152,128]{1,0:T(8,128)S(1)}, u32[]{:S(2)}, u32[]{:S(2)}) collective-permute-start(f32[1152,128]{1,0:T(8,128)S(1)} %shard_map.138), channel_id=1, source_target_pairs={{0,1},{1,0},{2,3},{3,2},{4,5},{5,4},{6,7},{7,6},{8,9},{9,8},{10,11... | collective-permute-start | bytes 1769480 | tf_op jit(solution)/shard_map/ppermute | solution.py:333
  58.1 47.6 %copy-start = (bf16[1,512,256]{2,1,0:T(8,128)(2,1)S(1)}, bf16[1,512,256]{2,1,0:T(8,128)(2,1)}, u32[]{:S(2)}) copy-start(bf16[1,512,256]{2,1,0:T(8,128)(2,1)} %q_ref.1) | copy-start | bytes 786436
  58.1 47.6 %copy-start.1 = (bf16[1,512,256]{2,1,0:T(8,128)(2,1)S(1)}, bf16[1,512,256]{2,1,0:T(8,128)(2,1)}, u32[]{:S(2)}) copy-start(bf16[1,512,256]{2,1,0:T(8,128)(2,1)} %k_ref.1) | copy-start | bytes 786436
  58.1 47.6 %copy-start.2 = (bf16[1,512,256]{2,1,0:T(8,128)(2,1)S(1)}, bf16[1,512,256]{2,1,0:T(8,128)(2,1)}, u32[]{:S(2)}) copy-start(bf16[1,512,256]{2,1,0:T(8,128)(2,1)} %v_ref.1) | copy-start | bytes 786436
  58.1 47.6 %copy-start.3 = (bf16[1,512,256]{2,1,0:T(8,128)(2,1)S(1)}, bf16[1,512,256]{2,1,0:T(8,128)(2,1)}, u32[]{:S(2)}) copy-start(bf16[1,512,256]{2,1,0:T(8,128)(2,1)} %u_ref.1) | copy-start | bytes 786436

commit v10 on v5

v10 whole, which is shorter than its diff:
```python
import math

import jax
import jax.numpy as jnp
import ml_dtypes
import numpy as np
from jax import lax
from jax.experimental import pallas as pl
from jax.experimental.pallas import tpu as pltpu
from jax.sharding import PartitionSpec as P

LANES = 128
BLOCK = 512
CHANNELS = 256
SEQS = 8
OWNERS = 32
PIECES = BLOCK // LANES
ROWS_IN = 2 * PIECES + 1
ROWS_OUT = 2 * PIECES
Z_CHIPS = 8
HALF = 128
LENGTH = 2 * BLOCK * OWNERS
GROUP = 2
VMEM_LIMIT = 32 << 20


def split_parts(values):
    high = values.astype(np.float32).astype(ml_dtypes.bfloat16)
    low = (values - high.astype(np.float64)).astype(np.float32).astype(ml_dtypes.bfloat16)
    return high, low


def constants():
    freq = np.arange(HALF, dtype=np.int64)
    rows = np.arange(HALF, dtype=np.int64)
    coarse = (rows % OWNERS) * PIECES + rows // OWNERS
    turn = 2.0 * np.pi * (np.outer(2 * freq + 1, coarse) % (4 * HALF)) / (4 * HALF)
    outer = np.concatenate([np.cos(turn), -np.sin(turn)], axis=0)
    outer_high, outer_low = split_parts(outer)
    outer_cat = np.concatenate([outer_high, outer_high, outer_low], axis=1)
    scale = 2.0 / LENGTH / math.sqrt(LENGTH // 2)
    back_outer = outer.T * scale
    back_high, back_low = split_parts(back_outer)
    back_cat = np.concatenate([back_high, back_high, back_low], axis=1)
    lanes = np.arange(LANES, dtype=np.int64)
    inner_turn = 2.0 * np.pi * (np.outer(lanes, lanes) % LANES) / LANES
    cos_in, sin_in = np.cos(inner_turn), np.sin(inner_turn)
    inner = np.block([[cos_in, -sin_in], [sin_in, cos_in]])
    inner_high, inner_low = split_parts(inner)
    inner_cat = np.concatenate([inner_high, inner_high, inner_low], axis=0)
    inner_back = np.concatenate([inner_high.T, inner_high.T, inner_low.T], axis=0)
    twist = 2.0 * np.pi * np.outer(2 * freq + 1, lanes) / (2 * LENGTH)
    twiddle = np.stack([np.cos(twist), np.sin(twist)]).astype(np.float32)
    return (outer_cat, inner_cat, inner_back, back_cat, twiddle)


def pre_kernel(q_hbm, k_hbm, v_hbm, u_hbm, f_hbm, out_ref, data, taps, sems, taps_sem):
    sources = (k_hbm, v_hbm, u_hbm, q_hbm)
    copies = []
    for piece in range(PIECES):
        at = pl.ds(piece * LANES, LANES)
        copies.append(
            [
                pltpu.make_async_copy(source.at[0, at, :], data.at[index, at, :], sems.at[index, piece])
                for index, source in enumerate(sources)
            ]
        )
        for copy in copies[-1]:
            copy.start()
    first = pl.multiple_of(lax.div(lax.axis_index("dp"), 2) * LANES, LANES)
    taps_copy = pltpu.make_async_copy(f_hbm.at[pl.ds(first, LANES), :], taps, taps_sem)
    taps_copy.start()
    for piece in range(PIECES):
        for copy in copies[piece]:
            copy.wait()
        key, value, grad, query = [
            data[index, pl.ds(piece * LANES, LANES), :].astype(jnp.float32) for index in range(4)
        ]
        out_ref[pl.ds(piece, CHANNELS, stride=ROWS_IN), :] = (key * value).T
        out_ref[pl.ds(PIECES + piece, CHANNELS, stride=ROWS_IN), :] = (grad * query).T
    taps_copy.wait()
    out_ref[pl.ds(2 * PIECES, CHANNELS, stride=ROWS_IN), :] = taps[...].T


def halves(value, axis):
    high = value.astype(jnp.bfloat16)
    low = (value - high.astype(jnp.float32)).astype(jnp.bfloat16)
    return jnp.concatenate([high, low, high], axis=axis)


def dot(left, right):
    return jnp.dot(left, right, preferred_element_type=jnp.float32)


def turn(real, imag, cos_t, sin_t, axis):
    return jnp.concatenate([real * cos_t + imag * sin_t, imag * cos_t - real * sin_t], axis=axis)


def inner(blocks, table_ref):
    return dot(halves(jnp.concatenate(blocks, axis=0), 1), table_ref[...])


def outer_back(rows, twiddle_ref, back_ref):
    turned = [
        turn(rows[at : at + HALF, :LANES], rows[at : at + HALF, LANES:], twiddle_ref[0], -twiddle_ref[1], 0)
        for at in range(0, rows.shape[0], HALF)
    ]
    return dot(back_ref[...], halves(jnp.concatenate(turned, axis=1), 0))


def forward_kernel(
    in_ref, outer_ref, inner_ref, inner_back_ref, back_ref, twiddle_ref, spec_ref, taps_ref, lag_ref, blocks
):
    def load(base):
        return jnp.concatenate(
            [in_ref[pl.ds(base + piece, OWNERS, stride=ROWS_IN), :] for piece in range(PIECES)], axis=0
        )

    def outer(signals):
        first = dot(outer_ref[...], halves(jnp.concatenate(signals, axis=1), 0))
        return [
            turn(first[:HALF, at : at + LANES], first[HALF:, at : at + LANES], twiddle_ref[0], twiddle_ref[1], 1)
            for at in range(0, first.shape[1], LANES)
        ]

    taps = jnp.concatenate(
        [
            in_ref[pl.ds(2 * piece * OWNERS * ROWS_IN + 2 * PIECES, OWNERS, stride=ROWS_IN), :]
            for piece in range(PIECES)
        ],
        axis=0,
    )
    groups = []
    for start in range(0, SEQS, GROUP):
        turned = []
        for seq in range(start, start + GROUP):
            base = seq * OWNERS * ROWS_IN
            turned += outer([load(base), load(base + PIECES)])
        groups.append(turned)
    groups[-1] += outer([taps])
    lag_real = jnp.zeros((HALF, LANES), jnp.float32)
    lag_imag = jnp.zeros((HALF, LANES), jnp.float32)
    spectra = [inner(turned, inner_ref) for turned in groups]
    for number, spec in enumerate(spectra):
        size = 2 * GROUP * HALF
        spec_ref[number * size : (number + 1) * size, :] = spec[:size]
        for index in range(GROUP):
            at = slice(2 * index * HALF, (2 * index + 1) * HALF)
            mixed_real, mixed_imag = spec[at, :LANES], spec[at, LANES:]
            at = slice((2 * index + 1) * HALF, (2 * index + 2) * HALF)
            gated_real, gated_imag = spec[at, :LANES], spec[at, LANES:]
            lag_real = lag_real + (mixed_real * gated_real + mixed_imag * gated_imag)
            lag_imag = lag_imag + (mixed_real * gated_imag - mixed_imag * gated_real)
    taps_ref[...] = spectra[-1][2 * GROUP * HALF :]
    rows = inner([jnp.concatenate([lag_real, lag_imag], axis=1)], inner_back_ref)
    lag = outer_back(rows, twiddle_ref, back_ref)
    for piece in range(PIECES):
        blocks[:, piece, :] = lag[piece * OWNERS : (piece + 1) * OWNERS, :]
    for chip in range(Z_CHIPS):
        for x in range(2):
            for core in range(2):
                owner = lax.bitwise_xor(lax.axis_index("x"), x) * (2 * Z_CHIPS) + chip * 2
                lag_ref[chip * 4 + x * 2 + core] = blocks[owner + lax.bitwise_xor(lax.axis_index("core"), core)]


def inverse_kernel(spec_ref, taps_ref, inner_back_ref, back_ref, twiddle_ref, out_ref):
    taps_real, taps_imag = taps_ref[:, :LANES], taps_ref[:, LANES:]
    groups = []
    for seq in range(SEQS):
        at = pl.ds(2 * seq * HALF, HALF)
        mixed_real, mixed_imag = spec_ref[at, :LANES], spec_ref[at, LANES:]
        at = pl.ds((2 * seq + 1) * HALF, HALF)
        gated_real, gated_imag = spec_ref[at, :LANES], spec_ref[at, LANES:]
        conv = [
            taps_real * mixed_real - taps_imag * mixed_imag,
            taps_real * mixed_imag + taps_imag * mixed_real,
        ]
        back = [
            taps_real * gated_real + taps_imag * gated_imag,
            taps_real * gated_imag - taps_imag * gated_real,
        ]
        groups.append([jnp.concatenate(conv, axis=1), jnp.concatenate(back, axis=1)])
    row_groups = [inner(products, inner_back_ref) for products in groups]
    for seq, rows in enumerate(row_groups):
        result = outer_back(rows, twiddle_ref, back_ref)
        for which in range(2):
            for piece in range(PIECES):
                base = seq * OWNERS * ROWS_OUT + which * PIECES + piece
                out_ref[pl.ds(base, OWNERS, stride=ROWS_OUT), :] = result[
                    piece * OWNERS : (piece + 1) * OWNERS, which * LANES : (which + 1) * LANES
                ]


def post_kernel(c_ref, q_ref, k_ref, v_ref, u_ref, o_hbm, qg_hbm, kg_hbm, vg_hbm, small, sems):
    copies = []
    for piece in range(PIECES):
        at = pl.ds(piece * LANES, LANES)
        conv = c_ref[pl.ds(piece, CHANNELS, stride=ROWS_OUT), :].T
        back = c_ref[pl.ds(PIECES + piece, CHANNELS, stride=ROWS_OUT), :].T
        pieces = (
            (q_ref, conv, o_hbm),
            (u_ref, conv, qg_hbm),
            (v_ref, back, kg_hbm),
            (k_ref, back, vg_hbm),
        )
        for index, (factor, result, target) in enumerate(pieces):
            small[index, at, :] = (factor[0, at, :].astype(jnp.float32) * result).astype(jnp.bfloat16)
            copies.append(
                pltpu.make_async_copy(small.at[index, at, :], target.at[0, at, :], sems.at[index, piece])
            )
            copies[-1].start()
    for copy in copies:
        copy.wait()


def taps_kernel(*refs):
    sources, fg_ref, blocks = refs[:SEQS], refs[SEQS], refs[SEQS + 1]
    x_place, core_place = lax.axis_index("x"), lax.axis_index("core")
    for other, source in enumerate(sources):
        row = lax.bitwise_xor(lax.axis_index("dp"), other) * OWNERS
        for x in range(2):
            for core in range(2):
                first = row + lax.bitwise_xor(x_place, x) * (2 * Z_CHIPS) + lax.bitwise_xor(core_place, core)
                for chip in range(Z_CHIPS):
                    blocks[first + chip * 2] = source[(x * 2 + core) * Z_CHIPS + chip]
    for piece in range(PIECES):
        fg_ref[pl.ds(piece * LANES, LANES), :] = blocks[:, piece, :].T


def params():
    return pltpu.CompilerParams(vmem_limit_bytes=VMEM_LIMIT)


def pre(*arrays):
    arrays = [pltpu.with_memory_space_constraint(array, pltpu.HBM) for array in arrays]
    return pl.pallas_call(
        pre_kernel,
        out_shape=jax.ShapeDtypeStruct((CHANNELS * ROWS_IN, LANES), jnp.float32),
        in_specs=[pl.BlockSpec(memory_space=pltpu.HBM)] * 5,
        out_specs=pl.BlockSpec(memory_space=pltpu.VMEM),
        scratch_shapes=[
            pltpu.VMEM((4, BLOCK, CHANNELS), jnp.bfloat16),
            pltpu.VMEM((LANES, CHANNELS), jnp.float32),
            pltpu.SemaphoreType.DMA((4, PIECES)),
            pltpu.SemaphoreType.DMA,
        ],
        compiler_params=params(),
    )(*arrays)


def forward(arrived, tables):
    return pl.pallas_call(
        forward_kernel,
        out_shape=(
            jax.ShapeDtypeStruct((2 * SEQS * HALF, 2 * LANES), jnp.float32),
            jax.ShapeDtypeStruct((HALF, 2 * LANES), jnp.float32),
            jax.ShapeDtypeStruct((OWNERS, PIECES, LANES), jnp.float32),
        ),
        scratch_shapes=[pltpu.VMEM((OWNERS, PIECES, LANES), jnp.float32)],
        compiler_params=params(),
    )(arrived, *tables)


def inverse(spec, taps_spec, tables):
    return pl.pallas_call(
        inverse_kernel,
        out_shape=jax.ShapeDtypeStruct((SEQS * OWNERS * ROWS_OUT, LANES), jnp.float32),
        cost_estimate=pl.CostEstimate(flops=4 << 30, bytes_accessed=4 << 20, transcendentals=0),
        compiler_params=params(),
    )(spec, taps_spec, *tables[2:])


def post(returned, query_seq, key_seq, value_seq, upstream):
    half = jax.ShapeDtypeStruct((1, BLOCK, CHANNELS), jnp.bfloat16)
    return pl.pallas_call(
        post_kernel,
        out_shape=(half, half, half, half),
        in_specs=[pl.BlockSpec(memory_space=pltpu.VMEM)] * 5,
        out_specs=[pl.BlockSpec(memory_space=pltpu.HBM)] * 4,
        scratch_shapes=[
            pltpu.VMEM((4, BLOCK, CHANNELS), jnp.bfloat16),
            pltpu.SemaphoreType.DMA((4, PIECES)),
        ],
        compiler_params=params(),
    )(returned, query_seq, key_seq, value_seq, upstream)


def taps_grad(sources):
    return pl.pallas_call(
        taps_kernel,
        out_shape=jax.ShapeDtypeStruct((BLOCK, CHANNELS), jnp.float32),
        scratch_shapes=[pltpu.VMEM((CHANNELS, PIECES, LANES), jnp.float32)],
        compiler_params=params(),
    )(*sources)


def exchange(rows, depth):
    shaped = rows.reshape(CHANNELS, depth, 1, LANES)
    moved = lax.all_to_all(shaped, ("dp", "x", "z", "core"), split_axis=0, concat_axis=0, tiled=True)
    return moved.reshape(CHANNELS * depth, LANES)


def swap(value, axis, bits):
    return lax.ppermute(value, axis, [(place, place ^ bits) for place in range(lax.axis_size(axis))])


def spread(columns):
    columns = columns.reshape(Z_CHIPS, 2, 2, PIECES, LANES)
    by_x = jnp.stack([columns[:, 0], swap(columns[:, 1], "x", 1)])
    mine = jnp.stack([by_x[:, :, 0], swap(by_x[:, :, 1], "core", 1)], axis=1)
    mine = mine.reshape(OWNERS, PIECES, LANES)
    return [mine] + [swap(mine, "dp", other) for other in range(1, SEQS)]


def local(query_seq, key_seq, value_seq, upstream, filter_param):
    tables = [jnp.asarray(table) for table in constants()]
    sent = pre(query_seq, key_seq, value_seq, upstream, filter_param)
    arrived = exchange(sent, ROWS_IN)
    spec, taps_spec, lag = forward(arrived, tables)
    columns = lax.all_to_all(lag, "z", split_axis=0, concat_axis=0, tiled=True)
    results = inverse(spec, taps_spec, tables)
    results, columns = lax.optimization_barrier((results, columns))
    returned = exchange(results, ROWS_OUT)
    filter_grad = taps_grad(spread(columns))
    return (*post(returned, query_seq, key_seq, value_seq, upstream), filter_grad)


def solution(mesh):
    placed = jax.sharding.Mesh(mesh.devices.reshape(SEQS, 2, Z_CHIPS, 2), ("dp", "x", "z", "core"))
    whole = P("dp", ("x", "z", "core"), None)
    taps = P(("x", "z", "core"), None)
    return jax.shard_map(
        local,
        mesh=placed,
        in_specs=(whole, whole, whole, whole, taps),
        out_specs=(whole, whole, whole, whole, taps),
        check_vma=False,
    )
```

time: 125 us -> 105 us (0.84); the launches traced: 123 us -> 105 us
  blocking collectives: 0 us -> 49.2 us
  waiting for transfers between devices: 53.4 us -> 19.3 us
  starting transfers between devices: 56.4 us -> 25.7 us
  Pallas kernels: 12.2 us -> 9.67 us
    all_to_all x0 -> x1, blocking collectives: none -> 49.2 us  [exchange(): lax.all_to_all(shaped, ('dp', 'x', 'z', 'core'), split_axis=0, concat_axi...]
    all_to_all x2, waiting for transfers between devices: 33.7 us -> 10.1 us  [the longest x1 5.53 us: exchange(): lax.all_to_all(shaped, ('dp', 'x', 'z', 'core'), split_axis=0, concat_axi...]
    ppermute x16 -> x9, starting transfers between devices: 33.4 us -> 14.9 us  [swap(): lax.ppermute(value, axis, [(place, place ^ bits) for place in range(lax.a...]
    all_to_all x2, starting transfers between devices: 23 us -> 10.8 us  [the longest x1 7.48 us: exchange(): lax.all_to_all(shaped, ('dp', 'x', 'z', 'core'), split_axis=0, concat_axi...]
    ppermute x16 -> x9, waiting for transfers between devices: 19.7 us -> 9.24 us  [swap(): lax.ppermute(value, axis, [(place, place ^ bits) for place in range(lax.a...]
    pallas_call x1 -> x2, Pallas kernels: 6.23 us -> 5.48 us  [the longest x1 2.85 us: forward(): pl.pallas_call(forward_kernel, out_shape=(jax.ShapeDtypeStruct((2 * SEQS...]
  transfers between devices with their start and end apart: 18 -> 11, of which waited for: 9 -> 8; matrix products, arithmetic and copies ran while one was open for 0% -> 0% of each run, Pallas kernels for 2% -> 4%
where the time goes in v10:
time: 105 us
  blocking collectives  49.2 us (47%)
  starting transfers between devices  25.7 us (24%)
  waiting for transfers between devices  19.3 us (18%)
  Pallas kernels  9.67 us (9%)
    all_to_all x1, blocking collectives, exchange(): lax.all_to_all(shaped, ('dp', 'x', 'z', 'core'), split_axis=0, concat_axi...  49.2 us
    ppermute x9, starting transfers between devices, swap(): lax.ppermute(value, axis, [(place, place ^ bits) for place in range(lax.a...  14.9 us
    ppermute x9, waiting for transfers between devices, swap(): lax.ppermute(value, axis, [(place, place ^ bits) for place in range(lax.a...  9.24 us
    all_to_all x1, starting transfers between devices, exchange(): lax.all_to_all(shaped, ('dp', 'x', 'z', 'core'), split_axis=0, concat_axi...  7.48 us
    all_to_all x1, waiting for transfers between devices, exchange(): lax.all_to_all(shaped, ('dp', 'x', 'z', 'core'), split_axis=0, concat_axi...  5.53 us
    all_to_all x1, waiting for transfers between devices, local(): columns = lax.all_to_all(lag, 'z', split_axis=0, concat_axis=0, tiled=True)  4.54 us
    all_to_all x1, starting transfers between devices, local(): columns = lax.all_to_all(lag, 'z', split_axis=0, concat_axis=0, tiled=True)  3.35 us
    pallas_call x1, Pallas kernels, forward(): pl.pallas_call(forward_kernel, out_shape=(jax.ShapeDtypeStruct((2 * SEQS...  2.85 us
  transfers between devices with their start and end apart: 11, of which 8 were waited for; matrix products, arithmetic and copies ran while one was open for 0% of the time, Pallas kernels for 4%

profile of v10, /device:TPU:1, one launch (start us, length us, event | category | flops | bytes accessed | tf_op | source)
XLA Modules:
  0.0 104.8 jit_solution(17422056688950965994)
XLA Ops:
  0.6 1.8 %shard_map.137 = f32[2304,128]{1,0:T(8,128)S(1)} custom-call(bf16[1,512,256]{2,1,0:T(8,128)(2,1)} %q_ref.1, bf16[1,512,256]{2,1,0:T(8,128)(2,1)} %k_ref.1, bf16[1,512,256]{2,1,0:T(8,128)(2,1)} %v_ref.1, bf16[1,512,256]{2,1,0:T(8,128)(2,1)} %u_ref.1, f32[512,256]{1,0:T(8,128)} %f_hbm.1), custom_call_target="tpu_custom_call" | custom-call | tf_op jit(solution)/shard_map/pallas_call | solution.py:236
  2.4 0.0 copy-start.4
  2.4 0.0 copy-start.5
  2.4 0.0 copy-start.6
  2.4 0.0 copy-start.7
  2.4 0.0 copy-start.8
  2.5 49.2 %all_to_all.15 = f32[256,9,1,128]{3,2,1,0:T(1,128)S(1)} all-to-all(f32[256,9,1,128]{3,2,1,0:T(1,128)S(1)} %bitcast.23), channel_id=1, replica_groups=mesh['dp'=8,'x'=2,'z'=8,'core'=2] {'dp','x','z','core'}, dimensions={0} | all-to-all | bytes 2359296 | tf_op jit(solution)/shard_map/all_to_all | solution.py:299
  51.6 0.0 copy-done.4
  51.7 0.0 copy-done.5
  51.7 0.0 copy-done.6
  51.7 0.0 copy-done.7
  51.7 0.0 copy-done.8
  51.7 2.8 %shard_map.138 = (f32[2048,256]{1,0:T(8,128)S(1)}, f32[128,256]{1,0:T(8,128)S(1)}, f32[32,4,128]{2,1,0:T(4,128)}) custom-call(f32[2304,128]{1,0:T(8,128)S(1)} %bitcast.22, bf16[256,384]{1,0:T(8,128)(2,1)S(1)} %copy-done.7, bf16[768,256]{1,0:T(8,128)(2,1)S(1)} %copy-done.5, bf16[768,256]{1,0:T(8,128)(2,1)S(1)} %copy-done.4, bf16[128,768]{1,0:T(8,128)(2,1)S(1)} %copy-done.6, ...), custom_call_target="tpu_custom_call" | custom-call | tf_op jit(solution)/shard_map/pallas_call | solution.py:252
  54.5 3.4 %all-to-all-start.1 = ((f32[32,4,128]{2,1,0:T(4,128)}), f32[32,4,128]{2,1,0:T(4,128)S(1)}, u32[]{:S(2)}, u32[]{:S(2)}) async-start(f32[32,4,128]{2,1,0:T(4,128)} %get-tuple-element.16), calls=%async_computation.1 | async-start | bytes 131072 | tf_op jit(solution)/shard_map/all_to_all | solution.py:320
  57.9 2.6 %shard_map.139 = f32[2048,128]{1,0:T(8,128)} custom-call(f32[2048,256]{1,0:T(8,128)S(1)} %get-tuple-element.14.spec_ref, f32[128,256]{1,0:T(8,128)S(1)} %get-tuple-element.15.taps_ref, bf16[768,256]{1,0:T(8,128)(2,1)S(1)} %copy-done.4, bf16[128,768]{1,0:T(8,128)(2,1)S(1)} %copy-done.6, f32[2,128,128]{2,1,0:T(8,128)S(1)} %copy-done.8), custom_call_target="tpu_custom_call" | custom-call | flops 4294967296 | bytes 4194304 | tf_op jit(solution)/shard_map/pallas_call | solution.py:265
  60.5 4.5 %all-to-all-done.1 = f32[32,4,128]{2,1,0:T(4,128)S(1)} async-done(((f32[32,4,128]{2,1,0:T(4,128)}), f32[32,4,128]{2,1,0:T(4,128)S(1)}, u32[]{:S(2)}, u32[]{:S(2)}) %all-to-all-start.1) | async-done | bytes 65568 | tf_op jit(solution)/shard_map/all_to_all | solution.py:320
  65.1 7.5 %all-to-all-start.2 = ((f32[256,8,1,128]{3,1,2,0:T(8,128)}), f32[256,8,1,128]{3,1,2,0:T(8,128)S(1)}, u32[]{:S(2)}, u32[]{:S(2)}) async-start(f32[256,8,1,128]{3,1,2,0:T(8,128)} %bitcast.3), calls=%async_computation.2 | async-start | bytes 2097152 | tf_op jit(solution)/shard_map/all_to_all | solution.py:299
  72.5 0.0 copy-start
  72.6 0.0 copy-start.1
  72.6 0.0 copy-start.2
  72.6 0.0 copy-start.3
  72.6 1.5 %collective-permute-start = (f32[8,2,4,128]{3,2,0,1:T(4,128)S(1)}, f32[8,2,4,128]{3,2,0,1:T(4,128)S(1)}, u32[]{:S(2)}, u32[]{:S(2)}) collective-permute-start(f32[8,2,4,128]{3,2,0,1:T(4,128)S(1)} %bitcast.35), channel_id=1, source_target_pairs={{0,16},{16,0},{1,17},{17,1},{2,18},{18,2},{3,19},{19,3},{4,20},{20... | collective-permute-start | bytes 98312 | tf_op jit(solution)/shard_map/ppermute | solution.py:304
  74.1 1.9 %collective-permute-done = f32[8,2,4,128]{3,2,0,1:T(4,128)S(1)} collective-permute-done((f32[8,2,4,128]{3,2,0,1:T(4,128)S(1)}, f32[8,2,4,128]{3,2,0,1:T(4,128)S(1)}, u32[]{:S(2)}, u32[]{:S(2)}) %collective-permute-start) | collective-permute-done | bytes 32800 | tf_op jit(solution)/shard_map/ppermute | solution.py:304
  76.1 3.2 %collective-permute-start.1 = (f32[2,8,4,128]{3,2,1,0:T(4,128)S(1)}, f32[2,8,4,128]{3,2,1,0:T(4,128)S(1)}, u32[]{:S(2)}, u32[]{:S(2)}) collective-permute-start(f32[2,8,4,128]{3,2,1,0:T(4,128)S(1)} %get-tuple-element.24), channel_id=1, source_target_pairs={{0,1},{1,0},{2,3},{3,2},{4,5},{5,4},{6,7},{7,6},{8,9},{9,8},{10,11... | collective-permute-start | bytes 98312 | tf_op jit(solution)/shard_map/ppermute | solution.py:304
  79.3 0.9 collective-permute-done.1
  80.1 3.2 %collective-permute-start.8 = (f32[32,4,128]{2,1,0:T(4,128)S(1)}, f32[32,4,128]{2,1,0:T(4,128)S(1)}, u32[]{:S(2)}, u32[]{:S(2)}) collective-permute-start(f32[32,4,128]{2,1,0:T(4,128)S(1)} %bitcast.25), channel_id=1, source_target_pairs={{0,224},{32,192},{64,160},{96,128},{128,96},{160,64},{192,32},{224... | collective-permute-start | bytes 196616 | tf_op jit(solution)/shard_map/ppermute | solution.py:304
  83.4 0.4 collective-permute-start.7
  83.8 2.6 %collective-permute-start.6 = (f32[32,4,128]{2,1,0:T(4,128)S(1)}, f32[32,4,128]{2,1,0:T(4,128)S(1)}, u32[]{:S(2)}, u32[]{:S(2)}) collective-permute-start(f32[32,4,128]{2,1,0:T(4,128)S(1)} %bitcast.27), channel_id=1, source_target_pairs={{0,160},{32,128},{64,224},{96,192},{128,32},{160,0},{192,96},{224,... | collective-permute-start | bytes 196616 | tf_op jit(solution)/shard_map/ppermute | solution.py:304
  86.4 2.2 %collective-permute-start.5 = (f32[32,4,128]{2,1,0:T(4,128)S(1)}, f32[32,4,128]{2,1,0:T(4,128)S(1)}, u32[]{:S(2)}, u32[]{:S(2)}) collective-permute-start(f32[32,4,128]{2,1,0:T(4,128)S(1)} %bitcast.28), channel_id=1, source_target_pairs={{0,128},{32,160},{64,192},{96,224},{128,0},{160,32},{192,64},{224,... | collective-permute-start | bytes 196616 | tf_op jit(solution)/shard_map/ppermute | solution.py:304
  88.6 0.7 collective-permute-start.4
  89.3 0.0 collective-permute-done.8.refs_7_
  89.3 0.5 collective-permute-start.3
  89.8 1.5 %collective-permute-done.7.refs_6_ = f32[32,4,128]{2,1,0:T(4,128)S(1)} collective-permute-done((f32[32,4,128]{2,1,0:T(4,128)S(1)}, f32[32,4,128]{2,1,0:T(4,128)S(1)}, u32[]{:S(2)}, u32[]{:S(2)}) %collective-permute-start.7) | collective-permute-done | bytes 65568 | tf_op jit(solution)/shard_map/ppermute | solution.py:304
  91.3 0.6 collective-permute-start.2
  91.8 0.0 collective-permute-done.6.refs_5_
  91.8 2.0 %collective-permute-done.5.refs_4_ = f32[32,4,128]{2,1,0:T(4,128)S(1)} collective-permute-done((f32[32,4,128]{2,1,0:T(4,128)S(1)}, f32[32,4,128]{2,1,0:T(4,128)S(1)}, u32[]{:S(2)}, u32[]{:S(2)}) %collective-permute-start.5) | collective-permute-done | bytes 65568 | tf_op jit(solution)/shard_map/ppermute | solution.py:304
  93.9 0.3 collective-permute-done.4.refs_3_
  94.2 2.6 %collective-permute-done.3.refs_2_ = f32[32,4,128]{2,1,0:T(4,128)S(1)} collective-permute-done((f32[32,4,128]{2,1,0:T(4,128)S(1)}, f32[32,4,128]{2,1,0:T(4,128)S(1)}, u32[]{:S(2)}, u32[]{:S(2)}) %collective-permute-start.3) | collective-permute-done | bytes 65568 | tf_op jit(solution)/shard_map/ppermute | solution.py:304
  96.8 0.0 collective-permute-done.2.refs_1_
  96.8 1.2 %shard_map.141 = f32[512,256]{1,0:T(8,128)} custom-call(f32[32,4,128]{2,1,0:T(4,128)S(1)} %bitcast.32, f32[32,4,128]{2,1,0:T(4,128)S(1)} %collective-permute-done.2.refs_1_, f32[32,4,128]{2,1,0:T(4,128)S(1)} %collective-permute-done.3.refs_2_, f32[32,4,128]{2,1,0:T(4,128)S(1)} %collective-permute-done.4.refs_3_, ...), custom_call_target="tpu_custom_call" | custom-call | tf_op jit(solution)/shard_map/pallas_call | solution.py:289
  98.0 5.5 %all-to-all-done.2 = f32[256,8,1,128]{3,1,2,0:T(8,128)S(1)} async-done(((f32[256,8,1,128]{3,1,2,0:T(8,128)}), f32[256,8,1,128]{3,1,2,0:T(8,128)S(1)}, u32[]{:S(2)}, u32[]{:S(2)}) %all-to-all-start.2) | async-done | bytes 1048608 | tf_op jit(solution)/shard_map/all_to_all | solution.py:299
  103.6 0.0 copy-done
  103.6 0.0 copy-done.1
  103.6 0.0 copy-done.2
  103.6 0.0 copy-done.3
  103.6 1.2 %shard_map.140 = (bf16[1,512,256]{2,1,0:T(8,128)(2,1)}, bf16[1,512,256]{2,1,0:T(8,128)(2,1)}, bf16[1,512,256]{2,1,0:T(8,128)(2,1)}, bf16[1,512,256]{2,1,0:T(8,128)(2,1)}) custom-call(f32[2048,128]{1,0:T(8,128)S(1)} %bitcast.24, bf16[1,512,256]{2,1,0:T(8,128)(2,1)S(1)} %copy-done, bf16[1,512,256]{2,1,0:T(8,128)(2,1)S(1)} %copy-done.1, ...), custom_call_target="tpu_custom_call" | custom-call | tf_op jit(solution)/shard_map/pallas_call | solution.py:275
  (5 shorter events, 0.1 us)
Async XLA Ops:
  2.4 49.3 %copy-start.4 = (bf16[768,256]{1,0:T(8,128)(2,1)S(1)}, bf16[768,256]{1,0:T(8,128)(2,1)}, u32[]{:S(2)}) copy-start(bf16[768,256]{1,0:T(8,128)(2,1)} %constant.12.clone.inner_back_ref) | copy-start | bytes 1179652
  2.4 49.3 %copy-start.5 = (bf16[768,256]{1,0:T(8,128)(2,1)S(1)}, bf16[768,256]{1,0:T(8,128)(2,1)}, u32[]{:S(2)}) copy-start(bf16[768,256]{1,0:T(8,128)(2,1)} %constant.11.clone.inner_ref) | copy-start | bytes 1179652
  2.4 49.2 %copy-start.6 = (bf16[128,768]{1,0:T(8,128)(2,1)S(1)}, bf16[128,768]{1,0:T(8,128)(2,1)}, u32[]{:S(2)}) copy-start(bf16[128,768]{1,0:T(8,128)(2,1)} %constant.13.clone.back_ref) | copy-start | bytes 589828
  2.4 49.2 %copy-start.7 = (bf16[256,384]{1,0:T(8,128)(2,1)S(1)}, bf16[256,384]{1,0:T(8,128)(2,1)}, u32[]{:S(2)}) copy-start(bf16[256,384]{1,0:T(8,128)(2,1)} %constant.10.clone.outer_ref) | copy-start | bytes 589828
  2.4 49.2 %copy-start.8 = (f32[2,128,128]{2,1,0:T(8,128)S(1)}, f32[2,128,128]{2,1,0:T(8,128)}, u32[]{:S(2)}) copy-start(f32[2,128,128]{2,1,0:T(8,128)} %constant.14.clone.twiddle_ref) | copy-start | bytes 393220
  54.5 10.5 %all-to-all-start.1 = ((f32[32,4,128]{2,1,0:T(4,128)}), f32[32,4,128]{2,1,0:T(4,128)S(1)}, u32[]{:S(2)}, u32[]{:S(2)}) async-start(f32[32,4,128]{2,1,0:T(4,128)} %get-tuple-element.16), calls=%async_computation.1 | async-start | bytes 131072 | tf_op jit(solution)/shard_map/all_to_all | solution.py:320
  65.1 38.5 %all-to-all-start.2 = ((f32[256,8,1,128]{3,1,2,0:T(8,128)}), f32[256,8,1,128]{3,1,2,0:T(8,128)S(1)}, u32[]{:S(2)}, u32[]{:S(2)}) async-start(f32[256,8,1,128]{3,1,2,0:T(8,128)} %bitcast.3), calls=%async_computation.2 | async-start | bytes 2097152 | tf_op jit(solution)/shard_map/all_to_all | solution.py:299
  72.5 31.0 %copy-start = (bf16[1,512,256]{2,1,0:T(8,128)(2,1)S(1)}, bf16[1,512,256]{2,1,0:T(8,128)(2,1)}, u32[]{:S(2)}) copy-start(bf16[1,512,256]{2,1,0:T(8,128)(2,1)} %q_ref.1) | copy-start | bytes 786436
  72.6 31.0 %copy-start.1 = (bf16[1,512,256]{2,1,0:T(8,128)(2,1)S(1)}, bf16[1,512,256]{2,1,0:T(8,128)(2,1)}, u32[]{:S(2)}) copy-start(bf16[1,512,256]{2,1,0:T(8,128)(2,1)} %k_ref.1) | copy-start | bytes 786436
  72.6 31.0 %copy-start.2 = (bf16[1,512,256]{2,1,0:T(8,128)(2,1)S(1)}, bf16[1,512,256]{2,1,0:T(8,128)(2,1)}, u32[]{:S(2)}) copy-start(bf16[1,512,256]{2,1,0:T(8,128)(2,1)} %v_ref.1) | copy-start | bytes 786436
  72.6 31.0 %copy-start.3 = (bf16[1,512,256]{2,1,0:T(8,128)(2,1)S(1)}, bf16[1,512,256]{2,1,0:T(8,128)(2,1)}, u32[]{:S(2)}) copy-start(bf16[1,512,256]{2,1,0:T(8,128)(2,1)} %u_ref.1) | copy-start | bytes 786436
  72.6 3.4 %collective-permute-start = (f32[8,2,4,128]{3,2,0,1:T(4,128)S(1)}, f32[8,2,4,128]{3,2,0,1:T(4,128)S(1)}, u32[]{:S(2)}, u32[]{:S(2)}) collective-permute-start(f32[8,2,4,128]{3,2,0,1:T(4,128)S(1)} %bitcast.35), channel_id=1, source_target_pairs={{0,16},{16,0},{1,17},{17,1},{2,18},{18,2},{3,19},{19,3},{4,20},{20... | collective-permute-start | bytes 98312 | tf_op jit(solution)/shard_map/ppermute | solution.py:304
  76.1 4.1 %collective-permute-start.1 = (f32[2,8,4,128]{3,2,1,0:T(4,128)S(1)}, f32[2,8,4,128]{3,2,1,0:T(4,128)S(1)}, u32[]{:S(2)}, u32[]{:S(2)}) collective-permute-start(f32[2,8,4,128]{3,2,1,0:T(4,128)S(1)} %get-tuple-element.24), channel_id=1, source_target_pairs={{0,1},{1,0},{2,3},{3,2},{4,5},{5,4},{6,7},{7,6},{8,9},{9,8},{10,11... | collective-permute-start | bytes 98312 | tf_op jit(solution)/shard_map/ppermute | solution.py:304
  80.1 9.1 %collective-permute-start.8 = (f32[32,4,128]{2,1,0:T(4,128)S(1)}, f32[32,4,128]{2,1,0:T(4,128)S(1)}, u32[]{:S(2)}, u32[]{:S(2)}) collective-permute-start(f32[32,4,128]{2,1,0:T(4,128)S(1)} %bitcast.25), channel_id=1, source_target_pairs={{0,224},{32,192},{64,160},{96,128},{128,96},{160,64},{192,32},{224... | collective-permute-start | bytes 196616 | tf_op jit(solution)/shard_map/ppermute | solution.py:304
  83.4 7.9 %collective-permute-start.7 = (f32[32,4,128]{2,1,0:T(4,128)S(1)}, f32[32,4,128]{2,1,0:T(4,128)S(1)}, u32[]{:S(2)}, u32[]{:S(2)}) collective-permute-start(f32[32,4,128]{2,1,0:T(4,128)S(1)} %bitcast.26), channel_id=1, source_target_pairs={{0,192},{32,224},{64,128},{96,160},{128,64},{160,96},{192,0},{224,... | collective-permute-start | bytes 196616 | tf_op jit(solution)/shard_map/ppermute | solution.py:304
  83.8 8.0 %collective-permute-start.6 = (f32[32,4,128]{2,1,0:T(4,128)S(1)}, f32[32,4,128]{2,1,0:T(4,128)S(1)}, u32[]{:S(2)}, u32[]{:S(2)}) collective-permute-start(f32[32,4,128]{2,1,0:T(4,128)S(1)} %bitcast.27), channel_id=1, source_target_pairs={{0,160},{32,128},{64,224},{96,192},{128,32},{160,0},{192,96},{224,... | collective-permute-start | bytes 196616 | tf_op jit(solution)/shard_map/ppermute | solution.py:304
  86.4 7.5 %collective-permute-start.5 = (f32[32,4,128]{2,1,0:T(4,128)S(1)}, f32[32,4,128]{2,1,0:T(4,128)S(1)}, u32[]{:S(2)}, u32[]{:S(2)}) collective-permute-start(f32[32,4,128]{2,1,0:T(4,128)S(1)} %bitcast.28), channel_id=1, source_target_pairs={{0,128},{32,160},{64,192},{96,224},{128,0},{160,32},{192,64},{224,... | collective-permute-start | bytes 196616 | tf_op jit(solution)/shard_map/ppermute | solution.py:304
  88.6 5.6 %collective-permute-start.4 = (f32[32,4,128]{2,1,0:T(4,128)S(1)}, f32[32,4,128]{2,1,0:T(4,128)S(1)}, u32[]{:S(2)}, u32[]{:S(2)}) collective-permute-start(f32[32,4,128]{2,1,0:T(4,128)S(1)} %bitcast.29), channel_id=1, source_target_pairs={{0,96},{32,64},{64,32},{96,0},{128,224},{160,192},{192,160},{224,1... | collective-permute-start | bytes 196616 | tf_op jit(solution)/shard_map/ppermute | solution.py:304
  89.3 7.5 %collective-permute-start.3 = (f32[32,4,128]{2,1,0:T(4,128)S(1)}, f32[32,4,128]{2,1,0:T(4,128)S(1)}, u32[]{:S(2)}, u32[]{:S(2)}) collective-permute-start(f32[32,4,128]{2,1,0:T(4,128)S(1)} %bitcast.30), channel_id=1, source_target_pairs={{0,64},{32,96},{64,0},{96,32},{128,192},{160,224},{192,128},{224,1... | collective-permute-start | bytes 196616 | tf_op jit(solution)/shard_map/ppermute | solution.py:304
  91.3 5.5 %collective-permute-start.2 = (f32[32,4,128]{2,1,0:T(4,128)S(1)}, f32[32,4,128]{2,1,0:T(4,128)S(1)}, u32[]{:S(2)}, u32[]{:S(2)}) collective-permute-start(f32[32,4,128]{2,1,0:T(4,128)S(1)} %bitcast.31), channel_id=1, source_target_pairs={{0,32},{32,0},{64,96},{96,64},{128,160},{160,128},{192,224},{224,1... | collective-permute-start | bytes 196616 | tf_op jit(solution)/shard_map/ppermute | solution.py:304

commit v11 on v10

--- a/solution.py
+++ b/solution.py
@@ -156,11 +156,14 @@
     lag = outer_back(rows, twiddle_ref, back_ref)
     for piece in range(PIECES):
         blocks[:, piece, :] = lag[piece * OWNERS : (piece + 1) * OWNERS, :]
-    for chip in range(Z_CHIPS):
-        for x in range(2):
-            for core in range(2):
-                owner = lax.bitwise_xor(lax.axis_index("x"), x) * (2 * Z_CHIPS) + chip * 2
-                lag_ref[chip * 4 + x * 2 + core] = blocks[owner + lax.bitwise_xor(lax.axis_index("core"), core)]
+    for low in range(2):
+        for high in range(Z_CHIPS // 2):
+            for x in range(2):
+                for core in range(2):
+                    owner = lax.bitwise_xor(lax.axis_index("x"), x) * (2 * Z_CHIPS) + high * 4
+                    owner = owner + lax.bitwise_xor(lax.axis_index("z_low"), low) * 2
+                    owner = owner + lax.bitwise_xor(lax.axis_index("core"), core)
+                    lag_ref[low * (OWNERS // 2) + high * 4 + x * 2 + core] = blocks[owner]
 
 
 def inverse_kernel(spec_ref, taps_ref, inner_back_ref, back_ref, twiddle_ref, out_ref):
@@ -221,8 +224,10 @@
         for x in range(2):
             for core in range(2):
                 first = row + lax.bitwise_xor(x_place, x) * (2 * Z_CHIPS) + lax.bitwise_xor(core_place, core)
-                for chip in range(Z_CHIPS):
-                    blocks[first + chip * 2] = source[(x * 2 + core) * Z_CHIPS + chip]
+                for high in range(Z_CHIPS // 2):
+                    for low in range(2):
+                        chip = high * 2 + lax.bitwise_xor(lax.axis_index("z_low"), low)
+                        blocks[first + chip * 2] = source[(x * 2 + core) * Z_CHIPS + high * 2 + low]
     for piece in range(PIECES):
         fg_ref[pl.ds(piece * LANES, LANES), :] = blocks[:, piece, :].T
 
@@ -296,7 +301,7 @@
 
 def exchange(rows, depth):
     shaped = rows.reshape(CHANNELS, depth, 1, LANES)
-    moved = lax.all_to_all(shaped, ("dp", "x", "z", "core"), split_axis=0, concat_axis=0, tiled=True)
+    moved = lax.all_to_all(shaped, ("dp", "x", "z_high", "z_low", "core"), split_axis=0, concat_axis=0, tiled=True)
     return moved.reshape(CHANNELS * depth, LANES)
 
 
@@ -304,10 +309,16 @@
     return lax.ppermute(value, axis, [(place, place ^ bits) for place in range(lax.axis_size(axis))])
 
 
+def along_z(lag):
+    pair = lag.reshape(2, Z_CHIPS // 2, 4, PIECES, LANES)
+    pair = jnp.stack([pair[0], swap(pair[1], "z_low", 1)], axis=1)
+    return lax.all_to_all(pair, "z_high", split_axis=0, concat_axis=0, tiled=True)
+
+
 def spread(columns):
-    columns = columns.reshape(Z_CHIPS, 2, 2, PIECES, LANES)
-    by_x = jnp.stack([columns[:, 0], swap(columns[:, 1], "x", 1)])
-    mine = jnp.stack([by_x[:, :, 0], swap(by_x[:, :, 1], "core", 1)], axis=1)
+    columns = columns.reshape(Z_CHIPS // 2, 2, 2, 2, PIECES, LANES)
+    by_x = jnp.stack([columns[:, :, 0], swap(columns[:, :, 1], "x", 1)])
+    mine = jnp.stack([by_x[:, :, :, 0], swap(by_x[:, :, :, 1], "core", 1)], axis=1)
     mine = mine.reshape(OWNERS, PIECES, LANES)
     return [mine] + [swap(mine, "dp", other) for other in range(1, SEQS)]
 
@@ -317,7 +328,7 @@
     sent = pre(query_seq, key_seq, value_seq, upstream, filter_param)
     arrived = exchange(sent, ROWS_IN)
     spec, taps_spec, lag = forward(arrived, tables)
-    columns = lax.all_to_all(lag, "z", split_axis=0, concat_axis=0, tiled=True)
+    columns = along_z(lag)
     results = inverse(spec, taps_spec, tables)
     results, columns = lax.optimization_barrier((results, columns))
     returned = exchange(results, ROWS_OUT)
@@ -326,9 +337,10 @@
 
 
 def solution(mesh):
-    placed = jax.sharding.Mesh(mesh.devices.reshape(SEQS, 2, Z_CHIPS, 2), ("dp", "x", "z", "core"))
-    whole = P("dp", ("x", "z", "core"), None)
-    taps = P(("x", "z", "core"), None)
+    names = ("dp", "x", "z_high", "z_low", "core")
+    placed = jax.sharding.Mesh(mesh.devices.reshape(SEQS, 2, Z_CHIPS // 2, 2, 2), names)
+    whole = P("dp", names[1:], None)
+    taps = P(names[1:], None)
     return jax.shard_map(
         local,
         mesh=placed,

time: 105 us -> 109 us (1.038)
  starting transfers between devices: 25.7 us -> 27.6 us
  waiting for transfers between devices: 19.3 us -> 21.1 us
    ppermute x9 -> x10, waiting for transfers between devices: 9.24 us -> 11.3 us  [swap(): lax.ppermute(value, axis, [(place, place ^ bits) for place in range(lax.a...]
    all_to_all x2, starting transfers between devices: 10.8 us -> 12 us  [the longest x1 8.72 us: exchange(): lax.all_to_all(shaped, ('dp', 'x', 'z_high', 'z_low', 'core'), split_axis...]
    ppermute x9 -> x10, starting transfers between devices: 14.9 us -> 15.6 us  [swap(): lax.ppermute(value, axis, [(place, place ^ bits) for place in range(lax.a...]
  transfers between devices with their start and end apart: 11 -> 12, of which waited for: 8 -> 9; matrix products, arithmetic and copies ran while one was open for 0% -> 0% of each run, Pallas kernels for 4% -> 4%
where the time goes in v11:
time: 109 us
  blocking collectives  49.2 us (45%)
  starting transfers between devices  27.6 us (25%)
  waiting for transfers between devices  21.1 us (19%)
  Pallas kernels  9.1 us (8%)
    all_to_all x1, blocking collectives, exchange(): lax.all_to_all(shaped, ('dp', 'x', 'z_high', 'z_low', 'core'), split_axis...  49.2 us
    ppermute x10, starting transfers between devices, swap(): lax.ppermute(value, axis, [(place, place ^ bits) for place in range(lax.a...  15.6 us
    ppermute x10, waiting for transfers between devices, swap(): lax.ppermute(value, axis, [(place, place ^ bits) for place in range(lax.a...  11.3 us
    all_to_all x1, starting transfers between devices, exchange(): lax.all_to_all(shaped, ('dp', 'x', 'z_high', 'z_low', 'core'), split_axis...  8.72 us
    all_to_all x1, waiting for transfers between devices, exchange(): lax.all_to_all(shaped, ('dp', 'x', 'z_high', 'z_low', 'core'), split_axis...  5.48 us
    all_to_all x1, waiting for transfers between devices, along_z(): lax.all_to_all(pair, 'z_high', split_axis=0, concat_axis=0, tiled=True)  4.31 us
    all_to_all x1, starting transfers between devices, along_z(): lax.all_to_all(pair, 'z_high', split_axis=0, concat_axis=0, tiled=True)  3.29 us
    pallas_call x1, Pallas kernels, inverse(): pl.pallas_call(inverse_kernel, out_shape=jax.ShapeDtypeStruct((SEQS * OWN...  2.64 us
  transfers between devices with their start and end apart: 12, of which 9 were waited for; matrix products, arithmetic and copies ran while one was open for 0% of the time, Pallas kernels for 4%

profile of v11, /device:TPU:1, one launch (start us, length us, event | category | flops | bytes accessed | tf_op | source)
XLA Modules:
  0.0 108.6 jit_solution(16543986739145559265)
XLA Ops:
  0.6 1.8 %shard_map.137 = f32[2304,128]{1,0:T(8,128)S(1)} custom-call(bf16[1,512,256]{2,1,0:T(8,128)(2,1)} %q_ref.1, bf16[1,512,256]{2,1,0:T(8,128)(2,1)} %k_ref.1, bf16[1,512,256]{2,1,0:T(8,128)(2,1)} %v_ref.1, bf16[1,512,256]{2,1,0:T(8,128)(2,1)} %u_ref.1, f32[512,256]{1,0:T(8,128)} %f_hbm.1), custom_call_target="tpu_custom_call" | custom-call | tf_op jit(solution)/shard_map/pallas_call | solution.py:241
  2.4 0.0 copy-start.4
  2.4 0.0 copy-start.5
  2.4 0.0 copy-start.6
  2.4 0.0 copy-start.7
  2.4 0.0 copy-start.8
  2.5 49.2 %all_to_all.15 = f32[256,9,1,128]{3,2,1,0:T(1,128)S(1)} all-to-all(f32[256,9,1,128]{3,2,1,0:T(1,128)S(1)} %bitcast.28), channel_id=1, replica_groups=mesh['dp'=8,'x'=2,'z_high'=4,'z_low'=2,'core'=2] {'dp','x','z_high','z_l..., dimensions={0} | all-to-all | bytes 2359296 | tf_op jit(solution)/shard_map/all_to_all | solution.py:304
  51.6 0.0 copy-done.4
  51.7 0.0 copy-done.5
  51.7 0.0 copy-done.6
  51.7 0.0 copy-done.7
  51.7 0.0 copy-done.8
  51.7 2.2 %shard_map.138 = (f32[2048,256]{1,0:T(8,128)S(1)}, f32[128,256]{1,0:T(8,128)S(1)}, f32[32,4,128]{2,1,0:T(4,128)S(1)}) custom-call(f32[2304,128]{1,0:T(8,128)S(1)} %bitcast.27, bf16[256,384]{1,0:T(8,128)(2,1)S(1)} %copy-done.7, bf16[768,256]{1,0:T(8,128)(2,1)S(1)} %copy-done.5, bf16[768,256]{1,0:T(8,128)(2,1)S(1)} %copy-done.4, ...), custom_call_target="tpu_custom_call" | custom-call | tf_op jit(solution)/shard_map/pallas_call | solution.py:257
  53.9 0.8 collective-permute-start
  54.7 2.1 %collective-permute-done = f32[4,4,4,128]{3,2,1,0:T(4,128)S(1)} collective-permute-done((f32[4,4,4,128]{3,2,1,0:T(4,128)S(1)}, f32[4,4,4,128]{3,2,1,0:T(4,128)S(1)}, u32[]{:S(2)}, u32[]{:S(2)}) %collective-permute-start) | collective-permute-done | bytes 32800 | tf_op jit(solution)/shard_map/ppermute | solution.py:309
  56.8 0.6 pad_maximum_fusion
  57.4 3.3 %all-to-all-start.1 = ((f32[4,2,4,4,128]{4,3,2,1,0:T(4,128)}), f32[4,2,4,4,128]{4,3,2,1,0:T(4,128)S(1)}, u32[]{:S(2)}, u32[]{:S(2)}) async-start(f32[4,2,4,4,128]{4,3,2,1,0:T(4,128)} %pad_maximum_fusion), calls=%async_computation.1 | async-start | bytes 131072 | tf_op jit(solution)/shard_map/all_to_all | solution.py:315
  60.7 2.6 %shard_map.139 = f32[2048,128]{1,0:T(8,128)} custom-call(f32[2048,256]{1,0:T(8,128)S(1)} %get-tuple-element.14.spec_ref, f32[128,256]{1,0:T(8,128)S(1)} %get-tuple-element.15.taps_ref, bf16[768,256]{1,0:T(8,128)(2,1)S(1)} %copy-done.4, bf16[128,768]{1,0:T(8,128)(2,1)S(1)} %copy-done.6, f32[2,128,128]{2,1,0:T(8,128)S(1)} %copy-done.8), custom_call_target="tpu_custom_call" | custom-call | flops 4294967296 | bytes 4194304 | tf_op jit(solution)/shard_map/pallas_call | solution.py:270
  63.4 4.3 %all-to-all-done.1 = f32[4,2,4,4,128]{4,3,2,1,0:T(4,128)S(1)} async-done(((f32[4,2,4,4,128]{4,3,2,1,0:T(4,128)}), f32[4,2,4,4,128]{4,3,2,1,0:T(4,128)S(1)}, u32[]{:S(2)}, u32[]{:S(2)}) %all-to-all-start.1) | async-done | bytes 65568 | tf_op jit(solution)/shard_map/all_to_all | solution.py:315
  67.7 8.7 %all-to-all-start.2 = ((f32[256,8,1,128]{3,1,2,0:T(8,128)}), f32[256,8,1,128]{3,1,2,0:T(8,128)S(1)}, u32[]{:S(2)}, u32[]{:S(2)}) async-start(f32[256,8,1,128]{3,1,2,0:T(8,128)} %bitcast.7), calls=%async_computation.2 | async-start | bytes 2097152 | tf_op jit(solution)/shard_map/all_to_all | solution.py:304
  76.4 0.0 copy-start
  76.4 0.0 copy-start.1
  76.4 0.0 copy-start.2
  76.4 0.0 copy-start.3
  76.5 1.5 %collective-permute-start.1 = (f32[4,2,2,4,128]{4,3,1,0,2:T(4,128)S(1)}, f32[4,2,2,4,128]{4,3,1,0,2:T(4,128)S(1)}, u32[]{:S(2)}, u32[]{:S(2)}) collective-permute-start(f32[4,2,2,4,128]{4,3,1,0,2:T(4,128)S(1)} %bitcast.41), channel_id=1, source_target_pairs={{0,16},{16,0},{1,17},{17,1},{2,18},{18,2},{3,19},{19,3},{4,20},{20... | collective-permute-start | bytes 98312 | tf_op jit(solution)/shard_map/ppermute | solution.py:309
  78.0 1.9 %collective-permute-done.1 = f32[4,2,2,4,128]{4,3,1,0,2:T(4,128)S(1)} collective-permute-done((f32[4,2,2,4,128]{4,3,1,0,2:T(4,128)S(1)}, f32[4,2,2,4,128]{4,3,1,0,2:T(4,128)S(1)}, u32[]{:S(2)}, u32[]{:S(2)}) %collective-permute-start.1) | collective-permute-done | bytes 32800 | tf_op jit(solution)/shard_map/ppermute | solution.py:309
  79.9 3.2 %collective-permute-start.2 = (f32[2,4,2,4,128]{4,3,2,1,0:T(4,128)S(1)}, f32[2,4,2,4,128]{4,3,2,1,0:T(4,128)S(1)}, u32[]{:S(2)}, u32[]{:S(2)}) collective-permute-start(f32[2,4,2,4,128]{4,3,2,1,0:T(4,128)S(1)} %get-tuple-element.24), channel_id=1, source_target_pairs={{0,1},{1,0},{2,3},{3,2},{4,5},{5,4},{6,7},{7,6},{8,9},{9,8},{10,11... | collective-permute-start | bytes 98312 | tf_op jit(solution)/shard_map/ppermute | solution.py:309
  83.1 0.9 collective-permute-done.2
  84.0 3.2 %collective-permute-start.9 = (f32[32,4,128]{2,1,0:T(4,128)S(1)}, f32[32,4,128]{2,1,0:T(4,128)S(1)}, u32[]{:S(2)}, u32[]{:S(2)}) collective-permute-start(f32[32,4,128]{2,1,0:T(4,128)S(1)} %bitcast.30), channel_id=1, source_target_pairs={{0,224},{32,192},{64,160},{96,128},{128,96},{160,64},{192,32},{224... | collective-permute-start | bytes 196616 | tf_op jit(solution)/shard_map/ppermute | solution.py:309
  87.2 0.4 collective-permute-start.8
  87.7 2.6 %collective-permute-start.7 = (f32[32,4,128]{2,1,0:T(4,128)S(1)}, f32[32,4,128]{2,1,0:T(4,128)S(1)}, u32[]{:S(2)}, u32[]{:S(2)}) collective-permute-start(f32[32,4,128]{2,1,0:T(4,128)S(1)} %bitcast.32), channel_id=1, source_target_pairs={{0,160},{32,128},{64,224},{96,192},{128,32},{160,0},{192,96},{224,... | collective-permute-start | bytes 196616 | tf_op jit(solution)/shard_map/ppermute | solution.py:309
  90.2 2.2 %collective-permute-start.6 = (f32[32,4,128]{2,1,0:T(4,128)S(1)}, f32[32,4,128]{2,1,0:T(4,128)S(1)}, u32[]{:S(2)}, u32[]{:S(2)}) collective-permute-start(f32[32,4,128]{2,1,0:T(4,128)S(1)} %bitcast.33), channel_id=1, source_target_pairs={{0,128},{32,160},{64,192},{96,224},{128,0},{160,32},{192,64},{224,... | collective-permute-start | bytes 196616 | tf_op jit(solution)/shard_map/ppermute | solution.py:309
  92.4 0.7 collective-permute-start.5
  93.1 0.0 collective-permute-done.9.refs_7_
  93.1 0.5 collective-permute-start.4
  93.6 1.5 %collective-permute-done.8.refs_6_ = f32[32,4,128]{2,1,0:T(4,128)S(1)} collective-permute-done((f32[32,4,128]{2,1,0:T(4,128)S(1)}, f32[32,4,128]{2,1,0:T(4,128)S(1)}, u32[]{:S(2)}, u32[]{:S(2)}) %collective-permute-start.8) | collective-permute-done | bytes 65568 | tf_op jit(solution)/shard_map/ppermute | solution.py:309
  95.1 0.6 collective-permute-start.3
  95.7 0.0 collective-permute-done.7.refs_5_
  95.7 2.0 %collective-permute-done.6.refs_4_ = f32[32,4,128]{2,1,0:T(4,128)S(1)} collective-permute-done((f32[32,4,128]{2,1,0:T(4,128)S(1)}, f32[32,4,128]{2,1,0:T(4,128)S(1)}, u32[]{:S(2)}, u32[]{:S(2)}) %collective-permute-start.6) | collective-permute-done | bytes 65568 | tf_op jit(solution)/shard_map/ppermute | solution.py:309
  97.7 0.3 collective-permute-done.5.refs_3_
  98.1 2.6 %collective-permute-done.4.refs_2_ = f32[32,4,128]{2,1,0:T(4,128)S(1)} collective-permute-done((f32[32,4,128]{2,1,0:T(4,128)S(1)}, f32[32,4,128]{2,1,0:T(4,128)S(1)}, u32[]{:S(2)}, u32[]{:S(2)}) %collective-permute-start.4) | collective-permute-done | bytes 65568 | tf_op jit(solution)/shard_map/ppermute | solution.py:309
  100.6 0.0 collective-permute-done.3.refs_1_
  100.7 1.3 %shard_map.141 = f32[512,256]{1,0:T(8,128)} custom-call(f32[32,4,128]{2,1,0:T(4,128)S(1)} %bitcast.37, f32[32,4,128]{2,1,0:T(4,128)S(1)} %collective-permute-done.3.refs_1_, f32[32,4,128]{2,1,0:T(4,128)S(1)} %collective-permute-done.4.refs_2_, f32[32,4,128]{2,1,0:T(4,128)S(1)} %collective-permute-done.5.refs_3_, ...), custom_call_target="tpu_custom_call" | custom-call | tf_op jit(solution)/shard_map/pallas_call | solution.py:294
  101.9 5.5 %all-to-all-done.2 = f32[256,8,1,128]{3,1,2,0:T(8,128)S(1)} async-done(((f32[256,8,1,128]{3,1,2,0:T(8,128)}), f32[256,8,1,128]{3,1,2,0:T(8,128)S(1)}, u32[]{:S(2)}, u32[]{:S(2)}) %all-to-all-start.2) | async-done | bytes 1048608 | tf_op jit(solution)/shard_map/all_to_all | solution.py:304
  107.4 0.0 copy-done
  107.4 0.0 copy-done.1
  107.4 0.0 copy-done.2
  107.4 0.0 copy-done.3
  107.4 1.2 %shard_map.140 = (bf16[1,512,256]{2,1,0:T(8,128)(2,1)}, bf16[1,512,256]{2,1,0:T(8,128)(2,1)}, bf16[1,512,256]{2,1,0:T(8,128)(2,1)}, bf16[1,512,256]{2,1,0:T(8,128)(2,1)}) custom-call(f32[2048,128]{1,0:T(8,128)S(1)} %bitcast.29, bf16[1,512,256]{2,1,0:T(8,128)(2,1)S(1)} %copy-done, bf16[1,512,256]{2,1,0:T(8,128)(2,1)S(1)} %copy-done.1, ...), custom_call_target="tpu_custom_call" | custom-call | tf_op jit(solution)/shard_map/pallas_call | solution.py:280
  (6 shorter events, 0.1 us)
Async XLA Ops:
  2.4 49.3 %copy-start.4 = (bf16[768,256]{1,0:T(8,128)(2,1)S(1)}, bf16[768,256]{1,0:T(8,128)(2,1)}, u32[]{:S(2)}) copy-start(bf16[768,256]{1,0:T(8,128)(2,1)} %constant.12.clone.inner_back_ref) | copy-start | bytes 1179652
  2.4 49.3 %copy-start.5 = (bf16[768,256]{1,0:T(8,128)(2,1)S(1)}, bf16[768,256]{1,0:T(8,128)(2,1)}, u32[]{:S(2)}) copy-start(bf16[768,256]{1,0:T(8,128)(2,1)} %constant.11.clone.inner_ref) | copy-start | bytes 1179652
  2.4 49.2 %copy-start.6 = (bf16[128,768]{1,0:T(8,128)(2,1)S(1)}, bf16[128,768]{1,0:T(8,128)(2,1)}, u32[]{:S(2)}) copy-start(bf16[128,768]{1,0:T(8,128)(2,1)} %constant.13.clone.back_ref) | copy-start | bytes 589828
  2.4 49.2 %copy-start.7 = (bf16[256,384]{1,0:T(8,128)(2,1)S(1)}, bf16[256,384]{1,0:T(8,128)(2,1)}, u32[]{:S(2)}) copy-start(bf16[256,384]{1,0:T(8,128)(2,1)} %constant.10.clone.outer_ref) | copy-start | bytes 589828
  2.4 49.2 %copy-start.8 = (f32[2,128,128]{2,1,0:T(8,128)S(1)}, f32[2,128,128]{2,1,0:T(8,128)}, u32[]{:S(2)}) copy-start(f32[2,128,128]{2,1,0:T(8,128)} %constant.14.clone.twiddle_ref) | copy-start | bytes 393220
  53.9 2.9 %collective-permute-start = (f32[4,4,4,128]{3,2,1,0:T(4,128)S(1)}, f32[4,4,4,128]{3,2,1,0:T(4,128)S(1)}, u32[]{:S(2)}, u32[]{:S(2)}) collective-permute-start(f32[4,4,4,128]{3,2,1,0:T(4,128)S(1)} %bitcast.43), channel_id=1, source_target_pairs={{0,2},{2,0},{1,3},{3,1},{4,6},{6,4},{5,7},{7,5},{8,10},{10,8},{9,1... | collective-permute-start | bytes 98312 | tf_op jit(solution)/shard_map/ppermute | solution.py:309
  57.4 10.2 %all-to-all-start.1 = ((f32[4,2,4,4,128]{4,3,2,1,0:T(4,128)}), f32[4,2,4,4,128]{4,3,2,1,0:T(4,128)S(1)}, u32[]{:S(2)}, u32[]{:S(2)}) async-start(f32[4,2,4,4,128]{4,3,2,1,0:T(4,128)} %pad_maximum_fusion), calls=%async_computation.1 | async-start | bytes 131072 | tf_op jit(solution)/shard_map/all_to_all | solution.py:315
  67.7 39.8 %all-to-all-start.2 = ((f32[256,8,1,128]{3,1,2,0:T(8,128)}), f32[256,8,1,128]{3,1,2,0:T(8,128)S(1)}, u32[]{:S(2)}, u32[]{:S(2)}) async-start(f32[256,8,1,128]{3,1,2,0:T(8,128)} %bitcast.7), calls=%async_computation.2 | async-start | bytes 2097152 | tf_op jit(solution)/shard_map/all_to_all | solution.py:304
  76.4 31.0 %copy-start = (bf16[1,512,256]{2,1,0:T(8,128)(2,1)S(1)}, bf16[1,512,256]{2,1,0:T(8,128)(2,1)}, u32[]{:S(2)}) copy-start(bf16[1,512,256]{2,1,0:T(8,128)(2,1)} %q_ref.1) | copy-start | bytes 786436
  76.4 31.0 %copy-start.1 = (bf16[1,512,256]{2,1,0:T(8,128)(2,1)S(1)}, bf16[1,512,256]{2,1,0:T(8,128)(2,1)}, u32[]{:S(2)}) copy-start(bf16[1,512,256]{2,1,0:T(8,128)(2,1)} %k_ref.1) | copy-start | bytes 786436
  76.4 31.0 %copy-start.2 = (bf16[1,512,256]{2,1,0:T(8,128)(2,1)S(1)}, bf16[1,512,256]{2,1,0:T(8,128)(2,1)}, u32[]{:S(2)}) copy-start(bf16[1,512,256]{2,1,0:T(8,128)(2,1)} %v_ref.1) | copy-start | bytes 786436
  76.4 31.0 %copy-start.3 = (bf16[1,512,256]{2,1,0:T(8,128)(2,1)S(1)}, bf16[1,512,256]{2,1,0:T(8,128)(2,1)}, u32[]{:S(2)}) copy-start(bf16[1,512,256]{2,1,0:T(8,128)(2,1)} %u_ref.1) | copy-start | bytes 786436
  76.5 3.4 %collective-permute-start.1 = (f32[4,2,2,4,128]{4,3,1,0,2:T(4,128)S(1)}, f32[4,2,2,4,128]{4,3,1,0,2:T(4,128)S(1)}, u32[]{:S(2)}, u32[]{:S(2)}) collective-permute-start(f32[4,2,2,4,128]{4,3,1,0,2:T(4,128)S(1)} %bitcast.41), channel_id=1, source_target_pairs={{0,16},{16,0},{1,17},{17,1},{2,18},{18,2},{3,19},{19,3},{4,20},{20... | collective-permute-start | bytes 98312 | tf_op jit(solution)/shard_map/ppermute | solution.py:309
  79.9 4.1 %collective-permute-start.2 = (f32[2,4,2,4,128]{4,3,2,1,0:T(4,128)S(1)}, f32[2,4,2,4,128]{4,3,2,1,0:T(4,128)S(1)}, u32[]{:S(2)}, u32[]{:S(2)}) collective-permute-start(f32[2,4,2,4,128]{4,3,2,1,0:T(4,128)S(1)} %get-tuple-element.24), channel_id=1, source_target_pairs={{0,1},{1,0},{2,3},{3,2},{4,5},{5,4},{6,7},{7,6},{8,9},{9,8},{10,11... | collective-permute-start | bytes 98312 | tf_op jit(solution)/shard_map/ppermute | solution.py:309
  84.0 9.1 %collective-permute-start.9 = (f32[32,4,128]{2,1,0:T(4,128)S(1)}, f32[32,4,128]{2,1,0:T(4,128)S(1)}, u32[]{:S(2)}, u32[]{:S(2)}) collective-permute-start(f32[32,4,128]{2,1,0:T(4,128)S(1)} %bitcast.30), channel_id=1, source_target_pairs={{0,224},{32,192},{64,160},{96,128},{128,96},{160,64},{192,32},{224... | collective-permute-start | bytes 196616 | tf_op jit(solution)/shard_map/ppermute | solution.py:309
  87.2 7.9 %collective-permute-start.8 = (f32[32,4,128]{2,1,0:T(4,128)S(1)}, f32[32,4,128]{2,1,0:T(4,128)S(1)}, u32[]{:S(2)}, u32[]{:S(2)}) collective-permute-start(f32[32,4,128]{2,1,0:T(4,128)S(1)} %bitcast.31), channel_id=1, source_target_pairs={{0,192},{32,224},{64,128},{96,160},{128,64},{160,96},{192,0},{224,... | collective-permute-start | bytes 196616 | tf_op jit(solution)/shard_map/ppermute | solution.py:309
  87.7 8.0 %collective-permute-start.7 = (f32[32,4,128]{2,1,0:T(4,128)S(1)}, f32[32,4,128]{2,1,0:T(4,128)S(1)}, u32[]{:S(2)}, u32[]{:S(2)}) collective-permute-start(f32[32,4,128]{2,1,0:T(4,128)S(1)} %bitcast.32), channel_id=1, source_target_pairs={{0,160},{32,128},{64,224},{96,192},{128,32},{160,0},{192,96},{224,... | collective-permute-start | bytes 196616 | tf_op jit(solution)/shard_map/ppermute | solution.py:309
  90.2 7.5 %collective-permute-start.6 = (f32[32,4,128]{2,1,0:T(4,128)S(1)}, f32[32,4,128]{2,1,0:T(4,128)S(1)}, u32[]{:S(2)}, u32[]{:S(2)}) collective-permute-start(f32[32,4,128]{2,1,0:T(4,128)S(1)} %bitcast.33), channel_id=1, source_target_pairs={{0,128},{32,160},{64,192},{96,224},{128,0},{160,32},{192,64},{224,... | collective-permute-start | bytes 196616 | tf_op jit(solution)/shard_map/ppermute | solution.py:309
  92.4 5.6 %collective-permute-start.5 = (f32[32,4,128]{2,1,0:T(4,128)S(1)}, f32[32,4,128]{2,1,0:T(4,128)S(1)}, u32[]{:S(2)}, u32[]{:S(2)}) collective-permute-start(f32[32,4,128]{2,1,0:T(4,128)S(1)} %bitcast.34), channel_id=1, source_target_pairs={{0,96},{32,64},{64,32},{96,0},{128,224},{160,192},{192,160},{224,1... | collective-permute-start | bytes 196616 | tf_op jit(solution)/shard_map/ppermute | solution.py:309
  93.1 7.5 %collective-permute-start.4 = (f32[32,4,128]{2,1,0:T(4,128)S(1)}, f32[32,4,128]{2,1,0:T(4,128)S(1)}, u32[]{:S(2)}, u32[]{:S(2)}) collective-permute-start(f32[32,4,128]{2,1,0:T(4,128)S(1)} %bitcast.35), channel_id=1, source_target_pairs={{0,64},{32,96},{64,0},{96,32},{128,192},{160,224},{192,128},{224,1... | collective-permute-start | bytes 196616 | tf_op jit(solution)/shard_map/ppermute | solution.py:309
  95.1 5.5 %collective-permute-start.3 = (f32[32,4,128]{2,1,0:T(4,128)S(1)}, f32[32,4,128]{2,1,0:T(4,128)S(1)}, u32[]{:S(2)}, u32[]{:S(2)}) collective-permute-start(f32[32,4,128]{2,1,0:T(4,128)S(1)} %bitcast.36), channel_id=1, source_target_pairs={{0,32},{32,0},{64,96},{96,64},{128,160},{160,128},{192,224},{224,1... | collective-permute-start | bytes 196616 | tf_op jit(solution)/shard_map/ppermute | solution.py:309

commit v12 on v8

--- a/solution.py
+++ b/solution.py
@@ -19,7 +19,7 @@
 ROWS_OUT = 3 * PIECES
 HALF = 128
 LENGTH = 2 * BLOCK * OWNERS
-GROUP = 2
+GROUP = 1
 VMEM_LIMIT = 32 << 20
 
 
@@ -199,9 +199,11 @@
     copies = []
     for piece in range(PIECES):
         at = pl.ds(piece * LANES, LANES)
+        large[at, :] = c_ref[pl.ds(2 * PIECES + piece, CHANNELS, stride=ROWS_OUT), :].T
+        copies.append(pltpu.make_async_copy(large.at[at, :], fg_hbm.at[at, :], large_sems.at[piece]))
+        copies[-1].start()
         conv = c_ref[pl.ds(piece, CHANNELS, stride=ROWS_OUT), :].T
         back = c_ref[pl.ds(PIECES + piece, CHANNELS, stride=ROWS_OUT), :].T
-        large[at, :] = c_ref[pl.ds(2 * PIECES + piece, CHANNELS, stride=ROWS_OUT), :].T
         pieces = (
             (q_ref, conv, o_hbm),
             (u_ref, conv, qg_hbm),
@@ -214,8 +216,6 @@
                 pltpu.make_async_copy(small.at[index, at, :], target.at[0, at, :], sems.at[index, piece])
             )
             copies[-1].start()
-        copies.append(pltpu.make_async_copy(large.at[at, :], fg_hbm.at[at, :], large_sems.at[piece]))
-        copies[-1].start()
     for copy in copies:
         copy.wait()
 

time: 105 us -> 105 us (level)
  no operation moved by 1% of the time
where the time goes in v12:
time: 105 us
  blocking collectives  97.7 us (93%)
  Pallas kernels  6.44 us (6%)
    all_to_all x2, blocking collectives, exchange(): lax.all_to_all(shaped, ('dp', 'seq'), split_axis=0, concat_axis=0, tiled=...  97.7 us
    pallas_call x1, Pallas kernels, transform(): pl.pallas_call(fft_kernel, out_shape=jax.ShapeDtypeStruct((SEQS * OWNERS...  3.29 us

profile of v12, /device:TPU:1, one launch (start us, length us, event | category | flops | bytes accessed | tf_op | source)
XLA Modules:
  0.0 105.0 jit_solution(5160557342870391890)
XLA Ops:
  0.6 1.8 %shard_map.137 = f32[2304,128]{1,0:T(8,128)S(1)} custom-call(bf16[1,512,256]{2,1,0:T(8,128)(2,1)} %q_ref.1, bf16[1,512,256]{2,1,0:T(8,128)(2,1)} %k_ref.1, bf16[1,512,256]{2,1,0:T(8,128)(2,1)} %v_ref.1, bf16[1,512,256]{2,1,0:T(8,128)(2,1)} %u_ref.1, f32[512,256]{1,0:T(8,128)} %f_hbm.1), custom_call_target="tpu_custom_call" | custom-call | tf_op jit(solution)/shard_map/pallas_call | solution.py:229
  2.4 0.0 copy-start.4
  2.4 0.0 copy-start.5
  2.4 0.0 copy-start.6
  2.4 0.0 copy-start.7
  2.4 0.0 copy-start.8
  2.5 49.2 %all_to_all.10 = f32[256,9,1,128]{3,2,1,0:T(1,128)S(1)} all-to-all(f32[256,9,1,128]{3,2,1,0:T(1,128)S(1)} %bitcast.7), channel_id=1, replica_groups=mesh['dp'=8,'seq'=32] {'dp','seq'}, dimensions={0} | all-to-all | bytes 2359296 | tf_op jit(solution)/shard_map/all_to_all | solution.py:271
  51.6 0.0 copy-done.4
  51.7 0.0 copy-done.5
  51.7 0.0 copy-done.6
  51.7 0.0 copy-done.7
  51.7 0.0 copy-done.8
  51.7 3.3 %shard_map.138 = f32[3072,128]{1,0:T(8,128)S(1)} custom-call(f32[2304,128]{1,0:T(8,128)S(1)} %bitcast.6, bf16[256,384]{1,0:T(8,128)(2,1)S(1)} %copy-done.7, bf16[768,256]{1,0:T(8,128)(2,1)S(1)} %copy-done.5, bf16[768,256]{1,0:T(8,128)(2,1)S(1)} %copy-done.4, bf16[128,768]{1,0:T(8,128)(2,1)S(1)} %copy-done.6, f32[2,128,128]{2,1,0:T(8,128)S(1)} %copy-done.8), custom_call_target="tpu_custom_call" | custom-call | tf_op jit(solution)/shard_map/pallas_call | solution.py:245
  55.0 0.0 copy-start
  55.0 0.0 copy-start.1
  55.0 0.0 copy-start.2
  55.0 0.0 copy-start.3
  55.0 48.5 %all_to_all.11 = f32[256,12,1,128]{3,2,1,0:T(1,128)S(1)} all-to-all(f32[256,12,1,128]{3,2,1,0:T(1,128)S(1)} %bitcast.5), channel_id=1, replica_groups=mesh['dp'=8,'seq'=32] {'dp','seq'}, dimensions={0} | all-to-all | bytes 3145728 | tf_op jit(solution)/shard_map/all_to_all | solution.py:271
  103.6 0.0 copy-done
  103.6 0.0 copy-done.1
  103.6 0.0 copy-done.2
  103.6 0.0 copy-done.3
  103.6 1.4 %shard_map.139 = (bf16[1,512,256]{2,1,0:T(8,128)(2,1)}, bf16[1,512,256]{2,1,0:T(8,128)(2,1)}, bf16[1,512,256]{2,1,0:T(8,128)(2,1)}, bf16[1,512,256]{2,1,0:T(8,128)(2,1)}, f32[512,256]{1,0:T(8,128)}) custom-call(f32[3072,128]{1,0:T(8,128)S(1)} %bitcast.4, bf16[1,512,256]{2,1,0:T(8,128)(2,1)S(1)} %copy-done, bf16[1,512,256]{2,1,0:T(8,128)(2,1)S(1)} %copy-done.1, ...), custom_call_target="tpu_custom_call" | custom-call | tf_op jit(solution)/shard_map/pallas_call | solution.py:254
Async XLA Ops:
  2.4 49.3 %copy-start.4 = (bf16[768,256]{1,0:T(8,128)(2,1)S(1)}, bf16[768,256]{1,0:T(8,128)(2,1)}, u32[]{:S(2)}) copy-start(bf16[768,256]{1,0:T(8,128)(2,1)} %constant.12.clone.inner_back_ref) | copy-start | bytes 1179652
  2.4 49.3 %copy-start.5 = (bf16[768,256]{1,0:T(8,128)(2,1)S(1)}, bf16[768,256]{1,0:T(8,128)(2,1)}, u32[]{:S(2)}) copy-start(bf16[768,256]{1,0:T(8,128)(2,1)} %constant.11.clone.inner_ref) | copy-start | bytes 1179652
  2.4 49.2 %copy-start.6 = (bf16[128,768]{1,0:T(8,128)(2,1)S(1)}, bf16[128,768]{1,0:T(8,128)(2,1)}, u32[]{:S(2)}) copy-start(bf16[128,768]{1,0:T(8,128)(2,1)} %constant.13.clone.back_ref) | copy-start | bytes 589828
  2.4 49.2 %copy-start.7 = (bf16[256,384]{1,0:T(8,128)(2,1)S(1)}, bf16[256,384]{1,0:T(8,128)(2,1)}, u32[]{:S(2)}) copy-start(bf16[256,384]{1,0:T(8,128)(2,1)} %constant.10.clone.outer_ref) | copy-start | bytes 589828
  2.4 49.2 %copy-start.8 = (f32[2,128,128]{2,1,0:T(8,128)S(1)}, f32[2,128,128]{2,1,0:T(8,128)}, u32[]{:S(2)}) copy-start(f32[2,128,128]{2,1,0:T(8,128)} %constant.14.clone.twiddle_ref) | copy-start | bytes 393220
  55.0 48.6 %copy-start = (bf16[1,512,256]{2,1,0:T(8,128)(2,1)S(1)}, bf16[1,512,256]{2,1,0:T(8,128)(2,1)}, u32[]{:S(2)}) copy-start(bf16[1,512,256]{2,1,0:T(8,128)(2,1)} %q_ref.1) | copy-start | bytes 786436
  55.0 48.6 %copy-start.1 = (bf16[1,512,256]{2,1,0:T(8,128)(2,1)S(1)}, bf16[1,512,256]{2,1,0:T(8,128)(2,1)}, u32[]{:S(2)}) copy-start(bf16[1,512,256]{2,1,0:T(8,128)(2,1)} %k_ref.1) | copy-start | bytes 786436
  55.0 48.6 %copy-start.2 = (bf16[1,512,256]{2,1,0:T(8,128)(2,1)S(1)}, bf16[1,512,256]{2,1,0:T(8,128)(2,1)}, u32[]{:S(2)}) copy-start(bf16[1,512,256]{2,1,0:T(8,128)(2,1)} %v_ref.1) | copy-start | bytes 786436
  55.0 48.6 %copy-start.3 = (bf16[1,512,256]{2,1,0:T(8,128)(2,1)S(1)}, bf16[1,512,256]{2,1,0:T(8,128)(2,1)}, u32[]{:S(2)}) copy-start(bf16[1,512,256]{2,1,0:T(8,128)(2,1)} %u_ref.1) | copy-start | bytes 786436

commit v13 on v8

--- a/solution.py
+++ b/solution.py
@@ -54,6 +54,9 @@
 
 
 def pre_kernel(q_hbm, k_hbm, v_hbm, u_hbm, f_hbm, out_ref, data, taps, sems, taps_sem):
+    first = pl.multiple_of(lax.div(lax.axis_index("dp"), 2) * LANES, LANES)
+    taps_copy = pltpu.make_async_copy(f_hbm.at[pl.ds(first, LANES), :], taps, taps_sem)
+    taps_copy.start()
     sources = (k_hbm, v_hbm, u_hbm, q_hbm)
     copies = []
     for piece in range(PIECES):
@@ -66,9 +69,6 @@
         )
         for copy in copies[-1]:
             copy.start()
-    first = pl.multiple_of(lax.div(lax.axis_index("dp"), 2) * LANES, LANES)
-    taps_copy = pltpu.make_async_copy(f_hbm.at[pl.ds(first, LANES), :], taps, taps_sem)
-    taps_copy.start()
     for piece in range(PIECES):
         for copy in copies[piece]:
             copy.wait()

time: 105 us -> 105 us (level)
  no operation moved by 1% of the time
where the time goes in v13:
time: 105 us
  blocking collectives  97.7 us (93%)
  Pallas kernels  6.45 us (6%)
    all_to_all x2, blocking collectives, exchange(): lax.all_to_all(shaped, ('dp', 'seq'), split_axis=0, concat_axis=0, tiled=...  97.7 us
    pallas_call x1, Pallas kernels, transform(): pl.pallas_call(fft_kernel, out_shape=jax.ShapeDtypeStruct((SEQS * OWNERS...  3.29 us

profile of v13, /device:TPU:1, one launch (start us, length us, event | category | flops | bytes accessed | tf_op | source)
XLA Modules:
  0.0 105.0 jit_solution(7243571304729534384)
XLA Ops:
  0.6 1.8 %shard_map.137 = f32[2304,128]{1,0:T(8,128)S(1)} custom-call(bf16[1,512,256]{2,1,0:T(8,128)(2,1)} %q_ref.1, bf16[1,512,256]{2,1,0:T(8,128)(2,1)} %k_ref.1, bf16[1,512,256]{2,1,0:T(8,128)(2,1)} %v_ref.1, bf16[1,512,256]{2,1,0:T(8,128)(2,1)} %u_ref.1, f32[512,256]{1,0:T(8,128)} %f_hbm.1), custom_call_target="tpu_custom_call" | custom-call | tf_op jit(solution)/shard_map/pallas_call | solution.py:229
  2.4 0.0 copy-start.4
  2.4 0.0 copy-start.5
  2.4 0.0 copy-start.6
  2.4 0.0 copy-start.7
  2.4 0.0 copy-start.8
  2.5 49.2 %all_to_all.10 = f32[256,9,1,128]{3,2,1,0:T(1,128)S(1)} all-to-all(f32[256,9,1,128]{3,2,1,0:T(1,128)S(1)} %bitcast.7), channel_id=1, replica_groups=mesh['dp'=8,'seq'=32] {'dp','seq'}, dimensions={0} | all-to-all | bytes 2359296 | tf_op jit(solution)/shard_map/all_to_all | solution.py:271
  51.6 0.0 copy-done.4
  51.7 0.0 copy-done.5
  51.7 0.0 copy-done.6
  51.7 0.0 copy-done.7
  51.7 0.0 copy-done.8
  51.7 3.3 %shard_map.138 = f32[3072,128]{1,0:T(8,128)S(1)} custom-call(f32[2304,128]{1,0:T(8,128)S(1)} %bitcast.6, bf16[256,384]{1,0:T(8,128)(2,1)S(1)} %copy-done.7, bf16[768,256]{1,0:T(8,128)(2,1)S(1)} %copy-done.5, bf16[768,256]{1,0:T(8,128)(2,1)S(1)} %copy-done.4, bf16[128,768]{1,0:T(8,128)(2,1)S(1)} %copy-done.6, f32[2,128,128]{2,1,0:T(8,128)S(1)} %copy-done.8), custom_call_target="tpu_custom_call" | custom-call | tf_op jit(solution)/shard_map/pallas_call | solution.py:245
  55.0 0.0 copy-start
  55.0 0.0 copy-start.1
  55.0 0.0 copy-start.2
  55.0 0.0 copy-start.3
  55.0 48.5 %all_to_all.11 = f32[256,12,1,128]{3,2,1,0:T(1,128)S(1)} all-to-all(f32[256,12,1,128]{3,2,1,0:T(1,128)S(1)} %bitcast.5), channel_id=1, replica_groups=mesh['dp'=8,'seq'=32] {'dp','seq'}, dimensions={0} | all-to-all | bytes 3145728 | tf_op jit(solution)/shard_map/all_to_all | solution.py:271
  103.6 0.0 copy-done
  103.6 0.0 copy-done.1
  103.6 0.0 copy-done.2
  103.6 0.0 copy-done.3
  103.6 1.4 %shard_map.139 = (bf16[1,512,256]{2,1,0:T(8,128)(2,1)}, bf16[1,512,256]{2,1,0:T(8,128)(2,1)}, bf16[1,512,256]{2,1,0:T(8,128)(2,1)}, bf16[1,512,256]{2,1,0:T(8,128)(2,1)}, f32[512,256]{1,0:T(8,128)}) custom-call(f32[3072,128]{1,0:T(8,128)S(1)} %bitcast.4, bf16[1,512,256]{2,1,0:T(8,128)(2,1)S(1)} %copy-done, bf16[1,512,256]{2,1,0:T(8,128)(2,1)S(1)} %copy-done.1, ...), custom_call_target="tpu_custom_call" | custom-call | tf_op jit(solution)/shard_map/pallas_call | solution.py:254
Async XLA Ops:
  2.4 49.3 %copy-start.4 = (bf16[768,256]{1,0:T(8,128)(2,1)S(1)}, bf16[768,256]{1,0:T(8,128)(2,1)}, u32[]{:S(2)}) copy-start(bf16[768,256]{1,0:T(8,128)(2,1)} %constant.12.clone.inner_back_ref) | copy-start | bytes 1179652
  2.4 49.3 %copy-start.5 = (bf16[768,256]{1,0:T(8,128)(2,1)S(1)}, bf16[768,256]{1,0:T(8,128)(2,1)}, u32[]{:S(2)}) copy-start(bf16[768,256]{1,0:T(8,128)(2,1)} %constant.11.clone.inner_ref) | copy-start | bytes 1179652
  2.4 49.2 %copy-start.6 = (bf16[128,768]{1,0:T(8,128)(2,1)S(1)}, bf16[128,768]{1,0:T(8,128)(2,1)}, u32[]{:S(2)}) copy-start(bf16[128,768]{1,0:T(8,128)(2,1)} %constant.13.clone.back_ref) | copy-start | bytes 589828
  2.4 49.2 %copy-start.7 = (bf16[256,384]{1,0:T(8,128)(2,1)S(1)}, bf16[256,384]{1,0:T(8,128)(2,1)}, u32[]{:S(2)}) copy-start(bf16[256,384]{1,0:T(8,128)(2,1)} %constant.10.clone.outer_ref) | copy-start | bytes 589828
  2.4 49.2 %copy-start.8 = (f32[2,128,128]{2,1,0:T(8,128)S(1)}, f32[2,128,128]{2,1,0:T(8,128)}, u32[]{:S(2)}) copy-start(f32[2,128,128]{2,1,0:T(8,128)} %constant.14.clone.twiddle_ref) | copy-start | bytes 393220
  55.0 48.6 %copy-start = (bf16[1,512,256]{2,1,0:T(8,128)(2,1)S(1)}, bf16[1,512,256]{2,1,0:T(8,128)(2,1)}, u32[]{:S(2)}) copy-start(bf16[1,512,256]{2,1,0:T(8,128)(2,1)} %q_ref.1) | copy-start | bytes 786436
  55.0 48.6 %copy-start.1 = (bf16[1,512,256]{2,1,0:T(8,128)(2,1)S(1)}, bf16[1,512,256]{2,1,0:T(8,128)(2,1)}, u32[]{:S(2)}) copy-start(bf16[1,512,256]{2,1,0:T(8,128)(2,1)} %k_ref.1) | copy-start | bytes 786436
  55.0 48.6 %copy-start.2 = (bf16[1,512,256]{2,1,0:T(8,128)(2,1)S(1)}, bf16[1,512,256]{2,1,0:T(8,128)(2,1)}, u32[]{:S(2)}) copy-start(bf16[1,512,256]{2,1,0:T(8,128)(2,1)} %v_ref.1) | copy-start | bytes 786436
  55.0 48.6 %copy-start.3 = (bf16[1,512,256]{2,1,0:T(8,128)(2,1)S(1)}, bf16[1,512,256]{2,1,0:T(8,128)(2,1)}, u32[]{:S(2)}) copy-start(bf16[1,512,256]{2,1,0:T(8,128)(2,1)} %u_ref.1) | copy-start | bytes 786436
